TPU v7x, 128 devices: a whole 4x4x4 slice. The times are simulated.
128 devices in a mesh: sec: 4 (over z_lo, core), lat: 32 (over x, z_hi, y).
Axes of the slice: x: 4, y: 4, z: 4 (z_hi: 2, z_lo: 2; z = z_hi * 2 + z_lo), core: 2. Of those that a mesh axis runs over, the one named last changes fastest.
Arguments:
- ocean_state: float32 [24, 512, 1024], P(None, 'lat', 'sec'), may hold values from -6 to 6
- land_mask: int32 [512, 1024], P('lat', 'sec'), may hold values from 0 to 1
- layer_count: int32 [512, 1024], P('lat', 'sec'), may hold values from 1 to 8
- conv1_weight: bfloat16 [5, 128, 120], replicated, may hold values from -1 to 1
- conv1_bias: float32 [128], replicated, may hold values from -3 to 3
- conv2_weight: bfloat16 [5, 64, 640], replicated, may hold values from -1 to 1
- conv2_bias: float32 [64], replicated, may hold values from -3 to 3
- conv3_weight: bfloat16 [5, 32, 320], replicated, may hold values from -1 to 1
- conv3_bias: float32 [32], replicated, may hold values from -3 to 3
- conv4_weight: bfloat16 [5, 16, 160], replicated, may hold values from -1 to 1
Outputs:
- final_state: float32 [24, 512, 1024], P(None, 'lat', 'sec')
- forcing: float32 [16, 512, 1024], P(None, 'lat', 'sec')
All inputs are finite; a program needn't handle non-finite values.
Results may differ from a plain program's by a relative error of at most 0.015.
Values may be sent and summed in bfloat16 or wider, within the bound.
No kernel may reach another device: no remote copies, remote signals or barrier semaphores. Data moves between devices by JAX's collectives and lax.ppermute only.
A program may use at most 128 MiB of HBM per device.

v0:
```python
import jax
import jax.numpy as jnp
from jax import lax
from jax.sharding import PartitionSpec as P

LEVELS = 8
STEPS = 4


time_step = 0.3
drag_rate = 0.05


def padded_2(block, sides, width):
    for axis, dim in sides:
        count = lax.axis_size(axis)
        forward = [(i, i + 1) for i in range(count - 1)]
        backward = [(target, source) for source, target in forward]
        low = lax.ppermute(
            lax.slice_in_dim(block, block.shape[dim] - width, None, axis=dim), axis, forward
        )
        high = lax.ppermute(lax.slice_in_dim(block, 0, width, axis=dim), axis, backward)
        block = jnp.concatenate([low, block, high], axis=dim)
    return block


def coupling(count_levels):
    row_index = lax.broadcasted_iota(jnp.int32, (count_levels, count_levels), 0)
    col_index = lax.broadcasted_iota(jnp.int32, (count_levels, count_levels), 1)
    return 0.5 + 0.1 * jnp.minimum(row_index, col_index).astype(jnp.float32)


def conv_layer(layer_in, weight):
    out_rows = layer_in.shape[1] - 4
    out_cols = layer_in.shape[2] - 4
    summed = jnp.zeros((weight.shape[1], out_rows, out_cols), jnp.float32)
    for shift_y in range(5):
        row_band = layer_in[:, shift_y : shift_y + out_rows, :]
        stacked = jnp.concatenate(
            [row_band[:, :, shift_x : shift_x + out_cols] for shift_x in range(5)], axis=0
        )
        summed = summed + jnp.einsum(
            "oc,crx->orx", weight[shift_y], stacked, preferred_element_type=jnp.float32
        )
    return summed


def ocean_step(padded, wet_pad, forcing, coriolis, coupling_matrix):
    zonal_vel = padded[:LEVELS]
    merid_vel = padded[LEVELS : 2 * LEVELS]
    thickness = padded[2 * LEVELS :]
    divergence = (zonal_vel[:, 1:-1, 2:] - zonal_vel[:, 1:-1, :-2]) * 0.5 + (
        merid_vel[:, 2:, 1:-1] - merid_vel[:, :-2, 1:-1]
    ) * 0.5
    h_cycle = (thickness[:, 1:-1, 1:-1] - time_step * divergence) * wet_pad[:, 1:-1, 1:-1]
    pressure = jnp.einsum("kj,jrx->krx", coupling_matrix, h_cycle, precision=lax.Precision.HIGHEST)
    grad_x = (pressure[:, 1:-1, 2:] - pressure[:, 1:-1, :-2]) * 0.5
    grad_y = (pressure[:, 2:, 1:-1] - pressure[:, :-2, 1:-1]) * 0.5
    zonal_mid = zonal_vel[:, 2:-2, 2:-2]
    merid_mid = merid_vel[:, 2:-2, 2:-2]
    wet_mid = wet_pad[:, 2:-2, 2:-2]
    zonal_new = (
        zonal_mid
        + time_step * (-grad_x + coriolis * merid_mid - drag_rate * zonal_mid + forcing[:LEVELS])
    ) * wet_mid
    merid_new = (
        merid_mid
        + time_step * (-grad_y - coriolis * zonal_mid - drag_rate * merid_mid + forcing[LEVELS:])
    ) * wet_mid
    return jnp.concatenate([zonal_new, merid_new, h_cycle[:, 1:-1, 1:-1]], axis=0)


def local(
    ocean_state,
    land_mask,
    layer_count,
    conv1_weight,
    conv1_bias,
    conv2_weight,
    conv2_bias,
    conv3_weight,
    conv3_bias,
    conv4_weight,
):
    dev_rows = ocean_state.shape[1]
    dev_cols = ocean_state.shape[2]
    row_start = lax.axis_index("lat") * dev_rows
    grid_rows = lax.axis_size("lat") * dev_rows
    levels = land_mask * layer_count
    levels_ext = padded_2(levels, (("sec", 1), ("lat", 0)), 8)
    wet_ext = (
        lax.broadcasted_iota(jnp.int32, (LEVELS, dev_rows + 16, dev_cols + 16), 0)
        < levels_ext[None]
    ).astype(jnp.float32)
    sea_ext = (levels_ext > 0).astype(jnp.float32)[None]
    wet_mask = wet_ext[:, 8:-8, 8:-8]
    wet_cycle = wet_ext[:, 6:-6, 6:-6]
    wet_two = jnp.concatenate([wet_mask, wet_mask], axis=0)
    wet_three = jnp.concatenate([wet_mask, wet_mask, wet_mask], axis=0)
    counts = jnp.maximum(lax.psum(jnp.sum(wet_mask, axis=(1, 2)), ("sec", "lat")), 1.0)
    counts_two = jnp.concatenate([counts, counts])
    global_rows = row_start + lax.broadcasted_iota(jnp.int32, (1, dev_rows, 1), 1)
    coriolis = 0.3 + 0.5 * global_rows.astype(jnp.float32) / grid_rows
    coupling_matrix = coupling(LEVELS)
    state = ocean_state * wet_three
    forcing = jnp.zeros((2 * LEVELS, dev_rows, dev_cols), jnp.float32)
    for step_index in range(STEPS):
        net_in = padded_2(state.astype(jnp.bfloat16), (("sec", 2), ("lat", 1)), 8)
        ocean_in = padded_2(state.astype(jnp.bfloat16), (("sec", 2), ("lat", 1)), 2).astype(
            state.dtype
        )
        hidden = net_in
        for weight, offset, margin in (
            (conv1_weight, conv1_bias, 6),
            (conv2_weight, conv2_bias, 4),
            (conv3_weight, conv3_bias, 2),
        ):
            activation = jax.nn.silu(conv_layer(hidden, weight) + offset[:, None, None])
            sea_part = sea_ext[
                :, 8 - margin : 8 + dev_rows + margin, 8 - margin : 8 + dev_cols + margin
            ]
            hidden = (activation * sea_part).astype(jnp.bfloat16)
        raw_forcing = conv_layer(hidden, conv4_weight)
        wet_sums = lax.psum(jnp.sum(raw_forcing * wet_two, axis=(1, 2)), ("sec", "lat"))
        forcing = (raw_forcing - (wet_sums / counts_two)[:, None, None]) * wet_two
        state = ocean_step(ocean_in, wet_cycle, forcing, coriolis, coupling_matrix)
    return (state, forcing)


def solution(mesh):
    return jax.shard_map(
        local,
        mesh=mesh,
        in_specs=(
            P(None, "lat", "sec"),
            P("lat", "sec"),
            P("lat", "sec"),
            P(),
            P(),
            P(),
            P(),
            P(),
            P(),
            P(),
        ),
        out_specs=(P(None, "lat", "sec"), P(None, "lat", "sec")),
        check_vma=False,
    )
```

profile of v0, /device:TPU:1, one launch (start us, length us, event | category | flops | bytes accessed | tf_op | source)
XLA Modules:
  0.0 689.2 jit_solution(12869634363887785392)
XLA Ops:
  1.4 4.9 collective-permute-start
  36.9 4.2 collective-permute-start.10
  43.7 7.6 %collective-permute-done.11 = bf16[24,8,272]{2,0,1:T(8,128)(2,1)S(1)} collective-permute-done((bf16[24,8,272]{2,0,1:T(8,128)(2,1)S(1)}, bf16[24,8,272]{2,0,1:T(8,128)(2,1)S(1)}, u32[]{:S(2)}, u32[]{:S(2)}) %collective-permute-start.11) | collective-permute-done | bytes 104480 | tf_op jit(solution)/shard_map/ppermute | solution.py:22
  63.9 4.3 slice_dynamic-update-slice_fusion.78
  68.2 4.3 slice_dynamic-update-slice_fusion.77
  72.6 4.3 slice_dynamic-update-slice_fusion.76
  76.8 4.5 slice_dynamic-update-slice_fusion.75
  115.2 74.6 %all-reduce = (f32[16]{0:T(128)S(1)}, f32[8]{0:T(128)S(1)}) all-reduce(f32[16]{0:T(128)S(1)} %get-tuple-element.452, f32[8]{0:T(128)S(1)} %get-tuple-element.420), channel_id=1, replica_groups=mesh['sec'=4,'lat'=32] {'sec','lat'}, use_global_device_ids=true, to_apply=%region_1.0 | all-reduce | flops 24 | bytes 192 | tf_op jit(solution)/shard_map/psum | solution.py:124
  211.4 4.1 collective-permute-done.19
  228.1 4.3 slice_dynamic-update-slice_fusion.53
  232.4 4.3 slice_dynamic-update-slice_fusion.52
  236.7 4.3 slice_dynamic-update-slice_fusion.51
  241.0 4.7 slice_dynamic-update-slice_fusion.50
  279.3 76.1 %psum.37 = f32[16]{0:T(128)S(1)} all-reduce(f32[16]{0:T(128)S(1)} %get-tuple-element.454), channel_id=1, replica_groups=mesh['sec'=4,'lat'=32] {'sec','lat'}, use_global_device_ids=true, to_apply=%region_5.6 | all-reduce | flops 16 | bytes 128 | tf_op jit(solution)/shard_map/psum | solution.py:124
  393.6 4.3 slice_dynamic-update-slice_fusion.28
  397.9 4.3 slice_dynamic-update-slice_fusion.27
  402.3 4.3 slice_dynamic-update-slice_fusion.26
  406.5 4.4 slice_dynamic-update-slice_fusion.25
  444.6 75.8 %psum.38 = f32[16]{0:T(128)S(1)} all-reduce(f32[16]{0:T(128)S(1)} %get-tuple-element.456), channel_id=1, replica_groups=mesh['sec'=4,'lat'=32] {'sec','lat'}, use_global_device_ids=true, to_apply=%region_7.8 | all-reduce | flops 16 | bytes 128 | tf_op jit(solution)/shard_map/psum | solution.py:124
  558.7 4.3 slice_dynamic-update-slice_fusion.3
  563.0 4.3 slice_dynamic-update-slice_fusion.2
  567.3 4.3 slice_dynamic-update-slice_fusion.1
  571.6 4.5 slice_dynamic-update-slice_fusion
  609.8 75.7 %psum.39 = f32[16]{0:T(128)S(1)} all-reduce(f32[16]{0:T(128)S(1)} %get-tuple-element.458), channel_id=1, replica_groups=mesh['sec'=4,'lat'=32] {'sec','lat'}, use_global_device_ids=true, to_apply=%region_9.10 | all-reduce | flops 16 | bytes 128 | tf_op jit(solution)/shard_map/psum | solution.py:124
  (363 shorter events, 293.4 us)
Async XLA Ops:
  1.4 6.9 collective-permute-start
  21.0 11.0 %collective-permute-start.4 = (bf16[24,16,2]{2,0,1:T(8,128)(2,1)S(1)}, bf16[24,16,2]{2,0,1:T(8,128)(2,1)S(1)}, u32[]{:S(2)}, u32[]{:S(2)}) collective-permute-start(bf16[24,16,2]{2,0,1:T(8,128)(2,1)S(1)} %get-tuple-element.446), channel_id=1, source_target_pairs={{0,32},{32,64},{64,96},{1,33},{33,65},{65,97},{2,34},{34,66},{66,9... | collective-permute-start | bytes 4616 | tf_op jit(solution)/shard_map/ppermute | solution.py:19
  24.4 7.6 %collective-permute-start.5 = (bf16[24,16,2]{2,0,1:T(8,128)(2,1)S(1)}, bf16[24,16,2]{2,0,1:T(8,128)(2,1)S(1)}, u32[]{:S(2)}, u32[]{:S(2)}) collective-permute-start(bf16[24,16,2]{2,0,1:T(8,128)(2,1)S(1)} %get-tuple-element.447), channel_id=1, source_target_pairs={{32,0},{64,32},{96,64},{33,1},{65,33},{97,65},{34,2},{66,34},{98,6... | collective-permute-start | bytes 4616 | tf_op jit(solution)/shard_map/ppermute | solution.py:22
  26.4 10.2 %collective-permute-start.8 = (bf16[24,16,8]{2,0,1:T(8,128)(2,1)S(1)}, bf16[24,16,8]{2,0,1:T(8,128)(2,1)S(1)}, u32[]{:S(2)}, u32[]{:S(2)}) collective-permute-start(bf16[24,16,8]{2,0,1:T(8,128)(2,1)S(1)} %get-tuple-element.444), channel_id=1, source_target_pairs={{0,32},{32,64},{64,96},{1,33},{33,65},{65,97},{2,34},{34,66},{66,9... | collective-permute-start | bytes 18440 | tf_op jit(solution)/shard_map/ppermute | solution.py:19
  32.1 10.2 %collective-permute-start.6 = (bf16[24,2,260]{2,0,1:T(8,128)(2,1)S(1)}, bf16[24,2,260]{2,0,1:T(8,128)(2,1)S(1)}, u32[]{:S(2)}, u32[]{:S(2)}) collective-permute-start(bf16[24,2,260]{2,0,1:T(8,128)(2,1)S(1)} %get-tuple-element.422), channel_id=1, source_target_pairs={{0,1},{1,2},{2,3},{3,4},{4,5},{5,6},{6,7},{7,8},{8,9},{9,10},{10,1... | collective-permute-start | bytes 74888 | tf_op jit(solution)/shard_map/ppermute | solution.py:19
  35.3 7.0 %collective-permute-start.7 = (bf16[24,2,260]{2,0,1:T(8,128)(2,1)S(1)}, bf16[24,2,260]{2,0,1:T(8,128)(2,1)S(1)}, u32[]{:S(2)}, u32[]{:S(2)}) collective-permute-start(bf16[24,2,260]{2,0,1:T(8,128)(2,1)S(1)} %get-tuple-element.423), channel_id=1, source_target_pairs={{1,0},{2,1},{3,2},{4,3},{5,4},{6,5},{7,6},{8,7},{9,8},{10,9},{11,1... | collective-permute-start | bytes 74888 | tf_op jit(solution)/shard_map/ppermute | solution.py:22
  41.0 10.2 %collective-permute-start.11 = (bf16[24,8,272]{2,0,1:T(8,128)(2,1)S(1)}, bf16[24,8,272]{2,0,1:T(8,128)(2,1)S(1)}, u32[]{:S(2)}, u32[]{:S(2)}) collective-permute-start(bf16[24,8,272]{2,0,1:T(8,128)(2,1)S(1)} %get-tuple-element.431), channel_id=1, source_target_pairs={{1,0},{2,1},{3,2},{4,3},{5,4},{6,5},{7,6},{8,7},{9,8},{10,9},{11,1... | collective-permute-start | bytes 313352 | tf_op jit(solution)/shard_map/ppermute | solution.py:22
  190.5 10.6 %collective-permute-start.12 = (bf16[24,16,2]{2,0,1:T(8,128)(2,1)S(1)}, bf16[24,16,2]{2,0,1:T(8,128)(2,1)S(1)}, u32[]{:S(2)}, u32[]{:S(2)}) collective-permute-start(bf16[24,16,2]{2,0,1:T(8,128)(2,1)S(1)} %get-tuple-element.442), channel_id=1, source_target_pairs={{0,32},{32,64},{64,96},{1,33},{33,65},{65,97},{2,34},{34,66},{66,9... | collective-permute-start | bytes 4616 | tf_op jit(solution)/shard_map/ppermute | solution.py:19
  193.5 7.6 %collective-permute-start.13 = (bf16[24,16,2]{2,0,1:T(8,128)(2,1)S(1)}, bf16[24,16,2]{2,0,1:T(8,128)(2,1)S(1)}, u32[]{:S(2)}, u32[]{:S(2)}) collective-permute-start(bf16[24,16,2]{2,0,1:T(8,128)(2,1)S(1)} %get-tuple-element.443), channel_id=1, source_target_pairs={{32,0},{64,32},{96,64},{33,1},{65,33},{97,65},{34,2},{66,34},{98,6... | collective-permute-start | bytes 4616 | tf_op jit(solution)/shard_map/ppermute | solution.py:22
  195.5 8.8 %collective-permute-start.16 = (bf16[24,16,8]{2,0,1:T(8,128)(2,1)S(1)}, bf16[24,16,8]{2,0,1:T(8,128)(2,1)S(1)}, u32[]{:S(2)}, u32[]{:S(2)}) collective-permute-start(bf16[24,16,8]{2,0,1:T(8,128)(2,1)S(1)} %get-tuple-element.440), channel_id=1, source_target_pairs={{0,32},{32,64},{64,96},{1,33},{33,65},{65,97},{2,34},{34,66},{66,9... | collective-permute-start | bytes 18440 | tf_op jit(solution)/shard_map/ppermute | solution.py:19
  201.2 8.6 %collective-permute-start.14 = (bf16[24,2,260]{2,0,1:T(8,128)(2,1)S(1)}, bf16[24,2,260]{2,0,1:T(8,128)(2,1)S(1)}, u32[]{:S(2)}, u32[]{:S(2)}) collective-permute-start(bf16[24,2,260]{2,0,1:T(8,128)(2,1)S(1)} %get-tuple-element.418), channel_id=1, source_target_pairs={{0,1},{1,2},{2,3},{3,4},{4,5},{5,6},{6,7},{7,8},{8,9},{9,10},{10,1... | collective-permute-start | bytes 74888 | tf_op jit(solution)/shard_map/ppermute | solution.py:19
  203.0 6.9 collective-permute-start.15
  208.5 6.9 %collective-permute-start.19 = (bf16[24,8,272]{2,0,1:T(8,128)(2,1)S(1)}, bf16[24,8,272]{2,0,1:T(8,128)(2,1)S(1)}, u32[]{:S(2)}, u32[]{:S(2)}) collective-permute-start(bf16[24,8,272]{2,0,1:T(8,128)(2,1)S(1)} %get-tuple-element.429), channel_id=1, source_target_pairs={{1,0},{2,1},{3,2},{4,3},{5,4},{6,5},{7,6},{8,7},{9,8},{10,9},{11,1... | collective-permute-start | bytes 313352 | tf_op jit(solution)/shard_map/ppermute | solution.py:22
  356.0 9.6 %collective-permute-start.20 = (bf16[24,16,2]{2,0,1:T(8,128)(2,1)S(1)}, bf16[24,16,2]{2,0,1:T(8,128)(2,1)S(1)}, u32[]{:S(2)}, u32[]{:S(2)}) collective-permute-start(bf16[24,16,2]{2,0,1:T(8,128)(2,1)S(1)} %get-tuple-element.438), channel_id=1, source_target_pairs={{0,32},{32,64},{64,96},{1,33},{33,65},{65,97},{2,34},{34,66},{66,9... | collective-permute-start | bytes 4616 | tf_op jit(solution)/shard_map/ppermute | solution.py:19
  358.0 7.6 %collective-permute-start.21 = (bf16[24,16,2]{2,0,1:T(8,128)(2,1)S(1)}, bf16[24,16,2]{2,0,1:T(8,128)(2,1)S(1)}, u32[]{:S(2)}, u32[]{:S(2)}) collective-permute-start(bf16[24,16,2]{2,0,1:T(8,128)(2,1)S(1)} %get-tuple-element.439), channel_id=1, source_target_pairs={{32,0},{64,32},{96,64},{33,1},{65,33},{97,65},{34,2},{66,34},{98,6... | collective-permute-start | bytes 4616 | tf_op jit(solution)/shard_map/ppermute | solution.py:22
  360.5 9.2 %collective-permute-start.24 = (bf16[24,16,8]{2,0,1:T(8,128)(2,1)S(1)}, bf16[24,16,8]{2,0,1:T(8,128)(2,1)S(1)}, u32[]{:S(2)}, u32[]{:S(2)}) collective-permute-start(bf16[24,16,8]{2,0,1:T(8,128)(2,1)S(1)} %get-tuple-element.436), channel_id=1, source_target_pairs={{0,32},{32,64},{64,96},{1,33},{33,65},{65,97},{2,34},{34,66},{66,9... | collective-permute-start | bytes 18440 | tf_op jit(solution)/shard_map/ppermute | solution.py:19
  365.8 9.4 %collective-permute-start.22 = (bf16[24,2,260]{2,0,1:T(8,128)(2,1)S(1)}, bf16[24,2,260]{2,0,1:T(8,128)(2,1)S(1)}, u32[]{:S(2)}, u32[]{:S(2)}) collective-permute-start(bf16[24,2,260]{2,0,1:T(8,128)(2,1)S(1)} %get-tuple-element.416), channel_id=1, source_target_pairs={{0,1},{1,2},{2,3},{3,4},{4,5},{5,6},{6,7},{7,8},{8,9},{9,10},{10,1... | collective-permute-start | bytes 74888 | tf_op jit(solution)/shard_map/ppermute | solution.py:19
  373.9 6.9 %collective-permute-start.27 = (bf16[24,8,272]{2,0,1:T(8,128)(2,1)S(1)}, bf16[24,8,272]{2,0,1:T(8,128)(2,1)S(1)}, u32[]{:S(2)}, u32[]{:S(2)}) collective-permute-start(bf16[24,8,272]{2,0,1:T(8,128)(2,1)S(1)} %get-tuple-element.427), channel_id=1, source_target_pairs={{1,0},{2,1},{3,2},{4,3},{5,4},{6,5},{7,6},{8,7},{9,8},{10,9},{11,1... | collective-permute-start | bytes 313352 | tf_op jit(solution)/shard_map/ppermute | solution.py:22
  521.0 9.5 %collective-permute-start.28 = (bf16[24,16,2]{2,0,1:T(8,128)(2,1)S(1)}, bf16[24,16,2]{2,0,1:T(8,128)(2,1)S(1)}, u32[]{:S(2)}, u32[]{:S(2)}) collective-permute-start(bf16[24,16,2]{2,0,1:T(8,128)(2,1)S(1)} %get-tuple-element.434), channel_id=1, source_target_pairs={{0,32},{32,64},{64,96},{1,33},{33,65},{65,97},{2,34},{34,66},{66,9... | collective-permute-start | bytes 4616 | tf_op jit(solution)/shard_map/ppermute | solution.py:19
  523.0 7.6 %collective-permute-start.29 = (bf16[24,16,2]{2,0,1:T(8,128)(2,1)S(1)}, bf16[24,16,2]{2,0,1:T(8,128)(2,1)S(1)}, u32[]{:S(2)}, u32[]{:S(2)}) collective-permute-start(bf16[24,16,2]{2,0,1:T(8,128)(2,1)S(1)} %get-tuple-element.435), channel_id=1, source_target_pairs={{32,0},{64,32},{96,64},{33,1},{65,33},{97,65},{34,2},{66,34},{98,6... | collective-permute-start | bytes 4616 | tf_op jit(solution)/shard_map/ppermute | solution.py:22
  525.5 9.2 %collective-permute-start.32 = (bf16[24,16,8]{2,0,1:T(8,128)(2,1)S(1)}, bf16[24,16,8]{2,0,1:T(8,128)(2,1)S(1)}, u32[]{:S(2)}, u32[]{:S(2)}) collective-permute-start(bf16[24,16,8]{2,0,1:T(8,128)(2,1)S(1)} %get-tuple-element.432), channel_id=1, source_target_pairs={{0,32},{32,64},{64,96},{1,33},{33,65},{65,97},{2,34},{34,66},{66,9... | collective-permute-start | bytes 18440 | tf_op jit(solution)/shard_map/ppermute | solution.py:19
  530.7 9.5 %collective-permute-start.30 = (bf16[24,2,260]{2,0,1:T(8,128)(2,1)S(1)}, bf16[24,2,260]{2,0,1:T(8,128)(2,1)S(1)}, u32[]{:S(2)}, u32[]{:S(2)}) collective-permute-start(bf16[24,2,260]{2,0,1:T(8,128)(2,1)S(1)} %get-tuple-element.414), channel_id=1, source_target_pairs={{0,1},{1,2},{2,3},{3,4},{4,5},{5,6},{6,7},{7,8},{8,9},{9,10},{10,1... | collective-permute-start | bytes 74888 | tf_op jit(solution)/shard_map/ppermute | solution.py:19
  534.9 7.0 %collective-permute-start.34 = (bf16[24,8,272]{2,0,1:T(8,128)(2,1)S(1)}, bf16[24,8,272]{2,0,1:T(8,128)(2,1)S(1)}, u32[]{:S(2)}, u32[]{:S(2)}) collective-permute-start(bf16[24,8,272]{2,0,1:T(8,128)(2,1)S(1)} %get-tuple-element.424), channel_id=1, source_target_pairs={{0,1},{1,2},{2,3},{3,4},{4,5},{5,6},{6,7},{7,8},{8,9},{9,10},{10,1... | collective-permute-start | bytes 313352 | tf_op jit(solution)/shard_map/ppermute | solution.py:19
  538.9 6.9 %collective-permute-start.35 = (bf16[24,8,272]{2,0,1:T(8,128)(2,1)S(1)}, bf16[24,8,272]{2,0,1:T(8,128)(2,1)S(1)}, u32[]{:S(2)}, u32[]{:S(2)}) collective-permute-start(bf16[24,8,272]{2,0,1:T(8,128)(2,1)S(1)} %get-tuple-element.425), channel_id=1, source_target_pairs={{1,0},{2,1},{3,2},{4,3},{5,4},{6,5},{7,6},{8,7},{9,8},{10,9},{11,1... | collective-permute-start | bytes 313352 | tf_op jit(solution)/shard_map/ppermute | solution.py:22
  (49 other events, 1758.2 us)
where the time goes:
time: 698 us; the launch traced here: 689 us
  blocking collectives  302 us (43%)
  local copies, waits for them, and re-layouts  136 us (19%)
  matrix products  123 us (18%)
  starting transfers between devices  87.5 us (13%)
  waiting for transfers between devices  28.1 us (4%)
  other arithmetic  9.43 us (1%)
    psum x4, blocking collectives, local(): lax.psum(jnp.sum(raw_forcing * wet_two, axis=(1, 2)), ('sec', 'lat'))  302 us
    dot_general x80, matrix products, conv_layer(): jnp.einsum('oc,crx->orx', weight[shift_y], stacked, preferred_element_typ...  121 us
    unnamed x140, local copies, waits for them, and re-layouts  104 us
    ppermute x18, starting transfers between devices, padded_2(): lax.ppermute(lax.slice_in_dim(block, block.shape[dim] - width, None, axis...  57.7 us
    concatenate x16, local copies, waits for them, and re-layouts, conv_layer(): jnp.concatenate([row_band[:, :, shift_x:shift_x + out_cols] for shift_x i...  30 us
    ppermute x18, starting transfers between devices, padded_2(): lax.ppermute(lax.slice_in_dim(block, 0, width, axis=dim), axis, backward)  29.8 us
    ppermute x18, waiting for transfers between devices, padded_2(): lax.ppermute(lax.slice_in_dim(block, 0, width, axis=dim), axis, backward)  26.6 us
  transfers between devices with their start and end apart: 36, of which 10 were waited for; matrix products, arithmetic and copies ran while one was open for 1% of the time, Pallas kernels for 0%

commit v1 on v0

--- a/solution.py
+++ b/solution.py
@@ -22,6 +22,15 @@
         high = lax.ppermute(lax.slice_in_dim(block, 0, width, axis=dim), axis, backward)
         block = jnp.concatenate([low, block, high], axis=dim)
     return block
+
+
+def total(values):
+    count = lax.axis_size("sec") * lax.axis_size("lat")
+    width = values.shape[0]
+    row = jnp.pad(values, (0, 128 - width))
+    copies = jnp.broadcast_to(row[None, None, :], (count, 1, 128))
+    received = lax.all_to_all(copies, ("sec", "lat"), 0, 0)
+    return jnp.sum(received, axis=(0, 1))[:width]
 
 
 def coupling(count_levels):
@@ -97,8 +106,7 @@
     wet_cycle = wet_ext[:, 6:-6, 6:-6]
     wet_two = jnp.concatenate([wet_mask, wet_mask], axis=0)
     wet_three = jnp.concatenate([wet_mask, wet_mask, wet_mask], axis=0)
-    counts = jnp.maximum(lax.psum(jnp.sum(wet_mask, axis=(1, 2)), ("sec", "lat")), 1.0)
-    counts_two = jnp.concatenate([counts, counts])
+    counts_two = None
     global_rows = row_start + lax.broadcasted_iota(jnp.int32, (1, dev_rows, 1), 1)
     coriolis = 0.3 + 0.5 * global_rows.astype(jnp.float32) / grid_rows
     coupling_matrix = coupling(LEVELS)
@@ -106,9 +114,7 @@
     forcing = jnp.zeros((2 * LEVELS, dev_rows, dev_cols), jnp.float32)
     for step_index in range(STEPS):
         net_in = padded_2(state.astype(jnp.bfloat16), (("sec", 2), ("lat", 1)), 8)
-        ocean_in = padded_2(state.astype(jnp.bfloat16), (("sec", 2), ("lat", 1)), 2).astype(
-            state.dtype
-        )
+        ocean_in = net_in[:, 6:-6, 6:-6].astype(state.dtype)
         hidden = net_in
         for weight, offset, margin in (
             (conv1_weight, conv1_bias, 6),
@@ -121,7 +127,14 @@
             ]
             hidden = (activation * sea_part).astype(jnp.bfloat16)
         raw_forcing = conv_layer(hidden, conv4_weight)
-        wet_sums = lax.psum(jnp.sum(raw_forcing * wet_two, axis=(1, 2)), ("sec", "lat"))
+        wet_sums = jnp.sum(raw_forcing * wet_two, axis=(1, 2))
+        if counts_two is None:
+            both = total(jnp.concatenate([wet_sums, jnp.sum(wet_mask, axis=(1, 2))]))
+            wet_sums = both[: 2 * LEVELS]
+            counts = jnp.maximum(both[2 * LEVELS :], 1.0)
+            counts_two = jnp.concatenate([counts, counts])
+        else:
+            wet_sums = total(wet_sums)
         forcing = (raw_forcing - (wet_sums / counts_two)[:, None, None]) * wet_two
         state = ocean_step(ocean_in, wet_cycle, forcing, coriolis, coupling_matrix)
     return (state, forcing)

time: 698 us -> 456 us (0.65)
  blocking collectives: 302 us -> 0 us
  waiting for transfers between devices: 28.1 us -> 75 us
  starting transfers between devices: 87.5 us -> 102 us
    psum x4 -> x0, blocking collectives: 302 us -> none  [local(): lax.psum(jnp.sum(raw_forcing * wet_two, axis=(1, 2)), ('sec', 'lat'))]
    all_to_all x0 -> x4, starting transfers between devices: none -> 56.7 us  [total(): received = lax.all_to_all(copies, ('sec', 'lat'), 0, 0)]
    all_to_all x0 -> x4, waiting for transfers between devices: none -> 34.7 us  [total(): received = lax.all_to_all(copies, ('sec', 'lat'), 0, 0)]
    ppermute x18 -> x10, starting transfers between devices: 57.7 us -> 29.2 us  [padded_2(): lax.ppermute(lax.slice_in_dim(block, block.shape[dim] - width, None, axis...]
    ppermute x18 -> x10, starting transfers between devices: 29.8 us -> 16.1 us  [padded_2(): lax.ppermute(lax.slice_in_dim(block, 0, width, axis=dim), axis, backward)]
    ppermute x18 -> x10, waiting for transfers between devices: 26.6 us -> 37.3 us  [padded_2(): lax.ppermute(lax.slice_in_dim(block, 0, width, axis=dim), axis, backward)]
    unnamed x140 -> x110, local copies, waits for them, and re-layouts: 104 us -> 104 us
  transfers between devices with their start and end apart: 36 -> 24, of which waited for: 10 -> 18; matrix products, arithmetic and copies ran while one was open for 1% -> 1% of each run, Pallas kernels for 0% -> 0%
where the time goes in v1:
time: 456 us; the launch traced here: 449 us
  local copies, waits for them, and re-layouts  138 us (30%)
  matrix products  123 us (27%)
  starting transfers between devices  102 us (22%)
  waiting for transfers between devices  75 us (16%)
  other arithmetic  9.16 us (2%)
    dot_general x80, matrix products, conv_layer(): jnp.einsum('oc,crx->orx', weight[shift_y], stacked, preferred_element_typ...  121 us
    unnamed x110, local copies, waits for them, and re-layouts  104 us
    all_to_all x4, starting transfers between devices, total(): received = lax.all_to_all(copies, ('sec', 'lat'), 0, 0)  56.7 us
    ppermute x10, waiting for transfers between devices, padded_2(): lax.ppermute(lax.slice_in_dim(block, 0, width, axis=dim), axis, backward)  37.3 us
    all_to_all x4, waiting for transfers between devices, total(): received = lax.all_to_all(copies, ('sec', 'lat'), 0, 0)  34.7 us
    concatenate x16, local copies, waits for them, and re-layouts, conv_layer(): jnp.concatenate([row_band[:, :, shift_x:shift_x + out_cols] for shift_x i...  29.9 us
    ppermute x10, starting transfers between devices, padded_2(): lax.ppermute(lax.slice_in_dim(block, block.shape[dim] - width, None, axis...  29.2 us
    ppermute x10, starting transfers between devices, padded_2(): lax.ppermute(lax.slice_in_dim(block, 0, width, axis=dim), axis, backward)  16.1 us
  transfers between devices with their start and end apart: 24, of which 18 were waited for; matrix products, arithmetic and copies ran while one was open for 1% of the time, Pallas kernels for 0%

profile of v1, /device:TPU:1, one launch (start us, length us, event | category | flops | bytes accessed | tf_op | source)
XLA Modules:
  0.0 449.3 jit_solution(16924008831330700038)
XLA Ops:
  1.4 4.9 %collective-permute-start = (s32[16,8]{1,0:T(8,128)S(1)}, s32[16,8]{1,0:T(8,128)S(1)}, u32[]{:S(2)}, u32[]{:S(2)}) collective-permute-start(s32[16,8]{1,0:T(8,128)S(1)} %get-tuple-element.436), channel_id=1, source_target_pairs={{0,32},{32,64},{64,96},{1,33},{33,65},{65,97},{2,34},{34,66},{66,9... | collective-permute-start | bytes 1544 | tf_op jit(solution)/shard_map/ppermute | solution.py:19
  52.3 4.3 slice_dynamic-update-slice_fusion.78
  56.6 4.3 slice_dynamic-update-slice_fusion.77
  61.0 4.3 slice_dynamic-update-slice_fusion.76
  65.3 4.5 slice_dynamic-update-slice_fusion.75
  104.3 16.6 %all-to-all-start = ((f32[128,1,128]{2,1,0:T(1,128)}), f32[128,1,128]{2,1,0:T(1,128)S(1)}, u32[]{:S(2)}, u32[]{:S(2)}) async-start(f32[128,1,128]{2,1,0:T(1,128)} %broadcast_in_dim.8), calls=%async_computation | async-start | bytes 131072 | tf_op jit(solution)/shard_map/all_to_all | solution.py:32
  121.7 8.7 %all-to-all-done = f32[128,1,128]{2,1,0:T(1,128)S(1)} async-done(((f32[128,1,128]{2,1,0:T(1,128)}), f32[128,1,128]{2,1,0:T(1,128)S(1)}, u32[]{:S(2)}, u32[]{:S(2)}) %all-to-all-start) | async-done | bytes 65568 | tf_op jit(solution)/shard_map/all_to_all | solution.py:32
  165.1 4.3 slice_dynamic-update-slice_fusion.52
  169.5 4.3 slice_dynamic-update-slice_fusion.51
  173.8 4.7 %slice_dynamic-update-slice_fusion.50 = (bf16[640,24,264]{0,2,1:T(8,128)(2,1)}, bf16[640,24,264]{0,2,1:T(8,128)(2,1)S(1)}, bf16[640,24,264]{0,2,1:T(8,128)(2,1)S...) fusion(bf16[640,24,264]{0,2,1:T(8,128)(2,1)} %get-tuple-element.63, ...), kind=kLoop, calls=%fused_computation.106 | loop fusion | bytes 16220160 | tf_op jit(solution)/shard_map/concatenate | solution.py:48
  212.6 13.4 %all-to-all-start.1 = ((f32[128,1,128]{2,1,0:T(1,128)}), f32[128,1,128]{2,1,0:T(1,128)S(1)}, u32[]{:S(2)}, u32[]{:S(2)}) async-start(f32[128,1,128]{2,1,0:T(1,128)} %broadcast_in_dim.9), calls=%async_computation.1 | async-start | bytes 131072 | tf_op jit(solution)/shard_map/all_to_all | solution.py:32
  226.8 8.7 %all-to-all-done.1 = f32[128,1,128]{2,1,0:T(1,128)S(1)} async-done(((f32[128,1,128]{2,1,0:T(1,128)}), f32[128,1,128]{2,1,0:T(1,128)S(1)}, u32[]{:S(2)}, u32[]{:S(2)}) %all-to-all-start.1) | async-done | bytes 65568 | tf_op jit(solution)/shard_map/all_to_all | solution.py:32
  266.0 4.3 slice_dynamic-update-slice_fusion.28
  270.3 4.3 slice_dynamic-update-slice_fusion.27
  274.7 4.3 slice_dynamic-update-slice_fusion.26
  279.0 4.4 slice_dynamic-update-slice_fusion.25
  317.7 13.6 %all-to-all-start.2 = ((f32[128,1,128]{2,1,0:T(1,128)}), f32[128,1,128]{2,1,0:T(1,128)S(1)}, u32[]{:S(2)}, u32[]{:S(2)}) async-start(f32[128,1,128]{2,1,0:T(1,128)} %broadcast_in_dim.10), calls=%async_computation.2 | async-start | bytes 131072 | tf_op jit(solution)/shard_map/all_to_all | solution.py:32
  332.1 8.7 %all-to-all-done.2 = f32[128,1,128]{2,1,0:T(1,128)S(1)} async-done(((f32[128,1,128]{2,1,0:T(1,128)}), f32[128,1,128]{2,1,0:T(1,128)S(1)}, u32[]{:S(2)}, u32[]{:S(2)}) %all-to-all-start.2) | async-done | bytes 65568 | tf_op jit(solution)/shard_map/all_to_all | solution.py:32
  372.1 4.3 slice_dynamic-update-slice_fusion.3
  376.4 4.3 slice_dynamic-update-slice_fusion.2
  380.7 4.3 slice_dynamic-update-slice_fusion.1
  385.1 4.5 slice_dynamic-update-slice_fusion
  424.0 13.1 %all-to-all-start.3 = ((f32[128,1,128]{2,1,0:T(1,128)}), f32[128,1,128]{2,1,0:T(1,128)S(1)}, u32[]{:S(2)}, u32[]{:S(2)}) async-start(f32[128,1,128]{2,1,0:T(1,128)} %broadcast_in_dim.11), calls=%async_computation.3 | async-start | bytes 131072 | tf_op jit(solution)/shard_map/all_to_all | solution.py:32
  438.0 8.7 %all-to-all-done.3 = f32[128,1,128]{2,1,0:T(1,128)S(1)} async-done(((f32[128,1,128]{2,1,0:T(1,128)}), f32[128,1,128]{2,1,0:T(1,128)S(1)}, u32[]{:S(2)}, u32[]{:S(2)}) %all-to-all-start.3) | async-done | bytes 65568 | tf_op jit(solution)/shard_map/all_to_all | solution.py:32
  (309 shorter events, 284.6 us)
Async XLA Ops:
  1.4 6.9 %collective-permute-start = (s32[16,8]{1,0:T(8,128)S(1)}, s32[16,8]{1,0:T(8,128)S(1)}, u32[]{:S(2)}, u32[]{:S(2)}) collective-permute-start(s32[16,8]{1,0:T(8,128)S(1)} %get-tuple-element.436), channel_id=1, source_target_pairs={{0,32},{32,64},{64,96},{1,33},{33,65},{65,97},{2,34},{34,66},{66,9... | collective-permute-start | bytes 1544 | tf_op jit(solution)/shard_map/ppermute | solution.py:19
  6.4 5.0 %collective-permute-start.1 = (s32[16,8]{1,0:T(8,128)S(1)}, s32[16,8]{1,0:T(8,128)S(1)}, u32[]{:S(2)}, u32[]{:S(2)}) collective-permute-start(s32[16,8]{1,0:T(8,128)S(1)} %get-tuple-element.437), channel_id=1, source_target_pairs={{32,0},{64,32},{96,64},{33,1},{65,33},{97,65},{34,2},{66,34},{98,6... | collective-permute-start | bytes 1544 | tf_op jit(solution)/shard_map/ppermute | solution.py:22
  11.4 4.6 %collective-permute-start.2 = (s32[8,272]{1,0:T(8,128)S(1)}, s32[8,272]{1,0:T(8,128)S(1)}, u32[]{:S(2)}, u32[]{:S(2)}) collective-permute-start(s32[8,272]{1,0:T(8,128)S(1)} %get-tuple-element.434), channel_id=1, source_target_pairs={{0,1},{1,2},{2,3},{3,4},{4,5},{5,6},{6,7},{7,8},{8,9},{9,10},{10,1... | collective-permute-start | bytes 26120 | tf_op jit(solution)/shard_map/ppermute | solution.py:19
  14.6 4.4 collective-permute-start.3
  20.7 5.5 %collective-permute-start.4 = (bf16[24,16,8]{2,0,1:T(8,128)(2,1)S(1)}, bf16[24,16,8]{2,0,1:T(8,128)(2,1)S(1)}, u32[]{:S(2)}, u32[]{:S(2)}) collective-permute-start(bf16[24,16,8]{2,0,1:T(8,128)(2,1)S(1)} %get-tuple-element.432), channel_id=1, source_target_pairs={{0,32},{32,64},{64,96},{1,33},{33,65},{65,97},{2,34},{34,66},{66,9... | collective-permute-start | bytes 18440 | tf_op jit(solution)/shard_map/ppermute | solution.py:19
  24.1 5.9 %collective-permute-start.5 = (bf16[24,16,8]{2,0,1:T(8,128)(2,1)S(1)}, bf16[24,16,8]{2,0,1:T(8,128)(2,1)S(1)}, u32[]{:S(2)}, u32[]{:S(2)}) collective-permute-start(bf16[24,16,8]{2,0,1:T(8,128)(2,1)S(1)} %get-tuple-element.433), channel_id=1, source_target_pairs={{32,0},{64,32},{96,64},{33,1},{65,33},{97,65},{34,2},{66,34},{98,6... | collective-permute-start | bytes 18440 | tf_op jit(solution)/shard_map/ppermute | solution.py:22
  30.3 5.3 %collective-permute-start.6 = (bf16[24,8,272]{2,0,1:T(8,128)(2,1)S(1)}, bf16[24,8,272]{2,0,1:T(8,128)(2,1)S(1)}, u32[]{:S(2)}, u32[]{:S(2)}) collective-permute-start(bf16[24,8,272]{2,0,1:T(8,128)(2,1)S(1)} %get-tuple-element.424), channel_id=1, source_target_pairs={{0,1},{1,2},{2,3},{3,4},{4,5},{5,6},{6,7},{7,8},{8,9},{9,10},{10,1... | collective-permute-start | bytes 313352 | tf_op jit(solution)/shard_map/ppermute | solution.py:19
  33.5 6.1 %collective-permute-start.7 = (bf16[24,8,272]{2,0,1:T(8,128)(2,1)S(1)}, bf16[24,8,272]{2,0,1:T(8,128)(2,1)S(1)}, u32[]{:S(2)}, u32[]{:S(2)}) collective-permute-start(bf16[24,8,272]{2,0,1:T(8,128)(2,1)S(1)} %get-tuple-element.425), channel_id=1, source_target_pairs={{1,0},{2,1},{3,2},{4,3},{5,4},{6,5},{7,6},{8,7},{9,8},{10,9},{11,1... | collective-permute-start | bytes 313352 | tf_op jit(solution)/shard_map/ppermute | solution.py:22
  104.3 26.1 %all-to-all-start = ((f32[128,1,128]{2,1,0:T(1,128)}), f32[128,1,128]{2,1,0:T(1,128)S(1)}, u32[]{:S(2)}, u32[]{:S(2)}) async-start(f32[128,1,128]{2,1,0:T(1,128)} %broadcast_in_dim.8), calls=%async_computation | async-start | bytes 131072 | tf_op jit(solution)/shard_map/all_to_all | solution.py:32
  131.1 5.1 %collective-permute-start.8 = (bf16[24,16,8]{2,0,1:T(8,128)(2,1)S(1)}, bf16[24,16,8]{2,0,1:T(8,128)(2,1)S(1)}, u32[]{:S(2)}, u32[]{:S(2)}) collective-permute-start(bf16[24,16,8]{2,0,1:T(8,128)(2,1)S(1)} %get-tuple-element.430), channel_id=1, source_target_pairs={{0,32},{32,64},{64,96},{1,33},{33,65},{65,97},{2,34},{34,66},{66,9... | collective-permute-start | bytes 18440 | tf_op jit(solution)/shard_map/ppermute | solution.py:19
  134.3 5.9 %collective-permute-start.9 = (bf16[24,16,8]{2,0,1:T(8,128)(2,1)S(1)}, bf16[24,16,8]{2,0,1:T(8,128)(2,1)S(1)}, u32[]{:S(2)}, u32[]{:S(2)}) collective-permute-start(bf16[24,16,8]{2,0,1:T(8,128)(2,1)S(1)} %get-tuple-element.431), channel_id=1, source_target_pairs={{32,0},{64,32},{96,64},{33,1},{65,33},{97,65},{34,2},{66,34},{98,6... | collective-permute-start | bytes 18440 | tf_op jit(solution)/shard_map/ppermute | solution.py:22
  140.5 3.7 collective-permute-start.10
  142.1 5.9 %collective-permute-start.11 = (bf16[24,8,272]{2,0,1:T(8,128)(2,1)S(1)}, bf16[24,8,272]{2,0,1:T(8,128)(2,1)S(1)}, u32[]{:S(2)}, u32[]{:S(2)}) collective-permute-start(bf16[24,8,272]{2,0,1:T(8,128)(2,1)S(1)} %get-tuple-element.423), channel_id=1, source_target_pairs={{1,0},{2,1},{3,2},{4,3},{5,4},{6,5},{7,6},{8,7},{9,8},{10,9},{11,1... | collective-permute-start | bytes 313352 | tf_op jit(solution)/shard_map/ppermute | solution.py:22
  212.6 22.9 %all-to-all-start.1 = ((f32[128,1,128]{2,1,0:T(1,128)}), f32[128,1,128]{2,1,0:T(1,128)S(1)}, u32[]{:S(2)}, u32[]{:S(2)}) async-start(f32[128,1,128]{2,1,0:T(1,128)} %broadcast_in_dim.9), calls=%async_computation.1 | async-start | bytes 131072 | tf_op jit(solution)/shard_map/all_to_all | solution.py:32
  236.2 5.1 %collective-permute-start.12 = (bf16[24,16,8]{2,0,1:T(8,128)(2,1)S(1)}, bf16[24,16,8]{2,0,1:T(8,128)(2,1)S(1)}, u32[]{:S(2)}, u32[]{:S(2)}) collective-permute-start(bf16[24,16,8]{2,0,1:T(8,128)(2,1)S(1)} %get-tuple-element.428), channel_id=1, source_target_pairs={{0,32},{32,64},{64,96},{1,33},{33,65},{65,97},{2,34},{34,66},{66,9... | collective-permute-start | bytes 18440 | tf_op jit(solution)/shard_map/ppermute | solution.py:19
  239.3 5.9 %collective-permute-start.13 = (bf16[24,16,8]{2,0,1:T(8,128)(2,1)S(1)}, bf16[24,16,8]{2,0,1:T(8,128)(2,1)S(1)}, u32[]{:S(2)}, u32[]{:S(2)}) collective-permute-start(bf16[24,16,8]{2,0,1:T(8,128)(2,1)S(1)} %get-tuple-element.429), channel_id=1, source_target_pairs={{32,0},{64,32},{96,64},{33,1},{65,33},{97,65},{34,2},{66,34},{98,6... | collective-permute-start | bytes 18440 | tf_op jit(solution)/shard_map/ppermute | solution.py:22
  245.5 3.7 collective-permute-start.14
  247.2 5.9 %collective-permute-start.15 = (bf16[24,8,272]{2,0,1:T(8,128)(2,1)S(1)}, bf16[24,8,272]{2,0,1:T(8,128)(2,1)S(1)}, u32[]{:S(2)}, u32[]{:S(2)}) collective-permute-start(bf16[24,8,272]{2,0,1:T(8,128)(2,1)S(1)} %get-tuple-element.421), channel_id=1, source_target_pairs={{1,0},{2,1},{3,2},{4,3},{5,4},{6,5},{7,6},{8,7},{9,8},{10,9},{11,1... | collective-permute-start | bytes 313352 | tf_op jit(solution)/shard_map/ppermute | solution.py:22
  317.7 23.1 %all-to-all-start.2 = ((f32[128,1,128]{2,1,0:T(1,128)}), f32[128,1,128]{2,1,0:T(1,128)S(1)}, u32[]{:S(2)}, u32[]{:S(2)}) async-start(f32[128,1,128]{2,1,0:T(1,128)} %broadcast_in_dim.10), calls=%async_computation.2 | async-start | bytes 131072 | tf_op jit(solution)/shard_map/all_to_all | solution.py:32
  341.4 5.1 %collective-permute-start.16 = (bf16[24,16,8]{2,0,1:T(8,128)(2,1)S(1)}, bf16[24,16,8]{2,0,1:T(8,128)(2,1)S(1)}, u32[]{:S(2)}, u32[]{:S(2)}) collective-permute-start(bf16[24,16,8]{2,0,1:T(8,128)(2,1)S(1)} %get-tuple-element.426), channel_id=1, source_target_pairs={{0,32},{32,64},{64,96},{1,33},{33,65},{65,97},{2,34},{34,66},{66,9... | collective-permute-start | bytes 18440 | tf_op jit(solution)/shard_map/ppermute | solution.py:19
  344.6 5.9 %collective-permute-start.17 = (bf16[24,16,8]{2,0,1:T(8,128)(2,1)S(1)}, bf16[24,16,8]{2,0,1:T(8,128)(2,1)S(1)}, u32[]{:S(2)}, u32[]{:S(2)}) collective-permute-start(bf16[24,16,8]{2,0,1:T(8,128)(2,1)S(1)} %get-tuple-element.427), channel_id=1, source_target_pairs={{32,0},{64,32},{96,64},{33,1},{65,33},{97,65},{34,2},{66,34},{98,6... | collective-permute-start | bytes 18440 | tf_op jit(solution)/shard_map/ppermute | solution.py:22
  350.7 3.7 collective-permute-start.18
  352.4 5.9 %collective-permute-start.19 = (bf16[24,8,272]{2,0,1:T(8,128)(2,1)S(1)}, bf16[24,8,272]{2,0,1:T(8,128)(2,1)S(1)}, u32[]{:S(2)}, u32[]{:S(2)}) collective-permute-start(bf16[24,8,272]{2,0,1:T(8,128)(2,1)S(1)} %get-tuple-element.419), channel_id=1, source_target_pairs={{1,0},{2,1},{3,2},{4,3},{5,4},{6,5},{7,6},{8,7},{9,8},{10,9},{11,1... | collective-permute-start | bytes 313352 | tf_op jit(solution)/shard_map/ppermute | solution.py:22
  424.0 22.6 %all-to-all-start.3 = ((f32[128,1,128]{2,1,0:T(1,128)}), f32[128,1,128]{2,1,0:T(1,128)S(1)}, u32[]{:S(2)}, u32[]{:S(2)}) async-start(f32[128,1,128]{2,1,0:T(1,128)} %broadcast_in_dim.11), calls=%async_computation.3 | async-start | bytes 131072 | tf_op jit(solution)/shard_map/all_to_all | solution.py:32
  (22 other events, 372.7 us)

commit v2 on v0

v2 whole, which is shorter than its diff:
```python
import functools

import jax
import jax.numpy as jnp
from jax import lax
from jax.experimental import pallas as pl
from jax.experimental.pallas import tpu as pltpu
from jax.sharding import PartitionSpec as P

LEVELS = 8
STEPS = 4
HALO = 8
TIME_STEP = 0.3
DRAG = 0.05
ROWS = 16
COLS = 256
EXT_ROWS = ROWS + 2 * HALO
WIDE = COLS + 128
SPAN = COLS + 2 * HALO
F32 = jnp.float32
BF16 = jnp.bfloat16


def banded(weight, in_pad, out_pad):
    out_width = weight.shape[1]
    in_width = weight.shape[2] // 5
    taps = weight.reshape(5, out_width, 5, in_width).transpose(2, 0, 3, 1)
    taps = jnp.pad(taps, ((0, 0), (0, 0), (0, in_pad - in_width), (0, 0)))
    bands = [jnp.pad(taps, ((0, 0), (j, 3 - j), (0, 0), (0, 0))) for j in range(4)]
    band = jnp.concatenate(bands, axis=3)
    halves = [
        band[:, 4 * i : 4 * i + 4].reshape(5 * 4 * in_pad, 4 * out_width) for i in range(2)
    ]
    full = jnp.concatenate(halves, axis=0)
    return jnp.pad(full, ((0, 0), (0, out_pad - 4 * out_width)))


def conv_rows(in_ref, weight_ref, group, count):
    lhs = jnp.concatenate([in_ref[group, 0:count, :], in_ref[group + 1, 0:count, :]], axis=1)
    return jnp.dot(lhs, weight_ref[...], preferred_element_type=F32)


def spread(value, work_ref, out_ref, group, width):
    work_ref[0:SPAN, 0:width] = value
    for shift in range(5):
        out_ref[group, :, shift * width : (shift + 1) * width] = work_ref[
            shift : shift + SPAN, 0:width
        ].astype(BF16)


def conv_layer(in_ref, weight_ref, bias_ref, sea_ref, work_ref, out_ref, layer, groups):
    width = weight_ref.shape[1]

    def body(group, carry):
        total = conv_rows(in_ref, weight_ref, group, SPAN)
        row_of = lax.broadcasted_iota(jnp.int32, (128, width), 0)
        lane_of = lax.broadcasted_iota(jnp.int32, (128, width), 1)
        wanted = 4 * group + 2 * (layer + 1) + lane_of // (width // 4)
        pick = jnp.where(row_of == wanted, 1.0, 0.0).astype(BF16)
        sea = jnp.dot(sea_ref[layer], pick, preferred_element_type=F32)
        biased = total + bias_ref[...]
        half = 0.5 * biased
        spread((half + half * jnp.tanh(half)) * sea, work_ref, out_ref, group, width)
        return carry

    lax.fori_loop(0, groups, body, 0)


def device_means(received):
    total = jnp.sum(received, axis=0, keepdims=True)
    column = jnp.transpose(jnp.broadcast_to(total, (128, 128)))
    counts = jnp.maximum(column[16:24], 1.0)
    return column[0:8] / counts, column[8:16] / counts


def step_kernel(*refs, first, last):
    refs = list(refs)
    start_ref = refs.pop(0)
    recv_ref = None if first else refs.pop(0)
    own_ref, left_ref, right_ref, top_ref, bottom_ref, wet_ref, sea_ref = refs[:7]
    w1_ref, w2_ref, w3_ref, w4_ref, b1_ref, b2_ref, b3_ref = refs[7:14]
    refs = refs[14:]
    new_ref = refs.pop(0)
    pay_ref = refs.pop(0)
    if last:
        raw_out_ref = refs.pop(0)
    else:
        send_left_ref = refs.pop(0)
        send_right_ref = refs.pop(0)
    state_ref, a0_ref, a1_ref, a2_ref, a3_ref, work_ref, raw_ref = refs

    lane = lax.broadcasted_iota(jnp.int32, (ROWS * 24, 128), 1)
    sides = jnp.where(lane < 64, right_ref[...].astype(F32), left_ref[...].astype(F32))
    state_ref[:, 24:32, :] = jnp.zeros((EXT_ROWS, 8, WIDE), F32)
    state_ref[HALO : HALO + ROWS, 0:24, 0:COLS] = own_ref[...]
    state_ref[HALO : HALO + ROWS, 0:24, COLS:WIDE] = sides.reshape(ROWS, 24, 128)
    state_ref[0:HALO, 0:24, :] = top_ref[...].astype(F32).reshape(HALO, 24, WIDE)
    state_ref[HALO + ROWS :, 0:24, :] = bottom_ref[...].astype(F32).reshape(HALO, 24, WIDE)
    if not first:
        zonal_mean, merid_mean = device_means(recv_ref[...])
        for base, mean in ((0, zonal_mean), (8, merid_mean)):
            scaled = jnp.concatenate([TIME_STEP * mean] * 3, axis=1)
            state_ref[:, base : base + 8, :] = (
                state_ref[:, base : base + 8, :] - scaled[None] * wet_ref[...]
            )

    work_ref[SPAN:, :] = jnp.zeros((8, 512), F32)
    for group in range(8):
        flat = state_ref[4 * group : 4 * group + 4].reshape(128, WIDE)
        turned = jnp.transpose(flat)
        spread(
            jnp.concatenate([turned[WIDE - HALO :], turned[0 : COLS + HALO]], axis=0),
            work_ref,
            a0_ref,
            group,
            128,
        )
    conv_layer(a0_ref, w1_ref, b1_ref, sea_ref, work_ref, a1_ref, 0, 7)
    conv_layer(a1_ref, w2_ref, b2_ref, sea_ref, work_ref, a2_ref, 1, 6)
    conv_layer(a2_ref, w3_ref, b3_ref, sea_ref, work_ref, a3_ref, 2, 5)
    for group in range(4):
        turned = jnp.transpose(conv_rows(a3_ref, w4_ref, group, COLS))
        raw_ref[4 * group : 4 * group + 4] = turned[0:64].reshape(4, 16, COLS)

    def shifted_difference(field):
        return (pltpu.roll(field, WIDE - 1, 2) - pltpu.roll(field, 1, 2)) * 0.5

    rows = ROWS + 2
    low = HALO - 1
    zonal = state_ref[low : low + rows, 0:8, :]
    merid_above = state_ref[low + 1 : low + 1 + rows, 8:16, :]
    merid_below = state_ref[low - 1 : low - 1 + rows, 8:16, :]
    divergence = shifted_difference(zonal) + (merid_above - merid_below) * 0.5
    thickness = state_ref[low : low + rows, 16:24, :]
    h_new = (thickness - TIME_STEP * divergence) * wet_ref[low : low + rows]
    level = lax.broadcasted_iota(jnp.int32, (1, 8, 1), 1)
    pressure = None
    for other in range(LEVELS):
        weight = 0.5 + 0.1 * jnp.minimum(level, other).astype(F32)
        term = weight * h_new[:, other : other + 1, :]
        pressure = term if pressure is None else pressure + term
    grad_x = shifted_difference(pressure[1:-1])[:, :, 0:COLS]
    grad_y = ((pressure[2:] - pressure[:-2]) * 0.5)[:, :, 0:COLS]
    wet = wet_ref[HALO : HALO + ROWS, :, 0:COLS]
    zonal_mid = state_ref[HALO : HALO + ROWS, 0:8, 0:COLS]
    merid_mid = state_ref[HALO : HALO + ROWS, 8:16, 0:COLS]
    global_row = start_ref[0] + lax.broadcasted_iota(jnp.int32, (ROWS, 8, COLS), 0)
    coriolis = 0.3 + 0.5 * global_row.astype(F32) / 512.0
    raw_zonal = raw_ref[:, 0:8, :]
    raw_merid = raw_ref[:, 8:16, :]
    zonal_new = (
        zonal_mid + TIME_STEP * (-grad_x + coriolis * merid_mid - DRAG * zonal_mid + raw_zonal)
    ) * wet
    merid_new = (
        merid_mid + TIME_STEP * (-grad_y - coriolis * zonal_mid - DRAG * merid_mid + raw_merid)
    ) * wet
    new_ref[:, 0:8, :] = zonal_new
    new_ref[:, 8:16, :] = merid_new
    new_ref[:, 16:24, :] = h_new[1:-1, :, 0:COLS]
    if last:
        raw_out_ref[...] = raw_ref[...]
    else:
        flat = new_ref[...].reshape(ROWS * 24, COLS).astype(BF16)
        send_left_ref[...] = flat[:, 0:128]
        send_right_ref[...] = flat[:, COLS - 128 :]

    def lanes_of(field):
        by_column = jnp.sum(field, axis=0)
        return by_column[:, 0:128] + by_column[:, 128:256]

    columns = jnp.concatenate(
        [
            lanes_of(raw_zonal * wet),
            lanes_of(raw_merid * wet),
            lanes_of(wet),
            jnp.zeros((104, 128), F32),
        ],
        axis=0,
    )
    row = jnp.sum(jnp.transpose(columns), axis=0, keepdims=True)
    pay_ref[...] = jnp.broadcast_to(row, (128, 128))


def ocean_network_step(first, last, args):
    n_vmem = len(args) - 1
    outs = [
        jax.ShapeDtypeStruct((ROWS, 24, COLS), F32),
        jax.ShapeDtypeStruct((128, 128), F32),
    ]
    if last:
        outs.append(jax.ShapeDtypeStruct((ROWS, 16, COLS), F32))
    else:
        outs += [jax.ShapeDtypeStruct((ROWS * 24, 128), BF16)] * 2
    vmem = pl.BlockSpec(memory_space=pltpu.VMEM)
    return pl.pallas_call(
        functools.partial(step_kernel, first=first, last=last),
        out_shape=outs,
        in_specs=[pl.BlockSpec(memory_space=pltpu.SMEM)] + [vmem] * n_vmem,
        out_specs=[vmem] * len(outs),
        scratch_shapes=[
            pltpu.VMEM((EXT_ROWS, 32, WIDE), F32),
            pltpu.VMEM((8, SPAN, 5 * 128), BF16),
            pltpu.VMEM((7, SPAN, 5 * 512), BF16),
            pltpu.VMEM((6, SPAN, 5 * 256), BF16),
            pltpu.VMEM((5, SPAN, 5 * 128), BF16),
            pltpu.VMEM((SPAN + 8, 512), F32),
            pltpu.VMEM((ROWS, 16, COLS), F32),
        ],
        name="last_step" if last else ("first_step" if first else "middle_step"),
    )(*args)


def finish_kernel(recv_ref, state_ref, raw_ref, wet_ref, final_ref, forcing_ref):
    zonal_mean, merid_mean = device_means(recv_ref[...])
    wet = wet_ref[HALO : HALO + ROWS, :, 0:COLS]
    zonal_mean = jnp.concatenate([zonal_mean] * 2, axis=1)[None]
    merid_mean = jnp.concatenate([merid_mean] * 2, axis=1)[None]
    forcing_ref[:, 0:8, :] = (raw_ref[:, 0:8, :] - zonal_mean) * wet
    forcing_ref[:, 8:16, :] = (raw_ref[:, 8:16, :] - merid_mean) * wet
    final_ref[:, 0:8, :] = state_ref[:, 0:8, :] - TIME_STEP * zonal_mean * wet
    final_ref[:, 8:16, :] = state_ref[:, 8:16, :] - TIME_STEP * merid_mean * wet
    final_ref[:, 16:24, :] = state_ref[:, 16:24, :]


def finish(received, state, raw, wet):
    return pl.pallas_call(
        finish_kernel,
        out_shape=[
            jax.ShapeDtypeStruct((ROWS, 24, COLS), F32),
            jax.ShapeDtypeStruct((ROWS, 16, COLS), F32),
        ],
        name="finish",
    )(received, state, raw, wet)


def exchange(send_left, send_right):
    def both_ways(axis, up, down):
        count = lax.axis_size(axis)
        forward = [(i, i + 1) for i in range(count - 1)]
        backward = [(target, source) for source, target in forward]
        return lax.ppermute(up, axis, forward), lax.ppermute(down, axis, backward)

    left, right = both_ways("sec", send_right, send_left)
    height = send_left.shape[0] // 2
    lane = lax.broadcasted_iota(jnp.int32, left.shape, 1)
    sides = jnp.where(lane < 64, right, left)
    whole = jnp.concatenate([send_left, send_right, sides], axis=1)
    top, bottom = both_ways("lat", whole[height:], whole[:height])
    return left, right, top, bottom


def local(
    ocean_state,
    land_mask,
    layer_count,
    conv1_weight,
    conv1_bias,
    conv2_weight,
    conv2_bias,
    conv3_weight,
    conv3_bias,
    conv4_weight,
):
    levels = land_mask * layer_count
    level_of = lax.broadcasted_iota(jnp.int32, (ROWS, LEVELS, COLS), 1)
    wet_own = (level_of < levels[:, None, :]).astype(F32)
    state = ocean_state.transpose(1, 0, 2) * jnp.concatenate([wet_own] * 3, axis=1)
    packed = jnp.concatenate(
        [state.astype(BF16), levels.astype(BF16)[:, None, :], jnp.zeros((ROWS, 7, COLS), BF16)],
        axis=1,
    ).reshape(ROWS * 32, COLS)
    parts = exchange(packed[:, :128], packed[:, 128:])
    left, right, top, bottom = [part.reshape(-1, 32, part.shape[1]) for part in parts]
    lane = lax.broadcasted_iota(jnp.int32, (1, 128), 1)
    middle = jnp.concatenate(
        [levels.astype(BF16), jnp.where(lane < 64, right[:, 24], left[:, 24])], axis=1
    )
    levels_ext = jnp.concatenate([top[:, 24], middle, bottom[:, 24]], axis=0).astype(F32)
    level_ext_of = lax.broadcasted_iota(jnp.int32, (EXT_ROWS, LEVELS, WIDE), 1).astype(F32)
    wet = (level_ext_of < levels_ext[:, None, :]).astype(F32)
    sea_turned = jnp.roll((levels_ext > 0).astype(BF16).T, HALO, axis=0)
    sea_turned = jnp.pad(sea_turned, ((0, 0), (0, 128 - EXT_ROWS)))
    sea = jnp.stack([sea_turned[shift : shift + SPAN] for shift in (2, 4, 6)])
    halos = [
        part[:, :24].reshape(-1, part.shape[2]) for part in (left, right, top, bottom)
    ]

    weights = [
        banded(conv1_weight, 32, 512),
        banded(conv2_weight, 128, 256),
        banded(conv3_weight, 64, 128),
        banded(conv4_weight, 32, 128),
        jnp.tile(conv1_bias, 4)[None],
        jnp.tile(conv2_bias, 4)[None],
        jnp.tile(conv3_bias, 4)[None],
    ]
    start = (lax.axis_index("lat") * ROWS).astype(jnp.int32)[None]
    received = []
    for step_index in range(STEPS):
        last = step_index == STEPS - 1
        results = ocean_network_step(
            step_index == 0, last, [start, *received, state, *halos, wet, sea, *weights]
        )
        state = results[0]
        if not last:
            halos = exchange(results[2], results[3])
        received = [lax.all_to_all(results[1], ("sec", "lat"), 0, 0)]
    final_state, forcing = finish(received[0], state, results[2], wet)
    return final_state.transpose(1, 0, 2), forcing.transpose(1, 0, 2)


def solution(mesh):
    return jax.shard_map(
        local,
        mesh=mesh,
        in_specs=(
            P(None, "lat", "sec"),
            P("lat", "sec"),
            P("lat", "sec"),
            P(),
            P(),
            P(),
            P(),
            P(),
            P(),
            P(),
        ),
        out_specs=(P(None, "lat", "sec"), P(None, "lat", "sec")),
        check_vma=False,
    )
```

time: 698 us -> 279 us (0.40); the launches traced: 689 us -> 277 us
  blocking collectives: 302 us -> 77.3 us
  matrix products: 123 us -> 0 us
  local copies, waits for them, and re-layouts: 136 us -> 31.2 us
  Pallas kernels: 0 us -> 88.7 us
  starting transfers between devices: 87.5 us -> 38.1 us
  other arithmetic: 9.43 us -> 21.9 us
  waiting for transfers between devices: 28.1 us -> 18.9 us
    psum x4 -> x0, blocking collectives: 302 us -> none  [local(): lax.psum(jnp.sum(raw_forcing * wet_two, axis=(1, 2)), ('sec', 'lat'))]
    dot_general x84 -> x0, matrix products: 123 us -> none  [the longest x80 121 us: conv_layer(): jnp.einsum('oc,crx->orx', weight[shift_y], stacked, preferred_element_typ...]
    unnamed x140 -> x51, local copies, waits for them, and re-layouts: 104 us -> 8.84 us
    pallas_call x0 -> x5, Pallas kernels: none -> 88.7 us  [the longest x4 86.5 us: ocean_network_step(): pl.pallas_call(functools.partial(step_kernel, first=first, last=last), ou...]
    all_to_all x0 -> x4, blocking collectives: none -> 77.3 us  [local(): received = [lax.all_to_all(results[1], ('sec', 'lat'), 0, 0)]]
    ppermute x36 -> x16, starting transfers between devices: 87.5 us -> 38.1 us  [both_ways(): return (lax.ppermute(up, axis, forward), lax.ppermute(down, axis, backward))]
    concatenate x16 -> x2, local copies, waits for them, and re-layouts: 30 us -> 0.21 us  [the longest x1 0.13 us: local(): sea_turned = jnp.roll((levels_ext > 0).astype(BF16).T, HALO, axis=0)]
    concatenate x15 -> x14, other arithmetic: 1.79 us -> 16.5 us  [the longest x4 8.63 us: banded(): band = jnp.concatenate(bands, axis=3)]
  transfers between devices with their start and end apart: 36 -> 16, of which waited for: 10 -> 5; matrix products, arithmetic and copies ran while one was open for 1% -> 12% of each run, Pallas kernels for 0% -> 0%
where the time goes in v2:
time: 279 us; the launch traced here: 277 us
  Pallas kernels  88.7 us (32%)
  blocking collectives  77.3 us (28%)
  starting transfers between devices  38.1 us (14%)
  local copies, waits for them, and re-layouts  31.2 us (11%)
  other arithmetic  21.9 us (8%)
  waiting for transfers between devices  18.9 us (7%)
    pallas_call x4, Pallas kernels, ocean_network_step(): pl.pallas_call(functools.partial(step_kernel, first=first, last=last), ou...  86.5 us
    all_to_all x4, blocking collectives, local(): received = [lax.all_to_all(results[1], ('sec', 'lat'), 0, 0)]  77.3 us
    ppermute x16, starting transfers between devices, both_ways(): return (lax.ppermute(up, axis, forward), lax.ppermute(down, axis, backward))  38.1 us
    ppermute x16, waiting for transfers between devices, both_ways(): return (lax.ppermute(up, axis, forward), lax.ppermute(down, axis, backward))  18.9 us
    slice x6, local copies, waits for them, and re-layouts, banded(): band[:, 4 * i:4 * i + 4].reshape(5 * 4 * in_pad, 4 * out_width)  9.11 us
    unnamed x51, local copies, waits for them, and re-layouts  8.84 us
    concatenate x4, other arithmetic, banded(): band = jnp.concatenate(bands, axis=3)  8.63 us
  transfers between devices with their start and end apart: 16, of which 5 were waited for; matrix products, arithmetic and copies ran while one was open for 12% of the time, Pallas kernels for 0%

profile of v2, /device:TPU:1, one launch (start us, length us, event | category | flops | bytes accessed | tf_op | source)
XLA Modules:
  0.0 277.3 jit_solution(8185703683022439887)
XLA Ops:
  4.4 4.9 %collective-permute-start = (bf16[512,128]{1,0:T(8,128)(2,1)}, bf16[512,128]{1,0:T(8,128)(2,1)}, u32[]{:S(2)}, u32[]{:S(2)}) collective-permute-start(bf16[512,128]{1,0:T(8,128)(2,1)} %get-tuple-element.67), channel_id=1, source_target_pairs={{0,32},{32,64},{64,96},{1,33},{33,65},{65,97},{2,34},{34,66},{66,9... | collective-permute-start | bytes 393224 | tf_op jit(solution)/shard_map/ppermute | solution.py:241
  12.8 5.9 %fusion.7 = bf16[5,8,128,256]{2,0,3,1:T(8,128)(2,1)S(1)} fusion(bf16[5,5,128,64]{2,0,3,1:T(8,128)(2,1)S(1)} %bitcast.69), kind=kLoop, calls=%fused_computation.13 | loop fusion | flops 26214400 | bytes 3031040 | tf_op jit(solution)/shard_map/concatenate | solution.py:30
  20.7 2.9 %copy.87 = bf16[5,4,128,256]{3,2,1,0:T(8,128)(2,1)S(1)} copy(bf16[5,4,128,256]{2,0,3,1:T(8,128)(2,1)} %get-tuple-element.50) | data formatting | bytes 2621440 | tf_op jit(solution)/shard_map/slice | solution.py:32
  23.6 2.4 copy.88
  30.9 2.3 fusion.25
  48.0 3.2 %collective-permute-start.2 = (bf16[256,384]{1,0:T(8,128)(2,1)S(1)}, bf16[256,384]{1,0:T(8,128)(2,1)S(1)}, u32[]{:S(2)}, u32[]{:S(2)}) collective-permute-start(bf16[256,384]{1,0:T(8,128)(2,1)S(1)} %get-tuple-element.57), channel_id=1, source_target_pairs={{0,1},{1,2},{2,3},{3,4},{4,5},{5,6},{6,7},{7,8},{8,9},{9,10},{10,1... | collective-permute-start | bytes 589832 | tf_op jit(solution)/shard_map/ppermute | solution.py:241
  52.5 2.2 collective-permute-done.2
  54.7 4.1 %collective-permute-done.3 = bf16[256,384]{1,0:T(8,128)(2,1)S(1)} collective-permute-done((bf16[256,384]{1,0:T(8,128)(2,1)S(1)}, bf16[256,384]{1,0:T(8,128)(2,1)S(1)}, u32[]{:S(2)}, u32[]{:S(2)}) %collective-permute-start.3) | collective-permute-done | bytes 196640 | tf_op jit(solution)/shard_map/ppermute | solution.py:241
  62.7 21.5 %first_step.1 = (f32[16,24,256]{2,1,0:T(8,128)}, f32[128,128]{1,0:T(8,128)}, bf16[384,128]{1,0:T(8,128)(2,1)}, bf16[384,128]{1,0:T(8,128)(2,1)}) custom-call(s32[1]{0:T(128)} %bitcast.refs_0_, f32[16,24,256]{2,1,0:T(8,128)} %get-tuple-element.47.refs_1_, bf16[384,128]{1,0:T(8,128)(2,1)} %bitcast.82, bf16[384,128]{1,0:T(8,128)(2,1)} %bitcast.83, ...), custom_call_target="tpu_custom_call" | custom-call | tf_op jit(solution)/shard_map/first_step/pallas_call | solution.py:195
  84.2 4.2 %collective-permute-start.4 = (bf16[384,128]{1,0:T(8,128)(2,1)}, bf16[384,128]{1,0:T(8,128)(2,1)S(1)}, u32[]{:S(2)}, u32[]{:S(2)}) collective-permute-start(bf16[384,128]{1,0:T(8,128)(2,1)} %get-tuple-element.21), channel_id=1, source_target_pairs={{0,32},{32,64},{64,96},{1,33},{33,65},{65,97},{2,34},{34,66},{66,9... | collective-permute-start | bytes 294920 | tf_op jit(solution)/shard_map/ppermute | solution.py:241
  90.3 4.2 %collective-permute-done.5.refs_4_ = bf16[384,128]{1,0:T(8,128)(2,1)S(1)} collective-permute-done((bf16[384,128]{1,0:T(8,128)(2,1)}, bf16[384,128]{1,0:T(8,128)(2,1)S(1)}, u32[]{:S(2)}, u32[]{:S(2)}) %collective-permute-start.5) | collective-permute-done | bytes 98336 | tf_op jit(solution)/shard_map/ppermute | solution.py:241
  95.6 3.2 %collective-permute-start.6 = (bf16[192,384]{1,0:T(8,128)(2,1)S(1)}, bf16[192,384]{1,0:T(8,128)(2,1)S(1)}, u32[]{:S(2)}, u32[]{:S(2)}) collective-permute-start(bf16[192,384]{1,0:T(8,128)(2,1)S(1)} %get-tuple-element.65), channel_id=1, source_target_pairs={{0,1},{1,2},{2,3},{3,4},{4,5},{5,6},{6,7},{7,8},{8,9},{9,10},{10,1... | collective-permute-start | bytes 442376 | tf_op jit(solution)/shard_map/ppermute | solution.py:241
  100.1 24.1 %all_to_all.44 = f32[128,1,128]{2,1,0:T(1,128)} all-to-all(f32[128,1,128]{2,1,0:T(1,128)} %bitcast.98), channel_id=1, replica_groups=mesh['sec'=4,'lat'=32] {'sec','lat'}, dimensions={0} | all-to-all | bytes 131072 | tf_op jit(solution)/shard_map/all_to_all | solution.py:307
  124.9 21.6 %middle_step.2 = (f32[16,24,256]{2,1,0:T(8,128)}, f32[128,128]{1,0:T(8,128)}, bf16[384,128]{1,0:T(8,128)(2,1)}, bf16[384,128]{1,0:T(8,128)(2,1)}) custom-call(s32[1]{0:T(128)} %bitcast.refs_0_, f32[128,128]{1,0:T(8,128)} %bitcast.85, f32[16,24,256]{2,1,0:T(8,128)} %get-tuple-element.20.refs_2_, bf16[384,128]{1,0:T(8,128)(2,1)} %copy-done.8, ...), custom_call_target="tpu_custom_call" | custom-call | tf_op jit(solution)/shard_map/middle_step/pallas_call | solution.py:195
  146.5 3.2 %collective-permute-start.8 = (bf16[384,128]{1,0:T(8,128)(2,1)}, bf16[384,128]{1,0:T(8,128)(2,1)S(1)}, u32[]{:S(2)}, u32[]{:S(2)}) collective-permute-start(bf16[384,128]{1,0:T(8,128)(2,1)} %get-tuple-element.25), channel_id=1, source_target_pairs={{0,32},{32,64},{64,96},{1,33},{33,65},{65,97},{2,34},{34,66},{66,9... | collective-permute-start | bytes 294920 | tf_op jit(solution)/shard_map/ppermute | solution.py:241
  151.6 4.2 %collective-permute-done.9.refs_4_ = bf16[384,128]{1,0:T(8,128)(2,1)S(1)} collective-permute-done((bf16[384,128]{1,0:T(8,128)(2,1)}, bf16[384,128]{1,0:T(8,128)(2,1)S(1)}, u32[]{:S(2)}, u32[]{:S(2)}) %collective-permute-start.9) | collective-permute-done | bytes 98336 | tf_op jit(solution)/shard_map/ppermute | solution.py:241
  159.9 18.9 %all_to_all.45 = f32[128,1,128]{2,1,0:T(1,128)} all-to-all(f32[128,1,128]{2,1,0:T(1,128)} %bitcast.97), channel_id=1, replica_groups=mesh['sec'=4,'lat'=32] {'sec','lat'}, dimensions={0} | all-to-all | bytes 131072 | tf_op jit(solution)/shard_map/all_to_all | solution.py:307
  179.5 21.7 %middle_step.3 = (f32[16,24,256]{2,1,0:T(8,128)}, f32[128,128]{1,0:T(8,128)}, bf16[384,128]{1,0:T(8,128)(2,1)}, bf16[384,128]{1,0:T(8,128)(2,1)}) custom-call(s32[1]{0:T(128)} %bitcast.refs_0_, f32[128,128]{1,0:T(8,128)} %bitcast.86, f32[16,24,256]{2,1,0:T(8,128)} %get-tuple-element.24.refs_2_, bf16[384,128]{1,0:T(8,128)(2,1)} %copy-done.9, ...), custom_call_target="tpu_custom_call" | custom-call | tf_op jit(solution)/shard_map/middle_step/pallas_call | solution.py:195
  201.2 3.1 %collective-permute-start.12 = (bf16[384,128]{1,0:T(8,128)(2,1)}, bf16[384,128]{1,0:T(8,128)(2,1)S(1)}, u32[]{:S(2)}, u32[]{:S(2)}) collective-permute-start(bf16[384,128]{1,0:T(8,128)(2,1)} %get-tuple-element.29), channel_id=1, source_target_pairs={{0,32},{32,64},{64,96},{1,33},{33,65},{65,97},{2,34},{34,66},{66,9... | collective-permute-start | bytes 294920 | tf_op jit(solution)/shard_map/ppermute | solution.py:241
  206.3 4.2 %collective-permute-done.13.refs_4_ = bf16[384,128]{1,0:T(8,128)(2,1)S(1)} collective-permute-done((bf16[384,128]{1,0:T(8,128)(2,1)}, bf16[384,128]{1,0:T(8,128)(2,1)S(1)}, u32[]{:S(2)}, u32[]{:S(2)}) %collective-permute-start.13) | collective-permute-done | bytes 98336 | tf_op jit(solution)/shard_map/ppermute | solution.py:241
  214.7 19.0 %all_to_all.46 = f32[128,1,128]{2,1,0:T(1,128)} all-to-all(f32[128,1,128]{2,1,0:T(1,128)} %bitcast.96), channel_id=1, replica_groups=mesh['sec'=4,'lat'=32] {'sec','lat'}, dimensions={0} | all-to-all | bytes 131072 | tf_op jit(solution)/shard_map/all_to_all | solution.py:307
  234.4 21.7 %last_step.1 = (f32[16,24,256]{2,1,0:T(8,128)}, f32[128,128]{1,0:T(8,128)}, f32[16,16,256]{2,1,0:T(8,128)}) custom-call(s32[1]{0:T(128)} %bitcast.refs_0_, f32[128,128]{1,0:T(8,128)} %bitcast.84, f32[16,24,256]{2,1,0:T(8,128)} %get-tuple-element.28.refs_2_, bf16[384,128]{1,0:T(8,128)(2,1)} %copy-done.6, bf16[384,128]{1,0:T(8,128)(2,1)} %copy-done.7, ...), custom_call_target="tpu_custom_call" | custom-call | tf_op jit(solution)/shard_map/last_step/pallas_call | solution.py:195
  256.1 15.3 %all_to_all.47 = f32[128,1,128]{2,1,0:T(1,128)} all-to-all(f32[128,1,128]{2,1,0:T(1,128)} %bitcast.99), channel_id=1, replica_groups=mesh['sec'=4,'lat'=32] {'sec','lat'}, dimensions={0} | all-to-all | bytes 131072 | tf_op jit(solution)/shard_map/all_to_all | solution.py:307
  271.4 2.2 finish.1
  (130 shorter events, 56.1 us)
Async XLA Ops:
  4.4 37.9 %collective-permute-start = (bf16[512,128]{1,0:T(8,128)(2,1)}, bf16[512,128]{1,0:T(8,128)(2,1)}, u32[]{:S(2)}, u32[]{:S(2)}) collective-permute-start(bf16[512,128]{1,0:T(8,128)(2,1)} %get-tuple-element.67), channel_id=1, source_target_pairs={{0,32},{32,64},{64,96},{1,33},{33,65},{65,97},{2,34},{34,66},{66,9... | collective-permute-start | bytes 393224 | tf_op jit(solution)/shard_map/ppermute | solution.py:241
  9.4 35.3 %collective-permute-start.1 = (bf16[512,128]{1,0:T(8,128)(2,1)}, bf16[512,128]{1,0:T(8,128)(2,1)}, u32[]{:S(2)}, u32[]{:S(2)}) collective-permute-start(bf16[512,128]{1,0:T(8,128)(2,1)} %get-tuple-element.66), channel_id=1, source_target_pairs={{32,0},{64,32},{96,64},{33,1},{65,33},{97,65},{34,2},{66,34},{98,6... | collective-permute-start | bytes 393224 | tf_op jit(solution)/shard_map/ppermute | solution.py:241
  38.0 9.9 %copy-start.3 = (bf16[16,32,256]{2,1,0:T(8,128)(2,1)S(1)}, bf16[16,32,256]{2,1,0:T(8,128)(2,1)}, u32[]{:S(2)}) copy-start(bf16[16,32,256]{2,1,0:T(8,128)(2,1)} %copy-done.2) | copy-start | bytes 786436
  39.2 22.9 %copy-start.22 = (f32[128]{0:T(128)S(1)}, f32[128]{0:T(128)}, u32[]{:S(2)}) copy-start(f32[128]{0:T(128)} %param.14) | copy-start | bytes 1540
  48.0 6.7 %collective-permute-start.2 = (bf16[256,384]{1,0:T(8,128)(2,1)S(1)}, bf16[256,384]{1,0:T(8,128)(2,1)S(1)}, u32[]{:S(2)}, u32[]{:S(2)}) collective-permute-start(bf16[256,384]{1,0:T(8,128)(2,1)S(1)} %get-tuple-element.57), channel_id=1, source_target_pairs={{0,1},{1,2},{2,3},{3,4},{4,5},{5,6},{6,7},{7,8},{8,9},{9,10},{10,1... | collective-permute-start | bytes 589832 | tf_op jit(solution)/shard_map/ppermute | solution.py:241
  51.2 7.6 %collective-permute-start.3 = (bf16[256,384]{1,0:T(8,128)(2,1)S(1)}, bf16[256,384]{1,0:T(8,128)(2,1)S(1)}, u32[]{:S(2)}, u32[]{:S(2)}) collective-permute-start(bf16[256,384]{1,0:T(8,128)(2,1)S(1)} %get-tuple-element.56), channel_id=1, source_target_pairs={{1,0},{2,1},{3,2},{4,3},{5,4},{6,5},{7,6},{8,7},{9,8},{10,9},{11,1... | collective-permute-start | bytes 589832 | tf_op jit(solution)/shard_map/ppermute | solution.py:241
  84.2 6.1 %collective-permute-start.4 = (bf16[384,128]{1,0:T(8,128)(2,1)}, bf16[384,128]{1,0:T(8,128)(2,1)S(1)}, u32[]{:S(2)}, u32[]{:S(2)}) collective-permute-start(bf16[384,128]{1,0:T(8,128)(2,1)} %get-tuple-element.21), channel_id=1, source_target_pairs={{0,32},{32,64},{64,96},{1,33},{33,65},{65,97},{2,34},{34,66},{66,9... | collective-permute-start | bytes 294920 | tf_op jit(solution)/shard_map/ppermute | solution.py:241
  88.4 6.1 %collective-permute-start.5 = (bf16[384,128]{1,0:T(8,128)(2,1)}, bf16[384,128]{1,0:T(8,128)(2,1)S(1)}, u32[]{:S(2)}, u32[]{:S(2)}) collective-permute-start(bf16[384,128]{1,0:T(8,128)(2,1)} %get-tuple-element.22), channel_id=1, source_target_pairs={{32,0},{64,32},{96,64},{33,1},{65,33},{97,65},{34,2},{66,34},{98,6... | collective-permute-start | bytes 294920 | tf_op jit(solution)/shard_map/ppermute | solution.py:241
  90.3 33.9 %copy-start.8 = (bf16[384,128]{1,0:T(8,128)(2,1)}, bf16[384,128]{1,0:T(8,128)(2,1)S(1)}, u32[]{:S(2)}) copy-start(bf16[384,128]{1,0:T(8,128)(2,1)S(1)} %collective-permute-done.4.refs_3_) | copy-start | bytes 294916
  94.5 29.7 %copy-start.10 = (bf16[384,128]{1,0:T(8,128)(2,1)}, bf16[384,128]{1,0:T(8,128)(2,1)S(1)}, u32[]{:S(2)}) copy-start(bf16[384,128]{1,0:T(8,128)(2,1)S(1)} %collective-permute-done.5.refs_4_) | copy-start | bytes 294916
  95.6 28.6 %collective-permute-start.6 = (bf16[192,384]{1,0:T(8,128)(2,1)S(1)}, bf16[192,384]{1,0:T(8,128)(2,1)S(1)}, u32[]{:S(2)}, u32[]{:S(2)}) collective-permute-start(bf16[192,384]{1,0:T(8,128)(2,1)S(1)} %get-tuple-element.65), channel_id=1, source_target_pairs={{0,1},{1,2},{2,3},{3,4},{4,5},{5,6},{6,7},{7,8},{8,9},{9,10},{10,1... | collective-permute-start | bytes 442376 | tf_op jit(solution)/shard_map/ppermute | solution.py:241
  98.8 25.4 %collective-permute-start.7 = (bf16[192,384]{1,0:T(8,128)(2,1)S(1)}, bf16[192,384]{1,0:T(8,128)(2,1)S(1)}, u32[]{:S(2)}, u32[]{:S(2)}) collective-permute-start(bf16[192,384]{1,0:T(8,128)(2,1)S(1)} %get-tuple-element.64), channel_id=1, source_target_pairs={{1,0},{2,1},{3,2},{4,3},{5,4},{6,5},{7,6},{8,7},{9,8},{10,9},{11,1... | collective-permute-start | bytes 442376 | tf_op jit(solution)/shard_map/ppermute | solution.py:241
  146.5 5.1 %collective-permute-start.8 = (bf16[384,128]{1,0:T(8,128)(2,1)}, bf16[384,128]{1,0:T(8,128)(2,1)S(1)}, u32[]{:S(2)}, u32[]{:S(2)}) collective-permute-start(bf16[384,128]{1,0:T(8,128)(2,1)} %get-tuple-element.25), channel_id=1, source_target_pairs={{0,32},{32,64},{64,96},{1,33},{33,65},{65,97},{2,34},{34,66},{66,9... | collective-permute-start | bytes 294920 | tf_op jit(solution)/shard_map/ppermute | solution.py:241
  149.7 6.1 %collective-permute-start.9 = (bf16[384,128]{1,0:T(8,128)(2,1)}, bf16[384,128]{1,0:T(8,128)(2,1)S(1)}, u32[]{:S(2)}, u32[]{:S(2)}) collective-permute-start(bf16[384,128]{1,0:T(8,128)(2,1)} %get-tuple-element.26), channel_id=1, source_target_pairs={{32,0},{64,32},{96,64},{33,1},{65,33},{97,65},{34,2},{66,34},{98,6... | collective-permute-start | bytes 294920 | tf_op jit(solution)/shard_map/ppermute | solution.py:241
  151.6 27.2 %copy-start.9 = (bf16[384,128]{1,0:T(8,128)(2,1)}, bf16[384,128]{1,0:T(8,128)(2,1)S(1)}, u32[]{:S(2)}) copy-start(bf16[384,128]{1,0:T(8,128)(2,1)S(1)} %collective-permute-done.8.refs_3_) | copy-start | bytes 294916
  155.8 23.0 %copy-start.11 = (bf16[384,128]{1,0:T(8,128)(2,1)}, bf16[384,128]{1,0:T(8,128)(2,1)S(1)}, u32[]{:S(2)}) copy-start(bf16[384,128]{1,0:T(8,128)(2,1)S(1)} %collective-permute-done.9.refs_4_) | copy-start | bytes 294916
  156.9 21.9 %collective-permute-start.10 = (bf16[192,384]{1,0:T(8,128)(2,1)S(1)}, bf16[192,384]{1,0:T(8,128)(2,1)S(1)}, u32[]{:S(2)}, u32[]{:S(2)}) collective-permute-start(bf16[192,384]{1,0:T(8,128)(2,1)S(1)} %get-tuple-element.63), channel_id=1, source_target_pairs={{0,1},{1,2},{2,3},{3,4},{4,5},{5,6},{6,7},{7,8},{8,9},{9,10},{10,1... | collective-permute-start | bytes 442376 | tf_op jit(solution)/shard_map/ppermute | solution.py:241
  158.6 20.2 %collective-permute-start.11 = (bf16[192,384]{1,0:T(8,128)(2,1)S(1)}, bf16[192,384]{1,0:T(8,128)(2,1)S(1)}, u32[]{:S(2)}, u32[]{:S(2)}) collective-permute-start(bf16[192,384]{1,0:T(8,128)(2,1)S(1)} %get-tuple-element.62), channel_id=1, source_target_pairs={{1,0},{2,1},{3,2},{4,3},{5,4},{6,5},{7,6},{8,7},{9,8},{10,9},{11,1... | collective-permute-start | bytes 442376 | tf_op jit(solution)/shard_map/ppermute | solution.py:241
  201.2 5.0 %collective-permute-start.12 = (bf16[384,128]{1,0:T(8,128)(2,1)}, bf16[384,128]{1,0:T(8,128)(2,1)S(1)}, u32[]{:S(2)}, u32[]{:S(2)}) collective-permute-start(bf16[384,128]{1,0:T(8,128)(2,1)} %get-tuple-element.29), channel_id=1, source_target_pairs={{0,32},{32,64},{64,96},{1,33},{33,65},{65,97},{2,34},{34,66},{66,9... | collective-permute-start | bytes 294920 | tf_op jit(solution)/shard_map/ppermute | solution.py:241
  204.3 6.1 %collective-permute-start.13 = (bf16[384,128]{1,0:T(8,128)(2,1)}, bf16[384,128]{1,0:T(8,128)(2,1)S(1)}, u32[]{:S(2)}, u32[]{:S(2)}) collective-permute-start(bf16[384,128]{1,0:T(8,128)(2,1)} %get-tuple-element.30), channel_id=1, source_target_pairs={{32,0},{64,32},{96,64},{33,1},{65,33},{97,65},{34,2},{66,34},{98,6... | collective-permute-start | bytes 294920 | tf_op jit(solution)/shard_map/ppermute | solution.py:241
  206.2 27.4 %copy-start.6 = (bf16[384,128]{1,0:T(8,128)(2,1)}, bf16[384,128]{1,0:T(8,128)(2,1)S(1)}, u32[]{:S(2)}) copy-start(bf16[384,128]{1,0:T(8,128)(2,1)S(1)} %collective-permute-done.12.refs_3_) | copy-start | bytes 294916
  210.5 23.2 %copy-start.7 = (bf16[384,128]{1,0:T(8,128)(2,1)}, bf16[384,128]{1,0:T(8,128)(2,1)S(1)}, u32[]{:S(2)}) copy-start(bf16[384,128]{1,0:T(8,128)(2,1)S(1)} %collective-permute-done.13.refs_4_) | copy-start | bytes 294916
  211.5 22.1 %collective-permute-start.14 = (bf16[192,384]{1,0:T(8,128)(2,1)S(1)}, bf16[192,384]{1,0:T(8,128)(2,1)S(1)}, u32[]{:S(2)}, u32[]{:S(2)}) collective-permute-start(bf16[192,384]{1,0:T(8,128)(2,1)S(1)} %get-tuple-element.61), channel_id=1, source_target_pairs={{0,1},{1,2},{2,3},{3,4},{4,5},{5,6},{6,7},{7,8},{8,9},{9,10},{10,1... | collective-permute-start | bytes 442376 | tf_op jit(solution)/shard_map/ppermute | solution.py:241
  213.4 20.3 %collective-permute-start.15 = (bf16[192,384]{1,0:T(8,128)(2,1)S(1)}, bf16[192,384]{1,0:T(8,128)(2,1)S(1)}, u32[]{:S(2)}, u32[]{:S(2)}) collective-permute-start(bf16[192,384]{1,0:T(8,128)(2,1)S(1)} %get-tuple-element.60), channel_id=1, source_target_pairs={{1,0},{2,1},{3,2},{4,3},{5,4},{6,5},{7,6},{8,7},{9,8},{10,9},{11,1... | collective-permute-start | bytes 442376 | tf_op jit(solution)/shard_map/ppermute | solution.py:241
  (15 other events, 37.9 us)

commit v3 on v2

v3 whole, which is shorter than its diff:
```python
import functools

import jax
import jax.numpy as jnp
from jax import lax
from jax.experimental import pallas as pl
from jax.experimental.pallas import tpu as pltpu
from jax.sharding import PartitionSpec as P

LEVELS = 8
STEPS = 4
HALO = 8
TIME_STEP = 0.3
DRAG = 0.05
ROWS = 16
COLS = 256
EXT_ROWS = ROWS + 2 * HALO
WIDE = COLS + 128
SIDE = 64
MARGINS = tuple(HALO * (STEPS - step) for step in range(STEPS))
LAND_OFFSET = -(2.0**24)
F32 = jnp.float32
BF16 = jnp.bfloat16


def banded_kernel(*refs):
    weight_refs, bias_refs, band_refs, row_refs = refs[:4], refs[4:7], refs[7:11], refs[11:14]
    flat_ref, turned_ref = refs[14:]
    for layer in range(4):
        weight_ref, band_ref = weight_refs[layer], band_refs[layer]
        out_width = weight_ref.shape[1]
        in_width = weight_ref.shape[2] // 5
        in_pad = band_ref.shape[0] // 40
        wide = -(-5 * in_width // 128) * 128
        flat_ref[...] = jnp.zeros(flat_ref.shape, F32)
        for offset in range(5):
            flat_ref[0:out_width, 0 : 5 * in_width] = weight_ref[offset].astype(F32)
            turned_ref[offset, 0:wide, :] = jnp.transpose(flat_ref[:, 0:wide])
        extra = in_pad - in_width
        for half in range(2):
            for shift in range(5):
                for row in range(4):
                    parts = []
                    for out_row in range(4):
                        offset = 4 * half + row - out_row
                        if not 0 <= offset < 5:
                            parts.append(jnp.zeros((in_pad, out_width), F32))
                            continue
                        part = turned_ref[
                            offset, shift * in_width : (shift + 1) * in_width, 0:out_width
                        ]
                        if extra:
                            pad = jnp.zeros((extra, out_width), F32)
                            if layer == 0 and offset == 2 and shift == 2:
                                first = lax.broadcasted_iota(jnp.int32, pad.shape, 0) == 0
                                pad = jnp.where(first, LAND_OFFSET, 0.0)
                            part = jnp.concatenate([part, pad], axis=0)
                        parts.append(part)
                    if 4 * out_width < band_ref.shape[1]:
                        parts.append(jnp.zeros((in_pad, band_ref.shape[1] - 4 * out_width), F32))
                    base = ((half * 5 + shift) * 4 + row) * in_pad
                    band_ref[base : base + in_pad, :] = jnp.concatenate(parts, axis=1).astype(BF16)
    for bias_ref, row_ref in zip(bias_refs, row_refs):
        row_ref[...] = jnp.concatenate([bias_ref[...]] * 4, axis=1)


def banded(weights, biases):
    shapes = [(1280, 512), (5120, 256), (2560, 128), (1280, 128)]
    outs = [jax.ShapeDtypeStruct(shape, BF16) for shape in shapes]
    outs += [jax.ShapeDtypeStruct((1, width), F32) for width in (512, 256, 128)]
    return pl.pallas_call(
        banded_kernel,
        out_shape=outs,
        scratch_shapes=[pltpu.VMEM((128, 640), F32), pltpu.VMEM((5, 640, 128), F32)],
        name="banded",
    )(*weights, *[bias[None] for bias in biases])


def prepare_kernel(state_ref, land_ref, count_ref, own_ref, left_ref, right_ref):
    levels = land_ref[...] * count_ref[...]
    own_ref[:, 24:32, :] = jnp.zeros((ROWS, 8, COLS), F32)
    own_ref[:, 24, :] = levels.astype(F32)
    for channel in range(24):
        wet = jnp.where(levels > channel % LEVELS, 1.0, 0.0)
        own_ref[:, channel, :] = state_ref[channel] * wet
    flat = own_ref[...].reshape(ROWS * 32, COLS).astype(BF16)
    left_ref[...] = flat[:, 0:128]
    right_ref[...] = flat[:, COLS - 128 :]


def prepare(ocean_state, land_mask, layer_count):
    return pl.pallas_call(
        prepare_kernel,
        out_shape=[jax.ShapeDtypeStruct((ROWS, 32, COLS), F32)]
        + [jax.ShapeDtypeStruct((ROWS * 32, 128), BF16)] * 2,
        name="prepare",
    )(ocean_state, land_mask, layer_count)


def conv_rows(in_ref, weight_ref, group, count):
    lhs = jnp.concatenate([in_ref[group, 0:count, :], in_ref[group + 1, 0:count, :]], axis=1)
    return jnp.dot(lhs, weight_ref[...], preferred_element_type=F32)


def spread(value, work_ref, out_ref, group, width):
    span = value.shape[0]
    work_ref[0:span, 0:width] = value
    for shift in range(5):
        out_ref[group, :, shift * width : (shift + 1) * width] = work_ref[
            shift : shift + span, 0:width
        ].astype(BF16)


def conv_layer(in_ref, weight_ref, bias_ref, sea_ref, work_ref, out_ref, layer, groups):
    width = weight_ref.shape[1]

    def body(group, carry):
        half = 0.5 * (conv_rows(in_ref, weight_ref, group, in_ref.shape[1]) + bias_ref[...])
        value = half + half * jnp.tanh(half)
        if layer:
            row_of = lax.broadcasted_iota(jnp.int32, (128, width), 0)
            lane_of = lax.broadcasted_iota(jnp.int32, (128, width), 1)
            wanted = 4 * group + 2 * (layer + 1) + lane_of // (width // 4)
            pick = jnp.where(row_of == wanted, 1.0, 0.0).astype(BF16)
            value = value * jnp.dot(sea_ref[layer - 1], pick, preferred_element_type=F32)
        spread(value, work_ref, out_ref, group, width)
        return carry

    lax.fori_loop(0, groups, body, 0)


def device_means(received):
    total = jnp.sum(received, axis=0, keepdims=True)
    column = jnp.transpose(jnp.broadcast_to(total, (128, 128)))
    counts = jnp.maximum(column[16:24], 1.0)
    return column[0:8] / counts, column[8:16] / counts


def step_kernel(*refs, step):
    first, last = step == 0, step == STEPS - 1
    margin = MARGINS[step]
    span = COLS + 2 * margin
    refs = list(refs)
    start_ref = refs.pop(0)
    own_ref, top_ref, bottom_ref = refs[:3]
    refs = refs[3:]
    if first:
        left_ref, right_ref = refs[:2]
        refs = refs[2:]
    else:
        recv_ref, wet_ref, sea_turned_ref = refs[:3]
        refs = refs[3:]
    w1_ref, w2_ref, w3_ref, w4_ref, b1_ref, b2_ref, b3_ref, new_ref, pay_ref = refs[:9]
    refs = refs[9:]
    if first:
        wet_ref, sea_turned_ref = refs[:2]
        refs = refs[2:]
    if last:
        raw_out_ref = refs.pop(0)
    else:
        send_up_ref, send_down_ref = refs[:2]
        refs = refs[2:]
    state_ref, a0_ref, a1_ref, a2_ref, a3_ref, work_ref, raw_ref, sea_ref = refs

    if first:
        lane = lax.broadcasted_iota(jnp.int32, (ROWS * 32, 128), 1)
        sides = jnp.where(lane < SIDE, right_ref[...].astype(F32), left_ref[...].astype(F32))
        state_ref[HALO : HALO + ROWS, :, 0:COLS] = own_ref[...]
        state_ref[HALO : HALO + ROWS, :, COLS:WIDE] = sides.reshape(ROWS, 32, 128)
        state_ref[0:HALO] = top_ref[...].astype(F32).reshape(HALO, 32, WIDE)
        state_ref[HALO + ROWS :] = bottom_ref[...].astype(F32).reshape(HALO, 32, WIDE)
        levels = jnp.broadcast_to(state_ref[:, 24:25, :], (EXT_ROWS, 8, WIDE))
        level_of = lax.broadcasted_iota(jnp.int32, levels.shape, 1).astype(F32)
        wet_ref[...] = jnp.where(level_of < levels, 1.0, 0.0)
        by_row = jnp.where(state_ref[:, 24, :] > 0.0, 1.0, 0.0)
        turned = jnp.transpose(
            jnp.concatenate([by_row, jnp.zeros((128 - EXT_ROWS, WIDE), F32)], axis=0)
        )
        sea_turned_ref[0:SIDE, :] = turned[WIDE - SIDE :]
        sea_turned_ref[SIDE:WIDE, :] = turned[0 : WIDE - SIDE]
        sea_turned_ref[WIDE:, :] = jnp.zeros((8, 128), F32)
    else:
        state_ref[HALO : HALO + ROWS, 0:24, :] = own_ref[...]
        state_ref[0:HALO, 0:24, :] = top_ref[...].astype(F32).reshape(HALO, 24, WIDE)
        state_ref[HALO + ROWS :, 0:24, :] = bottom_ref[...].astype(F32).reshape(HALO, 24, WIDE)
        zonal_mean, merid_mean = device_means(recv_ref[...])
        for base, mean in ((0, zonal_mean), (8, merid_mean)):
            scaled = jnp.concatenate([TIME_STEP * mean] * 3, axis=1)
            state_ref[:, base : base + 8, :] = (
                state_ref[:, base : base + 8, :] - scaled[None] * wet_ref[...]
            )
    first_channel = lax.broadcasted_iota(jnp.int32, (EXT_ROWS, 8, WIDE), 1) == 0
    state_ref[:, 24:32, :] = jnp.where(first_channel, 1.0 - wet_ref[...], 0.0)
    for layer in (1, 2):
        begin = SIDE - margin + 2 * (layer + 1)
        sea_ref[layer - 1] = sea_turned_ref[begin : begin + span, :].astype(BF16)

    work_ref[span:, :] = jnp.zeros((8, 512), F32)
    for group in range(8):
        flat = state_ref[4 * group : 4 * group + 4].reshape(128, WIDE)
        turned = jnp.transpose(flat)
        spread(
            jnp.concatenate([turned[WIDE - margin :], turned[0 : COLS + margin]], axis=0),
            work_ref,
            a0_ref,
            group,
            128,
        )
    conv_layer(a0_ref, w1_ref, b1_ref, sea_ref, work_ref, a1_ref, 0, 7)
    conv_layer(a1_ref, w2_ref, b2_ref, sea_ref, work_ref, a2_ref, 1, 6)
    conv_layer(a2_ref, w3_ref, b3_ref, sea_ref, work_ref, a3_ref, 2, 5)
    left = margin - HALO
    for group in range(4):
        found = conv_rows(a3_ref, w4_ref, group, COLS + 2 * left)
        around = [found[left:], jnp.zeros((WIDE - COLS - 2 * left, 128), F32)]
        if left:
            around.append(found[:left])
        turned = jnp.transpose(jnp.concatenate(around, axis=0))
        raw_ref[4 * group : 4 * group + 4] = turned[0:64].reshape(4, 16, WIDE)

    def shifted_difference(field):
        return (pltpu.roll(field, WIDE - 1, 2) - pltpu.roll(field, 1, 2)) * 0.5

    rows = ROWS + 2
    low = HALO - 1
    zonal = state_ref[low : low + rows, 0:8, :]
    merid_above = state_ref[low + 1 : low + 1 + rows, 8:16, :]
    merid_below = state_ref[low - 1 : low - 1 + rows, 8:16, :]
    divergence = shifted_difference(zonal) + (merid_above - merid_below) * 0.5
    thickness = state_ref[low : low + rows, 16:24, :]
    h_new = (thickness - TIME_STEP * divergence) * wet_ref[low : low + rows]
    level = lax.broadcasted_iota(jnp.int32, (1, 8, 1), 1)
    pressure = None
    for other in range(LEVELS):
        weight = 0.5 + 0.1 * jnp.minimum(level, other).astype(F32)
        term = weight * h_new[:, other : other + 1, :]
        pressure = term if pressure is None else pressure + term
    grad_x = shifted_difference(pressure[1:-1])
    grad_y = (pressure[2:] - pressure[:-2]) * 0.5
    wet = wet_ref[HALO : HALO + ROWS]
    zonal_mid = state_ref[HALO : HALO + ROWS, 0:8, :]
    merid_mid = state_ref[HALO : HALO + ROWS, 8:16, :]
    global_row = start_ref[0] + lax.broadcasted_iota(jnp.int32, (ROWS, 8, WIDE), 0)
    coriolis = 0.3 + 0.5 * global_row.astype(F32) / 512.0
    raw_zonal = raw_ref[:, 0:8, :]
    raw_merid = raw_ref[:, 8:16, :]
    zonal_new = (
        zonal_mid + TIME_STEP * (-grad_x + coriolis * merid_mid - DRAG * zonal_mid + raw_zonal)
    ) * wet
    merid_new = (
        merid_mid + TIME_STEP * (-grad_y - coriolis * zonal_mid - DRAG * merid_mid + raw_merid)
    ) * wet
    new_ref[:, 0:8, :] = zonal_new
    new_ref[:, 8:16, :] = merid_new
    new_ref[:, 16:24, :] = h_new[1:-1]
    if last:
        raw_out_ref[...] = raw_ref[...]
    else:
        flat = new_ref[...].reshape(ROWS * 24, WIDE).astype(BF16)
        send_down_ref[...] = flat[0 : HALO * 24]
        send_up_ref[...] = flat[(ROWS - HALO) * 24 :]

    def lanes_of(field):
        by_column = jnp.sum(field, axis=0)
        return by_column[:, 0:128] + by_column[:, 128:256]

    columns = jnp.concatenate(
        [
            lanes_of(raw_zonal * wet),
            lanes_of(raw_merid * wet),
            lanes_of(wet),
            jnp.zeros((104, 128), F32),
        ],
        axis=0,
    )
    row = jnp.sum(jnp.transpose(columns), axis=0, keepdims=True)
    pay_ref[...] = jnp.broadcast_to(row, (128, 128))


def ocean_network_step(step, args):
    first, last = step == 0, step == STEPS - 1
    span = COLS + 2 * MARGINS[step]
    outs = [
        jax.ShapeDtypeStruct((ROWS, 24, WIDE), F32),
        jax.ShapeDtypeStruct((128, 128), F32),
    ]
    if first:
        outs.append(jax.ShapeDtypeStruct((EXT_ROWS, LEVELS, WIDE), F32))
        outs.append(jax.ShapeDtypeStruct((WIDE + 8, 128), F32))
    if last:
        outs.append(jax.ShapeDtypeStruct((ROWS, 16, WIDE), F32))
    else:
        outs += [jax.ShapeDtypeStruct((HALO * 24, WIDE), BF16)] * 2
    vmem = pl.BlockSpec(memory_space=pltpu.VMEM)
    return pl.pallas_call(
        functools.partial(step_kernel, step=step),
        out_shape=outs,
        in_specs=[pl.BlockSpec(memory_space=pltpu.SMEM)] + [vmem] * (len(args) - 1),
        out_specs=[vmem] * len(outs),
        scratch_shapes=[
            pltpu.VMEM((EXT_ROWS, 32, WIDE), F32),
            pltpu.VMEM((8, span, 5 * 128), BF16),
            pltpu.VMEM((7, span, 5 * 512), BF16),
            pltpu.VMEM((6, span, 5 * 256), BF16),
            pltpu.VMEM((5, span, 5 * 128), BF16),
            pltpu.VMEM((span + 8, 512), F32),
            pltpu.VMEM((ROWS, 16, WIDE), F32),
            pltpu.VMEM((2, span, 128), BF16),
        ],
        name=f"step_{step}",
    )(*args)


def finish_kernel(recv_ref, state_ref, raw_ref, wet_ref, final_ref, forcing_ref, work_ref):
    zonal_mean, merid_mean = device_means(recv_ref[...])
    wet = wet_ref[HALO : HALO + ROWS, :, 0:COLS]
    zonal_mean = jnp.concatenate([zonal_mean] * 2, axis=1)[None]
    merid_mean = jnp.concatenate([merid_mean] * 2, axis=1)[None]
    work_ref[:, 0:8, :] = (raw_ref[:, 0:8, 0:COLS] - zonal_mean) * wet
    work_ref[:, 8:16, :] = (raw_ref[:, 8:16, 0:COLS] - merid_mean) * wet
    for channel in range(16):
        forcing_ref[channel] = work_ref[:, channel, :]
    work_ref[:, 0:8, :] = state_ref[:, 0:8, 0:COLS] - TIME_STEP * zonal_mean * wet
    work_ref[:, 8:16, :] = state_ref[:, 8:16, 0:COLS] - TIME_STEP * merid_mean * wet
    for channel in range(16):
        final_ref[channel] = work_ref[:, channel, :]
    for channel in range(16, 24):
        final_ref[channel] = state_ref[:, channel, 0:COLS]


def finish(received, state, raw, wet):
    return pl.pallas_call(
        finish_kernel,
        out_shape=[
            jax.ShapeDtypeStruct((24, ROWS, COLS), F32),
            jax.ShapeDtypeStruct((16, ROWS, COLS), F32),
        ],
        scratch_shapes=[pltpu.VMEM((ROWS, 16, COLS), F32)],
        name="finish",
    )(received, state, raw, wet)


def both_ways(axis, up, down):
    count = lax.axis_size(axis)
    forward = [(i, i + 1) for i in range(count - 1)]
    backward = [(target, source) for source, target in forward]
    return lax.ppermute(up, axis, forward), lax.ppermute(down, axis, backward)


def local(
    ocean_state,
    land_mask,
    layer_count,
    conv1_weight,
    conv1_bias,
    conv2_weight,
    conv2_bias,
    conv3_weight,
    conv3_bias,
    conv4_weight,
):
    state, send_left, send_right = prepare(ocean_state, land_mask, layer_count)
    left, right = both_ways("sec", send_right, send_left)
    weights = banded(
        [conv1_weight, conv2_weight, conv3_weight, conv4_weight],
        [conv1_bias, conv2_bias, conv3_bias],
    )
    lane = lax.broadcasted_iota(jnp.int32, left.shape, 1)
    sides = jnp.where(lane < SIDE, right, left)
    whole = jnp.concatenate([send_left, send_right, sides], axis=1)
    halos = both_ways("lat", whole[HALO * 32 :], whole[: HALO * 32])

    start = (lax.axis_index("lat") * ROWS).astype(jnp.int32)[None]
    extras = [left, right]
    for step in range(STEPS):
        results = ocean_network_step(step, [start, state, *halos, *extras, *weights])
        state = results[0]
        if step == 0:
            wet, sea = results[2:4]
        if step < STEPS - 1:
            halos = both_ways("lat", results[-2], results[-1])
        received = lax.all_to_all(results[1], ("sec", "lat"), 0, 0)
        extras = [received, wet, sea]
    return finish(received, state, results[2], wet)


def solution(mesh):
    return jax.shard_map(
        local,
        mesh=mesh,
        in_specs=(
            P(None, "lat", "sec"),
            P("lat", "sec"),
            P("lat", "sec"),
            P(),
            P(),
            P(),
            P(),
            P(),
            P(),
            P(),
        ),
        out_specs=(P(None, "lat", "sec"), P(None, "lat", "sec")),
        check_vma=False,
    )
```

time: 279 us -> 216 us (0.77)
  local copies, waits for them, and re-layouts: 31.2 us -> 4.6 us
  other arithmetic: 21.9 us -> 1.1 us
  waiting for transfers between devices: 18.9 us -> 2.25 us
  starting transfers between devices: 38.1 us -> 23.7 us
  Pallas kernels: 88.7 us -> 98.6 us
  blocking collectives: 77.3 us -> 84.9 us
    ppermute x16 -> x10, waiting for transfers between devices: 18.9 us -> 2.25 us  [both_ways(): return (lax.ppermute(up, axis, forward), lax.ppermute(down, axis, backward))]
    slice x19 -> x1, local copies, waits for them, and re-layouts: 16 us -> 0.04 us  [local(): halos = both_ways('lat', whole[HALO * 32:], whole[:HALO * 32])]
    concatenate x14 -> x1, other arithmetic: 16.5 us -> 1.08 us  [local(): whole = jnp.concatenate([send_left, send_right, sides], axis=1)]
    ppermute x16 -> x10, starting transfers between devices: 38.1 us -> 23.7 us  [both_ways(): return (lax.ppermute(up, axis, forward), lax.ppermute(down, axis, backward))]
    pallas_call x5 -> x7, Pallas kernels: 88.7 us -> 98.6 us  [the longest x4 89.6 us: ocean_network_step(): pl.pallas_call(functools.partial(step_kernel, step=step), out_shape=outs,...]
    all_to_all x4, blocking collectives: 77.3 us -> 84.9 us  [local(): received = lax.all_to_all(results[1], ('sec', 'lat'), 0, 0)]
    unnamed x51 -> x21, local copies, waits for them, and re-layouts: 8.84 us -> 4.56 us
    reshape x4 -> x0, local copies, waits for them, and re-layouts: 4.13 us -> none  [banded(): taps = weight.reshape(5, out_width, 5, in_width).transpose(2, 0, 3, 1)]
  transfers between devices with their start and end apart: 16 -> 10, of which waited for: 5 -> 2; matrix products, arithmetic and copies ran while one was open for 12% -> 1% of each run, Pallas kernels for 0% -> 2%
where the time goes in v3:
time: 216 us
  Pallas kernels  98.6 us (46%)
  blocking collectives  84.9 us (39%)
  starting transfers between devices  23.7 us (11%)
  local copies, waits for them, and re-layouts  4.6 us (2%)
  waiting for transfers between devices  2.25 us (1%)
    pallas_call x4, Pallas kernels, ocean_network_step(): pl.pallas_call(functools.partial(step_kernel, step=step), out_shape=outs,...  89.6 us
    all_to_all x4, blocking collectives, local(): received = lax.all_to_all(results[1], ('sec', 'lat'), 0, 0)  84.9 us
    ppermute x10, starting transfers between devices, both_ways(): return (lax.ppermute(up, axis, forward), lax.ppermute(down, axis, backward))  23.7 us
    unnamed x21, local copies, waits for them, and re-layouts  4.56 us
    pallas_call x1, Pallas kernels, banded(): pl.pallas_call(banded_kernel, out_shape=outs, scratch_shapes=[pltpu.VMEM(...  4.47 us
  transfers between devices with their start and end apart: 10, of which 2 were waited for; matrix products, arithmetic and copies ran while one was open for 1% of the time, Pallas kernels for 2%

profile of v3, /device:TPU:1, one launch (start us, length us, event | category | flops | bytes accessed | tf_op | source)
XLA Modules:
  0.0 215.9 jit_solution(16994147731169299371)
XLA Ops:
  0.6 2.1 prepare.1
  2.7 3.3 %collective-permute-start = (bf16[512,128]{1,0:T(8,128)(2,1)}, bf16[512,128]{1,0:T(8,128)(2,1)S(1)}, u32[]{:S(2)}, u32[]{:S(2)}) collective-permute-start(bf16[512,128]{1,0:T(8,128)(2,1)} %get-tuple-element.30), channel_id=1, source_target_pairs={{32,0},{64,32},{96,64},{33,1},{65,33},{97,65},{34,2},{66,34},{98,6... | collective-permute-start | bytes 393224 | tf_op jit(solution)/shard_map/ppermute | solution.py:347
  6.0 3.6 %collective-permute-start.1 = (bf16[512,128]{1,0:T(8,128)(2,1)}, bf16[512,128]{1,0:T(8,128)(2,1)S(1)}, u32[]{:S(2)}, u32[]{:S(2)}) collective-permute-start(bf16[512,128]{1,0:T(8,128)(2,1)} %get-tuple-element.31), channel_id=1, source_target_pairs={{0,32},{32,64},{64,96},{1,33},{33,65},{65,97},{2,34},{34,66},{66,9... | collective-permute-start | bytes 393224 | tf_op jit(solution)/shard_map/ppermute | solution.py:347
  10.5 1.3 collective-permute-done.1.refs_4_
  11.8 1.1 pad_maximum_fusion
  13.0 1.3 collective-permute-start.3
  14.3 4.0 %collective-permute-start.2 = (bf16[256,384]{1,0:T(8,128)(2,1)S(1)}, bf16[256,384]{1,0:T(8,128)(2,1)S(1)}, u32[]{:S(2)}, u32[]{:S(2)}) collective-permute-start(bf16[256,384]{1,0:T(8,128)(2,1)S(1)} %get-tuple-element.57), channel_id=1, source_target_pairs={{0,1},{1,2},{2,3},{3,4},{4,5},{5,6},{6,7},{7,8},{8,9},{9,10},{10,1... | collective-permute-start | bytes 589832 | tf_op jit(solution)/shard_map/ppermute | solution.py:347
  18.3 1.7 copy.13.refs_0_
  20.0 4.5 %banded.1 = (bf16[1280,512]{1,0:T(8,128)(2,1)}, bf16[5120,256]{1,0:T(8,128)(2,1)}, bf16[2560,128]{1,0:T(8,128)(2,1)}, bf16[1280,128]{1,0:T(8,128)(2,1)}, f32[1,5...) custom-call(bf16[5,128,120]{2,1,0:T(8,128)(2,1)} %copy.13.refs_0_, bf16[5,64,640]{2,1,0:T(8,128)(2,1)} %refs_1_.1, ...), custom_call_target="tpu_custom_call" | custom-call | tf_op jit(solution)/shard_map/banded/pallas_call | solution.py:71
  25.2 23.6 %step_0.1 = (f32[16,24,384]{2,1,0:T(8,128)}, f32[128,128]{1,0:T(8,128)}, f32[32,8,384]{2,1,0:T(8,128)}, f32[392,128]{1,0:T(8,128)}, bf16[192,384]{1,0:T(8,128)(2,1)}, /*index=5*/bf16[192,384]{1,0:T(8,128)(2,1)}) custom-call(s32[1]{0:T(128)} %bitcast.refs_0_, f32[16,32,256]{2,1,0:T(8,128)} %get-tuple-element.29.refs_1_, bf16[256,384]{1,0:T(8,128)(2,1)} %copy-done.3, ...), custom_call_target="tpu_custom_call" | custom-call | tf_op jit(solution)/shard_map/step_0/pallas_call | solution.py:295
  48.8 3.2 %collective-permute-start.4 = (bf16[192,384]{1,0:T(8,128)(2,1)}, bf16[192,384]{1,0:T(8,128)(2,1)S(1)}, u32[]{:S(2)}, u32[]{:S(2)}) collective-permute-start(bf16[192,384]{1,0:T(8,128)(2,1)} %get-tuple-element.40), channel_id=1, source_target_pairs={{0,1},{1,2},{2,3},{3,4},{4,5},{5,6},{6,7},{7,8},{8,9},{9,10},{10,1... | collective-permute-start | bytes 442376 | tf_op jit(solution)/shard_map/ppermute | solution.py:347
  52.0 1.3 collective-permute-start.5
  53.3 29.8 %all_to_all.44 = f32[128,1,128]{2,1,0:T(1,128)} all-to-all(f32[128,1,128]{2,1,0:T(1,128)} %bitcast.24), channel_id=1, replica_groups=mesh['sec'=4,'lat'=32] {'sec','lat'}, dimensions={0} | all-to-all | bytes 131072 | tf_op jit(solution)/shard_map/all_to_all | solution.py:382
  83.8 22.8 %step_1.1 = (f32[16,24,384]{2,1,0:T(8,128)}, f32[128,128]{1,0:T(8,128)}, bf16[192,384]{1,0:T(8,128)(2,1)}, bf16[192,384]{1,0:T(8,128)(2,1)}) custom-call(s32[1]{0:T(128)} %bitcast.refs_0_, f32[16,24,384]{2,1,0:T(8,128)} %get-tuple-element.39.refs_1_, bf16[192,384]{1,0:T(8,128)(2,1)} %copy-done.6, bf16[192,384]{1,0:T(8,128)(2,1)} %copy-done.8, ...), custom_call_target="tpu_custom_call" | custom-call | tf_op jit(solution)/shard_map/step_1/pallas_call | solution.py:295
  106.6 2.3 %collective-permute-start.6 = (bf16[192,384]{1,0:T(8,128)(2,1)}, bf16[192,384]{1,0:T(8,128)(2,1)S(1)}, u32[]{:S(2)}, u32[]{:S(2)}) collective-permute-start(bf16[192,384]{1,0:T(8,128)(2,1)} %get-tuple-element.46), channel_id=1, source_target_pairs={{0,1},{1,2},{2,3},{3,4},{4,5},{5,6},{6,7},{7,8},{8,9},{9,10},{10,1... | collective-permute-start | bytes 442376 | tf_op jit(solution)/shard_map/ppermute | solution.py:347
  108.9 1.3 collective-permute-start.7
  110.2 20.0 %all_to_all.45 = f32[128,1,128]{2,1,0:T(1,128)} all-to-all(f32[128,1,128]{2,1,0:T(1,128)} %bitcast.25), channel_id=1, replica_groups=mesh['sec'=4,'lat'=32] {'sec','lat'}, dimensions={0} | all-to-all | bytes 131072 | tf_op jit(solution)/shard_map/all_to_all | solution.py:382
  130.9 21.9 %step_2.1 = (f32[16,24,384]{2,1,0:T(8,128)}, f32[128,128]{1,0:T(8,128)}, bf16[192,384]{1,0:T(8,128)(2,1)}, bf16[192,384]{1,0:T(8,128)(2,1)}) custom-call(s32[1]{0:T(128)} %bitcast.refs_0_, f32[16,24,384]{2,1,0:T(8,128)} %get-tuple-element.45.refs_1_, bf16[192,384]{1,0:T(8,128)(2,1)} %copy-done.7, bf16[192,384]{1,0:T(8,128)(2,1)} %copy-done.9, ...), custom_call_target="tpu_custom_call" | custom-call | tf_op jit(solution)/shard_map/step_2/pallas_call | solution.py:295
  152.8 2.2 %collective-permute-start.8 = (bf16[192,384]{1,0:T(8,128)(2,1)}, bf16[192,384]{1,0:T(8,128)(2,1)S(1)}, u32[]{:S(2)}, u32[]{:S(2)}) collective-permute-start(bf16[192,384]{1,0:T(8,128)(2,1)} %get-tuple-element.50), channel_id=1, source_target_pairs={{0,1},{1,2},{2,3},{3,4},{4,5},{5,6},{6,7},{7,8},{8,9},{9,10},{10,1... | collective-permute-start | bytes 442376 | tf_op jit(solution)/shard_map/ppermute | solution.py:347
  155.0 1.3 collective-permute-start.9
  156.3 19.8 %all_to_all.46 = f32[128,1,128]{2,1,0:T(1,128)} all-to-all(f32[128,1,128]{2,1,0:T(1,128)} %bitcast.26), channel_id=1, replica_groups=mesh['sec'=4,'lat'=32] {'sec','lat'}, dimensions={0} | all-to-all | bytes 131072 | tf_op jit(solution)/shard_map/all_to_all | solution.py:382
  176.8 21.3 %step_3.1 = (f32[16,24,384]{2,1,0:T(8,128)}, f32[128,128]{1,0:T(8,128)}, f32[16,16,384]{2,1,0:T(8,128)}) custom-call(s32[1]{0:T(128)} %bitcast.refs_0_, f32[16,24,384]{2,1,0:T(8,128)} %get-tuple-element.49.refs_1_, bf16[192,384]{1,0:T(8,128)(2,1)} %copy-done.4, bf16[192,384]{1,0:T(8,128)(2,1)} %copy-done.5, f32[128,128]{1,0:T(8,128)} %bitcast.20, ...), custom_call_target="tpu_custom_call" | custom-call | tf_op jit(solution)/shard_map/step_3/pallas_call | solution.py:295
  198.1 15.3 %all_to_all.47 = f32[128,1,128]{2,1,0:T(1,128)} all-to-all(f32[128,1,128]{2,1,0:T(1,128)} %bitcast.27), channel_id=1, replica_groups=mesh['sec'=4,'lat'=32] {'sec','lat'}, dimensions={0} | all-to-all | bytes 131072 | tf_op jit(solution)/shard_map/all_to_all | solution.py:382
  213.5 2.4 %finish.1 = (f32[24,16,256]{2,1,0:T(8,128)}, f32[16,16,256]{2,1,0:T(8,128)}) custom-call(f32[128,128]{1,0:T(8,128)} %bitcast.23, f32[16,24,384]{2,1,0:T(8,128)} %get-tuple-element.54.state_ref, f32[16,16,384]{2,1,0:T(8,128)} %get-tuple-element.55.raw_ref, f32[32,8,384]{2,1,0:T(8,128)} %get-tuple-element.43.refs_5_.wet_ref), custom_call_target="tpu_custom_call" | custom-call | tf_op jit(solution)/shard_map/finish/pallas_call | solution.py:332
  (32 shorter events, 3.8 us)
Async XLA Ops:
  2.7 7.8 %collective-permute-start = (bf16[512,128]{1,0:T(8,128)(2,1)}, bf16[512,128]{1,0:T(8,128)(2,1)S(1)}, u32[]{:S(2)}, u32[]{:S(2)}) collective-permute-start(bf16[512,128]{1,0:T(8,128)(2,1)} %get-tuple-element.30), channel_id=1, source_target_pairs={{32,0},{64,32},{96,64},{33,1},{65,33},{97,65},{34,2},{66,34},{98,6... | collective-permute-start | bytes 393224 | tf_op jit(solution)/shard_map/ppermute | solution.py:347
  6.0 5.8 %collective-permute-start.1 = (bf16[512,128]{1,0:T(8,128)(2,1)}, bf16[512,128]{1,0:T(8,128)(2,1)S(1)}, u32[]{:S(2)}, u32[]{:S(2)}) collective-permute-start(bf16[512,128]{1,0:T(8,128)(2,1)} %get-tuple-element.31), channel_id=1, source_target_pairs={{0,32},{32,64},{64,96},{1,33},{33,65},{65,97},{2,34},{34,66},{66,9... | collective-permute-start | bytes 393224 | tf_op jit(solution)/shard_map/ppermute | solution.py:347
  10.5 14.0 %copy-start = (bf16[512,128]{1,0:T(8,128)(2,1)}, bf16[512,128]{1,0:T(8,128)(2,1)S(1)}, u32[]{:S(2)}) copy-start(bf16[512,128]{1,0:T(8,128)(2,1)S(1)} %collective-permute-done.refs_5_) | copy-start | bytes 393220
  11.8 12.7 %copy-start.1 = (bf16[512,128]{1,0:T(8,128)(2,1)}, bf16[512,128]{1,0:T(8,128)(2,1)S(1)}, u32[]{:S(2)}) copy-start(bf16[512,128]{1,0:T(8,128)(2,1)S(1)} %collective-permute-done.1.refs_4_) | copy-start | bytes 393220
  13.0 11.5 %collective-permute-start.3 = (bf16[256,384]{1,0:T(8,128)(2,1)S(1)}, bf16[256,384]{1,0:T(8,128)(2,1)S(1)}, u32[]{:S(2)}, u32[]{:S(2)}) collective-permute-start(bf16[256,384]{1,0:T(8,128)(2,1)S(1)} %get-tuple-element.56), channel_id=1, source_target_pairs={{1,0},{2,1},{3,2},{4,3},{5,4},{6,5},{7,6},{8,7},{9,8},{10,9},{11,1... | collective-permute-start | bytes 589832 | tf_op jit(solution)/shard_map/ppermute | solution.py:347
  14.3 10.2 %collective-permute-start.2 = (bf16[256,384]{1,0:T(8,128)(2,1)S(1)}, bf16[256,384]{1,0:T(8,128)(2,1)S(1)}, u32[]{:S(2)}, u32[]{:S(2)}) collective-permute-start(bf16[256,384]{1,0:T(8,128)(2,1)S(1)} %get-tuple-element.57), channel_id=1, source_target_pairs={{0,1},{1,2},{2,3},{3,4},{4,5},{5,6},{6,7},{7,8},{8,9},{9,10},{10,1... | collective-permute-start | bytes 589832 | tf_op jit(solution)/shard_map/ppermute | solution.py:347
  24.5 0.7 copy-start.2
  24.5 0.8 copy-start.3
  48.8 34.3 %collective-permute-start.4 = (bf16[192,384]{1,0:T(8,128)(2,1)}, bf16[192,384]{1,0:T(8,128)(2,1)S(1)}, u32[]{:S(2)}, u32[]{:S(2)}) collective-permute-start(bf16[192,384]{1,0:T(8,128)(2,1)} %get-tuple-element.40), channel_id=1, source_target_pairs={{0,1},{1,2},{2,3},{3,4},{4,5},{5,6},{6,7},{7,8},{8,9},{9,10},{10,1... | collective-permute-start | bytes 442376 | tf_op jit(solution)/shard_map/ppermute | solution.py:347
  52.0 31.1 %collective-permute-start.5 = (bf16[192,384]{1,0:T(8,128)(2,1)}, bf16[192,384]{1,0:T(8,128)(2,1)S(1)}, u32[]{:S(2)}, u32[]{:S(2)}) collective-permute-start(bf16[192,384]{1,0:T(8,128)(2,1)} %get-tuple-element.41), channel_id=1, source_target_pairs={{1,0},{2,1},{3,2},{4,3},{5,4},{6,5},{7,6},{8,7},{9,8},{10,9},{11,1... | collective-permute-start | bytes 442376 | tf_op jit(solution)/shard_map/ppermute | solution.py:347
  83.1 0.7 copy-start.6
  83.1 0.7 copy-start.8
  106.6 23.6 %collective-permute-start.6 = (bf16[192,384]{1,0:T(8,128)(2,1)}, bf16[192,384]{1,0:T(8,128)(2,1)S(1)}, u32[]{:S(2)}, u32[]{:S(2)}) collective-permute-start(bf16[192,384]{1,0:T(8,128)(2,1)} %get-tuple-element.46), channel_id=1, source_target_pairs={{0,1},{1,2},{2,3},{3,4},{4,5},{5,6},{6,7},{7,8},{8,9},{9,10},{10,1... | collective-permute-start | bytes 442376 | tf_op jit(solution)/shard_map/ppermute | solution.py:347
  108.9 21.3 %collective-permute-start.7 = (bf16[192,384]{1,0:T(8,128)(2,1)}, bf16[192,384]{1,0:T(8,128)(2,1)S(1)}, u32[]{:S(2)}, u32[]{:S(2)}) collective-permute-start(bf16[192,384]{1,0:T(8,128)(2,1)} %get-tuple-element.47), channel_id=1, source_target_pairs={{1,0},{2,1},{3,2},{4,3},{5,4},{6,5},{7,6},{8,7},{9,8},{10,9},{11,1... | collective-permute-start | bytes 442376 | tf_op jit(solution)/shard_map/ppermute | solution.py:347
  130.2 0.7 copy-start.7
  130.2 0.7 copy-start.9
  152.8 23.3 %collective-permute-start.8 = (bf16[192,384]{1,0:T(8,128)(2,1)}, bf16[192,384]{1,0:T(8,128)(2,1)S(1)}, u32[]{:S(2)}, u32[]{:S(2)}) collective-permute-start(bf16[192,384]{1,0:T(8,128)(2,1)} %get-tuple-element.50), channel_id=1, source_target_pairs={{0,1},{1,2},{2,3},{3,4},{4,5},{5,6},{6,7},{7,8},{8,9},{9,10},{10,1... | collective-permute-start | bytes 442376 | tf_op jit(solution)/shard_map/ppermute | solution.py:347
  155.0 21.1 %collective-permute-start.9 = (bf16[192,384]{1,0:T(8,128)(2,1)}, bf16[192,384]{1,0:T(8,128)(2,1)S(1)}, u32[]{:S(2)}, u32[]{:S(2)}) collective-permute-start(bf16[192,384]{1,0:T(8,128)(2,1)} %get-tuple-element.51), channel_id=1, source_target_pairs={{1,0},{2,1},{3,2},{4,3},{5,4},{6,5},{7,6},{8,7},{9,8},{10,9},{11,1... | collective-permute-start | bytes 442376 | tf_op jit(solution)/shard_map/ppermute | solution.py:347
  176.1 0.6 copy-start.4
  176.1 0.7 copy-start.5

commit v4 on v3

--- a/solution.py
+++ b/solution.py
@@ -19,6 +19,7 @@
 SIDE = 64
 MARGINS = tuple(HALO * (STEPS - step) for step in range(STEPS))
 LAND_OFFSET = -(2.0**24)
+PADDED = (32, 128, 64, 32)
 F32 = jnp.float32
 BF16 = jnp.bfloat16
 
@@ -30,19 +31,21 @@
         weight_ref, band_ref = weight_refs[layer], band_refs[layer]
         out_width = weight_ref.shape[1]
         in_width = weight_ref.shape[2] // 5
-        in_pad = band_ref.shape[0] // 40
+        in_pad = PADDED[layer]
+        groups = band_ref.shape[0] // (20 * in_pad)
+        out_rows = band_ref.shape[1] // out_width
         wide = -(-5 * in_width // 128) * 128
         flat_ref[...] = jnp.zeros(flat_ref.shape, F32)
         for offset in range(5):
             flat_ref[0:out_width, 0 : 5 * in_width] = weight_ref[offset].astype(F32)
             turned_ref[offset, 0:wide, :] = jnp.transpose(flat_ref[:, 0:wide])
         extra = in_pad - in_width
-        for half in range(2):
+        for group in range(groups):
             for shift in range(5):
                 for row in range(4):
                     parts = []
-                    for out_row in range(4):
-                        offset = 4 * half + row - out_row
+                    for out_row in range(out_rows):
+                        offset = 4 * group + row - out_row
                         if not 0 <= offset < 5:
                             parts.append(jnp.zeros((in_pad, out_width), F32))
                             continue
@@ -56,16 +59,14 @@
                                 pad = jnp.where(first, LAND_OFFSET, 0.0)
                             part = jnp.concatenate([part, pad], axis=0)
                         parts.append(part)
-                    if 4 * out_width < band_ref.shape[1]:
-                        parts.append(jnp.zeros((in_pad, band_ref.shape[1] - 4 * out_width), F32))
-                    base = ((half * 5 + shift) * 4 + row) * in_pad
+                    base = ((group * 5 + shift) * 4 + row) * in_pad
                     band_ref[base : base + in_pad, :] = jnp.concatenate(parts, axis=1).astype(BF16)
     for bias_ref, row_ref in zip(bias_refs, row_refs):
         row_ref[...] = jnp.concatenate([bias_ref[...]] * 4, axis=1)
 
 
 def banded(weights, biases):
-    shapes = [(1280, 512), (5120, 256), (2560, 128), (1280, 128)]
+    shapes = [(1280, 512), (5120, 256), (2560, 128), (3200, 256)]
     outs = [jax.ShapeDtypeStruct(shape, BF16) for shape in shapes]
     outs += [jax.ShapeDtypeStruct((1, width), F32) for width in (512, 256, 128)]
     return pl.pallas_call(
@@ -97,25 +98,25 @@
     )(ocean_state, land_mask, layer_count)
 
 
-def conv_rows(in_ref, weight_ref, group, count):
-    lhs = jnp.concatenate([in_ref[group, 0:count, :], in_ref[group + 1, 0:count, :]], axis=1)
-    return jnp.dot(lhs, weight_ref[...], preferred_element_type=F32)
-
-
-def spread(value, work_ref, out_ref, group, width):
-    span = value.shape[0]
-    work_ref[0:span, 0:width] = value
-    for shift in range(5):
-        out_ref[group, :, shift * width : (shift + 1) * width] = work_ref[
-            shift : shift + span, 0:width
-        ].astype(BF16)
-
-
-def conv_layer(in_ref, weight_ref, bias_ref, sea_ref, work_ref, out_ref, layer, groups):
+def spread(value, work_ref, out_ref, group, zero):
+    span, width = value.shape
+    out_ref[group, :, 0:width] = value.astype(BF16)
+    for tile in range(width // 128):
+        work_ref[tile, 0:span, :] = value[:, 128 * tile : 128 * tile + 128]
+    for shift in range(1, 5):
+        for tile in range(width // 128):
+            base = shift * width + 128 * tile
+            out_ref[group, :, base : base + 128] = work_ref[
+                tile, pl.ds(zero + shift, span), :
+            ].astype(BF16)
+
+
+def conv_layer(refs, raw_ref, sea_ref, work_ref, zero, layer, groups):
+    in_ref, weight_ref, bias_ref, out_ref = refs
     width = weight_ref.shape[1]
 
-    def body(group, carry):
-        half = 0.5 * (conv_rows(in_ref, weight_ref, group, in_ref.shape[1]) + bias_ref[...])
+    def activate(group):
+        half = 0.5 * (raw_ref[:, 0:width] + bias_ref[...])
         value = half + half * jnp.tanh(half)
         if layer:
             row_of = lax.broadcasted_iota(jnp.int32, (128, width), 0)
@@ -123,10 +124,16 @@
             wanted = 4 * group + 2 * (layer + 1) + lane_of // (width // 4)
             pick = jnp.where(row_of == wanted, 1.0, 0.0).astype(BF16)
             value = value * jnp.dot(sea_ref[layer - 1], pick, preferred_element_type=F32)
-        spread(value, work_ref, out_ref, group, width)
+        spread(value, work_ref, out_ref, group, zero)
+
+    def body(group, carry):
+        activate(jnp.maximum(group - 1, 0))
+        lhs = jnp.concatenate([in_ref[group], in_ref[group + 1]], axis=1)
+        raw_ref[:, 0:width] = jnp.dot(lhs, weight_ref[...], preferred_element_type=F32)
         return carry
 
     lax.fori_loop(0, groups, body, 0)
+    activate(groups - 1)
 
 
 def device_means(received):
@@ -160,7 +167,8 @@
     else:
         send_up_ref, send_down_ref = refs[:2]
         refs = refs[2:]
-    state_ref, a0_ref, a1_ref, a2_ref, a3_ref, work_ref, raw_ref, sea_ref = refs
+    state_ref, a0_ref, a1_ref, a2_ref, a3_ref, work_ref, raw_ref, sea_ref, sum_ref = refs
+    zero = start_ref[1]
 
     if first:
         lane = lax.broadcasted_iota(jnp.int32, (ROWS * 32, 128), 1)
@@ -195,28 +203,28 @@
         begin = SIDE - margin + 2 * (layer + 1)
         sea_ref[layer - 1] = sea_turned_ref[begin : begin + span, :].astype(BF16)
 
-    work_ref[span:, :] = jnp.zeros((8, 512), F32)
+    work_ref[:, span:, :] = jnp.zeros((4, 8, 128), F32)
     for group in range(8):
         flat = state_ref[4 * group : 4 * group + 4].reshape(128, WIDE)
         turned = jnp.transpose(flat)
-        spread(
-            jnp.concatenate([turned[WIDE - margin :], turned[0 : COLS + margin]], axis=0),
-            work_ref,
-            a0_ref,
-            group,
-            128,
+        around = jnp.concatenate([turned[WIDE - margin :], turned[0 : COLS + margin]], axis=0)
+        spread(around, work_ref, a0_ref, group, zero)
+    for layer, refs in enumerate(
+        (
+            (a0_ref, w1_ref, b1_ref, a1_ref),
+            (a1_ref, w2_ref, b2_ref, a2_ref),
+            (a2_ref, w3_ref, b3_ref, a3_ref),
         )
-    conv_layer(a0_ref, w1_ref, b1_ref, sea_ref, work_ref, a1_ref, 0, 7)
-    conv_layer(a1_ref, w2_ref, b2_ref, sea_ref, work_ref, a2_ref, 1, 6)
-    conv_layer(a2_ref, w3_ref, b3_ref, sea_ref, work_ref, a3_ref, 2, 5)
+    ):
+        conv_layer(refs, sum_ref, sea_ref, work_ref, zero, layer, 7 - layer)
     left = margin - HALO
-    for group in range(4):
-        found = conv_rows(a3_ref, w4_ref, group, COLS + 2 * left)
-        around = [found[left:], jnp.zeros((WIDE - COLS - 2 * left, 128), F32)]
-        if left:
-            around.append(found[:left])
-        turned = jnp.transpose(jnp.concatenate(around, axis=0))
-        raw_ref[4 * group : 4 * group + 4] = turned[0:64].reshape(4, 16, WIDE)
+    count = COLS + 2 * left
+    lhs = jnp.concatenate([a3_ref[group, 0:count, :] for group in range(5)], axis=1)
+    found = jnp.dot(lhs, w4_ref[...], preferred_element_type=F32)
+    around = [found[left:], jnp.zeros((WIDE - count, 256), F32)]
+    if left:
+        around.append(found[:left])
+    raw_ref[...] = jnp.transpose(jnp.concatenate(around, axis=0)).reshape(ROWS, 16, WIDE)
 
     def shifted_difference(field):
         return (pltpu.roll(field, WIDE - 1, 2) - pltpu.roll(field, 1, 2)) * 0.5
@@ -303,9 +311,10 @@
             pltpu.VMEM((7, span, 5 * 512), BF16),
             pltpu.VMEM((6, span, 5 * 256), BF16),
             pltpu.VMEM((5, span, 5 * 128), BF16),
-            pltpu.VMEM((span + 8, 512), F32),
+            pltpu.VMEM((4, span + 8, 128), F32),
             pltpu.VMEM((ROWS, 16, WIDE), F32),
             pltpu.VMEM((2, span, 128), BF16),
+            pltpu.VMEM((span, 512), F32),
         ],
         name=f"step_{step}",
     )(*args)
@@ -370,7 +379,8 @@
     whole = jnp.concatenate([send_left, send_right, sides], axis=1)
     halos = both_ways("lat", whole[HALO * 32 :], whole[: HALO * 32])
 
-    start = (lax.axis_index("lat") * ROWS).astype(jnp.int32)[None]
+    start = (lax.axis_index("lat") * ROWS).astype(jnp.int32)
+    start = jnp.stack([start, jnp.zeros((), jnp.int32)])
     extras = [left, right]
     for step in range(STEPS):
         results = ocean_network_step(step, [start, state, *halos, *extras, *weights])

time: 216 us -> 211 us (0.977)
  Pallas kernels: 98.6 us -> 93.7 us
    pallas_call x4, Pallas kernels: 89.6 us -> 84.3 us  [ocean_network_step(): pl.pallas_call(functools.partial(step_kernel, step=step), out_shape=outs,...]
    unnamed x21 -> x23, local copies, waits for them, and re-layouts: 4.56 us -> 3.61 us
where the time goes in v4:
time: 211 us
  Pallas kernels  93.7 us (44%)
  blocking collectives  84.8 us (40%)
  starting transfers between devices  23.5 us (11%)
  local copies, waits for them, and re-layouts  3.65 us (2%)
  waiting for transfers between devices  2.25 us (1%)
    all_to_all x4, blocking collectives, local(): received = lax.all_to_all(results[1], ('sec', 'lat'), 0, 0)  84.8 us
    pallas_call x4, Pallas kernels, ocean_network_step(): pl.pallas_call(functools.partial(step_kernel, step=step), out_shape=outs,...  84.3 us
    ppermute x10, starting transfers between devices, both_ways(): return (lax.ppermute(up, axis, forward), lax.ppermute(down, axis, backward))  23.5 us
    pallas_call x1, Pallas kernels, banded(): pl.pallas_call(banded_kernel, out_shape=outs, scratch_shapes=[pltpu.VMEM(...  4.9 us
  transfers between devices with their start and end apart: 10, of which 2 were waited for; matrix products, arithmetic and copies ran while one was open for 1% of the time, Pallas kernels for 2%

profile of v4, /device:TPU:1, one launch (start us, length us, event | category | flops | bytes accessed | tf_op | source)
XLA Modules:
  0.0 210.6 jit_solution(17095483901174037249)
XLA Ops:
  0.6 2.1 %prepare.1 = (f32[16,32,256]{2,1,0:T(8,128)}, bf16[512,128]{1,0:T(8,128)(2,1)}, bf16[512,128]{1,0:T(8,128)(2,1)}) custom-call(f32[24,16,256]{2,1,0:T(8,128)} %state_ref.1, s32[16,256]{1,0:T(8,128)} %land_ref.1, s32[16,256]{1,0:T(8,128)} %count_ref.1), custom_call_target="tpu_custom_call" | custom-call | tf_op jit(solution)/shard_map/prepare/pallas_call | solution.py:93
  2.8 3.3 %collective-permute-start = (bf16[512,128]{1,0:T(8,128)(2,1)}, bf16[512,128]{1,0:T(8,128)(2,1)S(1)}, u32[]{:S(2)}, u32[]{:S(2)}) collective-permute-start(bf16[512,128]{1,0:T(8,128)(2,1)} %get-tuple-element.30), channel_id=1, source_target_pairs={{32,0},{64,32},{96,64},{33,1},{65,33},{97,65},{34,2},{66,34},{98,6... | collective-permute-start | bytes 393224 | tf_op jit(solution)/shard_map/ppermute | solution.py:356
  6.1 3.6 %collective-permute-start.1 = (bf16[512,128]{1,0:T(8,128)(2,1)}, bf16[512,128]{1,0:T(8,128)(2,1)S(1)}, u32[]{:S(2)}, u32[]{:S(2)}) collective-permute-start(bf16[512,128]{1,0:T(8,128)(2,1)} %get-tuple-element.31), channel_id=1, source_target_pairs={{0,32},{32,64},{64,96},{1,33},{33,65},{65,97},{2,34},{34,66},{66,9... | collective-permute-start | bytes 393224 | tf_op jit(solution)/shard_map/ppermute | solution.py:356
  9.6 0.9 collective-permute-done.refs_5_
  10.5 1.3 collective-permute-done.1.refs_4_
  11.9 1.1 pad_maximum_fusion
  13.0 1.3 collective-permute-start.3
  14.3 4.0 %collective-permute-start.2 = (bf16[256,384]{1,0:T(8,128)(2,1)S(1)}, bf16[256,384]{1,0:T(8,128)(2,1)S(1)}, u32[]{:S(2)}, u32[]{:S(2)}) collective-permute-start(bf16[256,384]{1,0:T(8,128)(2,1)S(1)} %get-tuple-element.57), channel_id=1, source_target_pairs={{0,1},{1,2},{2,3},{3,4},{4,5},{5,6},{6,7},{7,8},{8,9},{9,10},{10,1... | collective-permute-start | bytes 589832 | tf_op jit(solution)/shard_map/ppermute | solution.py:356
  19.2 4.9 %banded.1 = (bf16[1280,512]{1,0:T(8,128)(2,1)}, bf16[5120,256]{1,0:T(8,128)(2,1)}, bf16[2560,128]{1,0:T(8,128)(2,1)}, bf16[3200,256]{1,0:T(8,128)(2,1)}, f32[1,5...) custom-call(bf16[5,128,120]{2,1,0:T(8,128)(2,1)} %copy.13.refs_0_, bf16[5,64,640]{2,1,0:T(8,128)(2,1)} %refs_1_.1, ...), custom_call_target="tpu_custom_call" | custom-call | tf_op jit(solution)/shard_map/banded/pallas_call | solution.py:72
  25.5 22.2 %step_0.1 = (f32[16,24,384]{2,1,0:T(8,128)}, f32[128,128]{1,0:T(8,128)}, f32[32,8,384]{2,1,0:T(8,128)}, f32[392,128]{1,0:T(8,128)}, bf16[192,384]{1,0:T(8,128)(2,1)}, /*index=5*/bf16[192,384]{1,0:T(8,128)(2,1)}) custom-call(s32[2]{0:T(128)} %pad_add_fusion.refs_0_, f32[16,32,256]{2,1,0:T(8,128)} %get-tuple-element.29.refs_1_, bf16[256,384]{1,0:T(8,128)(2,1)} %copy-done.3, ...), custom_call_target="tpu_custom_call" | custom-call | tf_op jit(solution)/shard_map/step_0/pallas_call | solution.py:303
  47.7 3.2 %collective-permute-start.4 = (bf16[192,384]{1,0:T(8,128)(2,1)}, bf16[192,384]{1,0:T(8,128)(2,1)S(1)}, u32[]{:S(2)}, u32[]{:S(2)}) collective-permute-start(bf16[192,384]{1,0:T(8,128)(2,1)} %get-tuple-element.40), channel_id=1, source_target_pairs={{0,1},{1,2},{2,3},{3,4},{4,5},{5,6},{6,7},{7,8},{8,9},{9,10},{10,1... | collective-permute-start | bytes 442376 | tf_op jit(solution)/shard_map/ppermute | solution.py:356
  50.9 1.3 collective-permute-start.5
  52.2 29.6 %all_to_all.44 = f32[128,1,128]{2,1,0:T(1,128)} all-to-all(f32[128,1,128]{2,1,0:T(1,128)} %bitcast.24), channel_id=1, replica_groups=mesh['sec'=4,'lat'=32] {'sec','lat'}, dimensions={0} | all-to-all | bytes 131072 | tf_op jit(solution)/shard_map/all_to_all | solution.py:392
  82.5 21.5 %step_1.1 = (f32[16,24,384]{2,1,0:T(8,128)}, f32[128,128]{1,0:T(8,128)}, bf16[192,384]{1,0:T(8,128)(2,1)}, bf16[192,384]{1,0:T(8,128)(2,1)}) custom-call(s32[2]{0:T(128)} %pad_add_fusion.refs_0_, f32[16,24,384]{2,1,0:T(8,128)} %get-tuple-element.39.refs_1_, bf16[192,384]{1,0:T(8,128)(2,1)} %copy-done.7, bf16[192,384]{1,0:T(8,128)(2,1)} %copy-done.9, ...), custom_call_target="tpu_custom_call" | custom-call | tf_op jit(solution)/shard_map/step_1/pallas_call | solution.py:303
  104.0 2.2 %collective-permute-start.6 = (bf16[192,384]{1,0:T(8,128)(2,1)}, bf16[192,384]{1,0:T(8,128)(2,1)S(1)}, u32[]{:S(2)}, u32[]{:S(2)}) collective-permute-start(bf16[192,384]{1,0:T(8,128)(2,1)} %get-tuple-element.46), channel_id=1, source_target_pairs={{0,1},{1,2},{2,3},{3,4},{4,5},{5,6},{6,7},{7,8},{8,9},{9,10},{10,1... | collective-permute-start | bytes 442376 | tf_op jit(solution)/shard_map/ppermute | solution.py:356
  106.1 1.3 collective-permute-start.7
  107.4 20.0 %all_to_all.45 = f32[128,1,128]{2,1,0:T(1,128)} all-to-all(f32[128,1,128]{2,1,0:T(1,128)} %bitcast.25), channel_id=1, replica_groups=mesh['sec'=4,'lat'=32] {'sec','lat'}, dimensions={0} | all-to-all | bytes 131072 | tf_op jit(solution)/shard_map/all_to_all | solution.py:392
  128.1 20.6 %step_2.1 = (f32[16,24,384]{2,1,0:T(8,128)}, f32[128,128]{1,0:T(8,128)}, bf16[192,384]{1,0:T(8,128)(2,1)}, bf16[192,384]{1,0:T(8,128)(2,1)}) custom-call(s32[2]{0:T(128)} %pad_add_fusion.refs_0_, f32[16,24,384]{2,1,0:T(8,128)} %get-tuple-element.45.refs_1_, bf16[192,384]{1,0:T(8,128)(2,1)} %copy-done.8, bf16[192,384]{1,0:T(8,128)(2,1)} %copy-done.10, ...), custom_call_target="tpu_custom_call" | custom-call | tf_op jit(solution)/shard_map/step_2/pallas_call | solution.py:303
  148.7 2.2 %collective-permute-start.8 = (bf16[192,384]{1,0:T(8,128)(2,1)}, bf16[192,384]{1,0:T(8,128)(2,1)S(1)}, u32[]{:S(2)}, u32[]{:S(2)}) collective-permute-start(bf16[192,384]{1,0:T(8,128)(2,1)} %get-tuple-element.50), channel_id=1, source_target_pairs={{0,1},{1,2},{2,3},{3,4},{4,5},{5,6},{6,7},{7,8},{8,9},{9,10},{10,1... | collective-permute-start | bytes 442376 | tf_op jit(solution)/shard_map/ppermute | solution.py:356
  150.9 1.3 collective-permute-start.9
  152.2 19.9 %all_to_all.46 = f32[128,1,128]{2,1,0:T(1,128)} all-to-all(f32[128,1,128]{2,1,0:T(1,128)} %bitcast.26), channel_id=1, replica_groups=mesh['sec'=4,'lat'=32] {'sec','lat'}, dimensions={0} | all-to-all | bytes 131072 | tf_op jit(solution)/shard_map/all_to_all | solution.py:392
  172.8 20.0 %step_3.1 = (f32[16,24,384]{2,1,0:T(8,128)}, f32[128,128]{1,0:T(8,128)}, f32[16,16,384]{2,1,0:T(8,128)}) custom-call(s32[2]{0:T(128)} %pad_add_fusion.refs_0_, f32[16,24,384]{2,1,0:T(8,128)} %get-tuple-element.49.refs_1_, bf16[192,384]{1,0:T(8,128)(2,1)} %copy-done.5, bf16[192,384]{1,0:T(8,128)(2,1)} %copy-done.6, f32[128,128]{1,0:T(8,128)} %bitcast.20, ...), custom_call_target="tpu_custom_call" | custom-call | tf_op jit(solution)/shard_map/step_3/pallas_call | solution.py:303
  192.8 15.4 %all_to_all.47 = f32[128,1,128]{2,1,0:T(1,128)} all-to-all(f32[128,1,128]{2,1,0:T(1,128)} %bitcast.27), channel_id=1, replica_groups=mesh['sec'=4,'lat'=32] {'sec','lat'}, dimensions={0} | all-to-all | bytes 131072 | tf_op jit(solution)/shard_map/all_to_all | solution.py:392
  208.2 2.4 %finish.1 = (f32[24,16,256]{2,1,0:T(8,128)}, f32[16,16,256]{2,1,0:T(8,128)}) custom-call(f32[128,128]{1,0:T(8,128)} %bitcast.23, f32[16,24,384]{2,1,0:T(8,128)} %get-tuple-element.54.state_ref, f32[16,16,384]{2,1,0:T(8,128)} %get-tuple-element.55.raw_ref, f32[32,8,384]{2,1,0:T(8,128)} %get-tuple-element.43.refs_5_.wet_ref), custom_call_target="tpu_custom_call" | custom-call | tf_op jit(solution)/shard_map/finish/pallas_call | solution.py:341
  (35 shorter events, 4.4 us)
Async XLA Ops:
  0.6 17.7 %copy-start.4 = (bf16[5,128,120]{1,2,0:T(8,128)(2,1)S(1)}, bf16[5,128,120]{1,2,0:T(8,128)(2,1)}, u32[]{:S(2)}) copy-start(bf16[5,128,120]{1,2,0:T(8,128)(2,1)} %param.13) | copy-start | bytes 460804
  2.8 7.8 %collective-permute-start = (bf16[512,128]{1,0:T(8,128)(2,1)}, bf16[512,128]{1,0:T(8,128)(2,1)S(1)}, u32[]{:S(2)}, u32[]{:S(2)}) collective-permute-start(bf16[512,128]{1,0:T(8,128)(2,1)} %get-tuple-element.30), channel_id=1, source_target_pairs={{32,0},{64,32},{96,64},{33,1},{65,33},{97,65},{34,2},{66,34},{98,6... | collective-permute-start | bytes 393224 | tf_op jit(solution)/shard_map/ppermute | solution.py:356
  6.1 5.8 %collective-permute-start.1 = (bf16[512,128]{1,0:T(8,128)(2,1)}, bf16[512,128]{1,0:T(8,128)(2,1)S(1)}, u32[]{:S(2)}, u32[]{:S(2)}) collective-permute-start(bf16[512,128]{1,0:T(8,128)(2,1)} %get-tuple-element.31), channel_id=1, source_target_pairs={{0,32},{32,64},{64,96},{1,33},{33,65},{65,97},{2,34},{34,66},{66,9... | collective-permute-start | bytes 393224 | tf_op jit(solution)/shard_map/ppermute | solution.py:356
  10.5 14.2 %copy-start = (bf16[512,128]{1,0:T(8,128)(2,1)}, bf16[512,128]{1,0:T(8,128)(2,1)S(1)}, u32[]{:S(2)}) copy-start(bf16[512,128]{1,0:T(8,128)(2,1)S(1)} %collective-permute-done.refs_5_) | copy-start | bytes 393220
  11.9 12.9 %copy-start.1 = (bf16[512,128]{1,0:T(8,128)(2,1)}, bf16[512,128]{1,0:T(8,128)(2,1)S(1)}, u32[]{:S(2)}) copy-start(bf16[512,128]{1,0:T(8,128)(2,1)S(1)} %collective-permute-done.1.refs_4_) | copy-start | bytes 393220
  13.0 11.7 %collective-permute-start.3 = (bf16[256,384]{1,0:T(8,128)(2,1)S(1)}, bf16[256,384]{1,0:T(8,128)(2,1)S(1)}, u32[]{:S(2)}, u32[]{:S(2)}) collective-permute-start(bf16[256,384]{1,0:T(8,128)(2,1)S(1)} %get-tuple-element.56), channel_id=1, source_target_pairs={{1,0},{2,1},{3,2},{4,3},{5,4},{6,5},{7,6},{8,7},{9,8},{10,9},{11,1... | collective-permute-start | bytes 589832 | tf_op jit(solution)/shard_map/ppermute | solution.py:356
  14.3 10.4 %collective-permute-start.2 = (bf16[256,384]{1,0:T(8,128)(2,1)S(1)}, bf16[256,384]{1,0:T(8,128)(2,1)S(1)}, u32[]{:S(2)}, u32[]{:S(2)}) collective-permute-start(bf16[256,384]{1,0:T(8,128)(2,1)S(1)} %get-tuple-element.57), channel_id=1, source_target_pairs={{0,1},{1,2},{2,3},{3,4},{4,5},{5,6},{6,7},{7,8},{8,9},{9,10},{10,1... | collective-permute-start | bytes 589832 | tf_op jit(solution)/shard_map/ppermute | solution.py:356
  24.7 0.7 copy-start.2
  24.7 0.7 copy-start.3
  47.7 34.1 %collective-permute-start.4 = (bf16[192,384]{1,0:T(8,128)(2,1)}, bf16[192,384]{1,0:T(8,128)(2,1)S(1)}, u32[]{:S(2)}, u32[]{:S(2)}) collective-permute-start(bf16[192,384]{1,0:T(8,128)(2,1)} %get-tuple-element.40), channel_id=1, source_target_pairs={{0,1},{1,2},{2,3},{3,4},{4,5},{5,6},{6,7},{7,8},{8,9},{9,10},{10,1... | collective-permute-start | bytes 442376 | tf_op jit(solution)/shard_map/ppermute | solution.py:356
  50.9 30.9 %collective-permute-start.5 = (bf16[192,384]{1,0:T(8,128)(2,1)}, bf16[192,384]{1,0:T(8,128)(2,1)S(1)}, u32[]{:S(2)}, u32[]{:S(2)}) collective-permute-start(bf16[192,384]{1,0:T(8,128)(2,1)} %get-tuple-element.41), channel_id=1, source_target_pairs={{1,0},{2,1},{3,2},{4,3},{5,4},{6,5},{7,6},{8,7},{9,8},{10,9},{11,1... | collective-permute-start | bytes 442376 | tf_op jit(solution)/shard_map/ppermute | solution.py:356
  81.8 0.7 copy-start.7
  81.8 0.7 copy-start.9
  104.0 23.4 %collective-permute-start.6 = (bf16[192,384]{1,0:T(8,128)(2,1)}, bf16[192,384]{1,0:T(8,128)(2,1)S(1)}, u32[]{:S(2)}, u32[]{:S(2)}) collective-permute-start(bf16[192,384]{1,0:T(8,128)(2,1)} %get-tuple-element.46), channel_id=1, source_target_pairs={{0,1},{1,2},{2,3},{3,4},{4,5},{5,6},{6,7},{7,8},{8,9},{9,10},{10,1... | collective-permute-start | bytes 442376 | tf_op jit(solution)/shard_map/ppermute | solution.py:356
  106.1 21.3 %collective-permute-start.7 = (bf16[192,384]{1,0:T(8,128)(2,1)}, bf16[192,384]{1,0:T(8,128)(2,1)S(1)}, u32[]{:S(2)}, u32[]{:S(2)}) collective-permute-start(bf16[192,384]{1,0:T(8,128)(2,1)} %get-tuple-element.47), channel_id=1, source_target_pairs={{1,0},{2,1},{3,2},{4,3},{5,4},{6,5},{7,6},{8,7},{9,8},{10,9},{11,1... | collective-permute-start | bytes 442376 | tf_op jit(solution)/shard_map/ppermute | solution.py:356
  127.4 0.7 copy-start.8
  127.4 0.7 copy-start.10
  148.7 23.4 %collective-permute-start.8 = (bf16[192,384]{1,0:T(8,128)(2,1)}, bf16[192,384]{1,0:T(8,128)(2,1)S(1)}, u32[]{:S(2)}, u32[]{:S(2)}) collective-permute-start(bf16[192,384]{1,0:T(8,128)(2,1)} %get-tuple-element.50), channel_id=1, source_target_pairs={{0,1},{1,2},{2,3},{3,4},{4,5},{5,6},{6,7},{7,8},{8,9},{9,10},{10,1... | collective-permute-start | bytes 442376 | tf_op jit(solution)/shard_map/ppermute | solution.py:356
  150.9 21.2 %collective-permute-start.9 = (bf16[192,384]{1,0:T(8,128)(2,1)}, bf16[192,384]{1,0:T(8,128)(2,1)S(1)}, u32[]{:S(2)}, u32[]{:S(2)}) collective-permute-start(bf16[192,384]{1,0:T(8,128)(2,1)} %get-tuple-element.51), channel_id=1, source_target_pairs={{1,0},{2,1},{3,2},{4,3},{5,4},{6,5},{7,6},{8,7},{9,8},{10,9},{11,1... | collective-permute-start | bytes 442376 | tf_op jit(solution)/shard_map/ppermute | solution.py:356
  172.1 0.7 copy-start.5
  172.1 0.7 copy-start.6

commit v5 on v4

--- a/solution.py
+++ b/solution.py
@@ -73,6 +73,7 @@
         banded_kernel,
         out_shape=outs,
         scratch_shapes=[pltpu.VMEM((128, 640), F32), pltpu.VMEM((5, 640, 128), F32)],
+        compiler_params=pltpu.CompilerParams(vmem_limit_bytes=24 * 2**20),
         name="banded",
     )(*weights, *[bias[None] for bias in biases])
 
@@ -94,6 +95,7 @@
         prepare_kernel,
         out_shape=[jax.ShapeDtypeStruct((ROWS, 32, COLS), F32)]
         + [jax.ShapeDtypeStruct((ROWS * 32, 128), BF16)] * 2,
+        compiler_params=pltpu.CompilerParams(vmem_limit_bytes=24 * 2**20),
         name="prepare",
     )(ocean_state, land_mask, layer_count)
 
@@ -316,6 +318,7 @@
             pltpu.VMEM((2, span, 128), BF16),
             pltpu.VMEM((span, 512), F32),
         ],
+        compiler_params=pltpu.CompilerParams(vmem_limit_bytes=40 * 2**20),
         name=f"step_{step}",
     )(*args)
 
@@ -345,6 +348,7 @@
             jax.ShapeDtypeStruct((16, ROWS, COLS), F32),
         ],
         scratch_shapes=[pltpu.VMEM((ROWS, 16, COLS), F32)],
+        compiler_params=pltpu.CompilerParams(vmem_limit_bytes=24 * 2**20),
         name="finish",
     )(received, state, raw, wet)
 

time: 211 us -> 189 us (0.90)
  Pallas kernels: 93.7 us -> 73.1 us
    pallas_call x4, Pallas kernels: 84.3 us -> 69.6 us  [ocean_network_step(): pl.pallas_call(functools.partial(step_kernel, step=step), out_shape=outs,...]
    pallas_call x1, Pallas kernels: 4.9 us -> 2.16 us  [banded(): pl.pallas_call(banded_kernel, out_shape=outs, scratch_shapes=[pltpu.VMEM(...]
  transfers between devices with their start and end apart: 10 -> 10, of which waited for: 2 -> 3; matrix products, arithmetic and copies ran while one was open for 1% -> 0% of each run, Pallas kernels for 2% -> 1%
where the time goes in v5:
time: 189 us; the launch traced here: 188 us
  blocking collectives  83.9 us (44%)
  Pallas kernels  73.1 us (39%)
  starting transfers between devices  24.5 us (13%)
  waiting for transfers between devices  2.77 us (1%)
  local copies, waits for them, and re-layouts  2.71 us (1%)
    all_to_all x4, blocking collectives, local(): received = lax.all_to_all(results[1], ('sec', 'lat'), 0, 0)  83.9 us
    pallas_call x4, Pallas kernels, ocean_network_step(): pl.pallas_call(functools.partial(step_kernel, step=step), out_shape=outs,...  69.6 us
    ppermute x10, starting transfers between devices, both_ways(): return (lax.ppermute(up, axis, forward), lax.ppermute(down, axis, backward))  24.5 us
  transfers between devices with their start and end apart: 10, of which 3 were waited for; matrix products, arithmetic and copies ran while one was open for 0% of the time, Pallas kernels for 1%

profile of v5, /device:TPU:1, one launch (start us, length us, event | category | flops | bytes accessed | tf_op | source)
XLA Modules:
  0.0 188.0 jit_solution(14497530739742281485)
XLA Ops:
  0.7 1.0 copy-done.1
  1.7 0.7 copy-done.4
  3.4 3.4 %collective-permute-start = (bf16[512,128]{1,0:T(8,128)(2,1)S(1)}, bf16[512,128]{1,0:T(8,128)(2,1)S(1)}, u32[]{:S(2)}, u32[]{:S(2)}) collective-permute-start(bf16[512,128]{1,0:T(8,128)(2,1)S(1)} %get-tuple-element.30), channel_id=1, source_target_pairs={{32,0},{64,32},{96,64},{33,1},{65,33},{97,65},{34,2},{66,34},{98,6... | collective-permute-start | bytes 393224 | tf_op jit(solution)/shard_map/ppermute | solution.py:360
  6.8 3.6 %collective-permute-start.1 = (bf16[512,128]{1,0:T(8,128)(2,1)S(1)}, bf16[512,128]{1,0:T(8,128)(2,1)S(1)}, u32[]{:S(2)}, u32[]{:S(2)}) collective-permute-start(bf16[512,128]{1,0:T(8,128)(2,1)S(1)} %get-tuple-element.31), channel_id=1, source_target_pairs={{0,32},{32,64},{64,96},{1,33},{33,65},{65,97},{2,34},{34,66},{66,9... | collective-permute-start | bytes 393224 | tf_op jit(solution)/shard_map/ppermute | solution.py:360
  11.1 1.2 collective-permute-done.1.refs_4_
  12.4 1.3 collective-permute-start.3
  13.7 4.0 %collective-permute-start.2 = (bf16[256,384]{1,0:T(8,128)(2,1)S(1)}, bf16[256,384]{1,0:T(8,128)(2,1)S(1)}, u32[]{:S(2)}, u32[]{:S(2)}) collective-permute-start(bf16[256,384]{1,0:T(8,128)(2,1)S(1)} %get-tuple-element.57), channel_id=1, source_target_pairs={{0,1},{1,2},{2,3},{3,4},{4,5},{5,6},{6,7},{7,8},{8,9},{9,10},{10,1... | collective-permute-start | bytes 589832 | tf_op jit(solution)/shard_map/ppermute | solution.py:360
  18.0 2.2 %banded.1 = (bf16[1280,512]{1,0:T(8,128)(2,1)S(1)}, bf16[5120,256]{1,0:T(8,128)(2,1)S(1)}, bf16[2560,128]{1,0:T(8,128)(2,1)S(1)}, bf16[3200,256]{1,0:T(8,128)(2,...) custom-call(bf16[5,128,120]{2,1,0:T(8,128)(2,1)S(1)} %copy.13.refs_0_, ...), custom_call_target="tpu_custom_call" | custom-call | tf_op jit(solution)/shard_map/banded/pallas_call | solution.py:72
  20.2 0.8 collective-permute-done.2.refs_2_
  21.1 18.6 %step_0.1 = (f32[16,24,384]{2,1,0:T(8,128)S(1)}, f32[128,128]{1,0:T(8,128)S(1)}, f32[32,8,384]{2,1,0:T(8,128)S(1)}, f32[392,128]{1,0:T(8,128)S(1)}, bf16[192,384...) custom-call(s32[2]{0:T(128)S(1)} %pad_add_fusion.refs_0_, f32[16,32,256]{2,1,0:T(8,128)S(1)} %get-tuple-element.29.refs_1_, ...), custom_call_target="tpu_custom_call" | custom-call | tf_op jit(solution)/shard_map/step_0/pallas_call | solution.py:305
  39.7 3.8 %collective-permute-start.4 = (bf16[192,384]{1,0:T(8,128)(2,1)S(1)}, bf16[192,384]{1,0:T(8,128)(2,1)S(1)}, u32[]{:S(2)}, u32[]{:S(2)}) collective-permute-start(bf16[192,384]{1,0:T(8,128)(2,1)S(1)} %get-tuple-element.40), channel_id=1, source_target_pairs={{0,1},{1,2},{2,3},{3,4},{4,5},{5,6},{6,7},{7,8},{8,9},{9,10},{10,1... | collective-permute-start | bytes 442376 | tf_op jit(solution)/shard_map/ppermute | solution.py:360
  43.5 1.3 collective-permute-start.5
  44.8 31.5 %all_to_all.44 = f32[128,1,128]{2,1,0:T(1,128)S(1)} all-to-all(f32[128,1,128]{2,1,0:T(1,128)S(1)} %bitcast.24), channel_id=1, replica_groups=mesh['sec'=4,'lat'=32] {'sec','lat'}, dimensions={0} | all-to-all | bytes 131072 | tf_op jit(solution)/shard_map/all_to_all | solution.py:396
  76.3 17.8 %step_1.1 = (f32[16,24,384]{2,1,0:T(8,128)S(1)}, f32[128,128]{1,0:T(8,128)S(1)}, bf16[192,384]{1,0:T(8,128)(2,1)S(1)}, bf16[192,384]{1,0:T(8,128)(2,1)S(1)}) custom-call(s32[2]{0:T(128)S(1)} %pad_add_fusion.refs_0_, f32[16,24,384]{2,1,0:T(8,128)S(1)} %get-tuple-element.39.refs_1_, bf16[192,384]{1,0:T(8,128)(2,1)S(1)} %collective-permute-done.4.refs_2_, ...), custom_call_target="tpu_custom_call" | custom-call | tf_op jit(solution)/shard_map/step_1/pallas_call | solution.py:305
  94.2 2.3 %collective-permute-start.6 = (bf16[192,384]{1,0:T(8,128)(2,1)S(1)}, bf16[192,384]{1,0:T(8,128)(2,1)S(1)}, u32[]{:S(2)}, u32[]{:S(2)}) collective-permute-start(bf16[192,384]{1,0:T(8,128)(2,1)S(1)} %get-tuple-element.46), channel_id=1, source_target_pairs={{0,1},{1,2},{2,3},{3,4},{4,5},{5,6},{6,7},{7,8},{8,9},{9,10},{10,1... | collective-permute-start | bytes 442376 | tf_op jit(solution)/shard_map/ppermute | solution.py:360
  96.4 1.3 collective-permute-start.7
  97.7 19.2 %all_to_all.45 = f32[128,1,128]{2,1,0:T(1,128)S(1)} all-to-all(f32[128,1,128]{2,1,0:T(1,128)S(1)} %bitcast.25), channel_id=1, replica_groups=mesh['sec'=4,'lat'=32] {'sec','lat'}, dimensions={0} | all-to-all | bytes 131072 | tf_op jit(solution)/shard_map/all_to_all | solution.py:396
  117.0 17.0 %step_2.1 = (f32[16,24,384]{2,1,0:T(8,128)S(1)}, f32[128,128]{1,0:T(8,128)S(1)}, bf16[192,384]{1,0:T(8,128)(2,1)S(1)}, bf16[192,384]{1,0:T(8,128)(2,1)S(1)}) custom-call(s32[2]{0:T(128)S(1)} %pad_add_fusion.refs_0_, f32[16,24,384]{2,1,0:T(8,128)S(1)} %get-tuple-element.45.refs_1_, bf16[192,384]{1,0:T(8,128)(2,1)S(1)} %collective-permute-done.6.refs_2_, ...), custom_call_target="tpu_custom_call" | custom-call | tf_op jit(solution)/shard_map/step_2/pallas_call | solution.py:305
  134.0 2.3 %collective-permute-start.8 = (bf16[192,384]{1,0:T(8,128)(2,1)S(1)}, bf16[192,384]{1,0:T(8,128)(2,1)S(1)}, u32[]{:S(2)}, u32[]{:S(2)}) collective-permute-start(bf16[192,384]{1,0:T(8,128)(2,1)S(1)} %get-tuple-element.50), channel_id=1, source_target_pairs={{0,1},{1,2},{2,3},{3,4},{4,5},{5,6},{6,7},{7,8},{8,9},{9,10},{10,1... | collective-permute-start | bytes 442376 | tf_op jit(solution)/shard_map/ppermute | solution.py:360
  136.2 1.3 collective-permute-start.9
  137.5 19.2 %all_to_all.46 = f32[128,1,128]{2,1,0:T(1,128)S(1)} all-to-all(f32[128,1,128]{2,1,0:T(1,128)S(1)} %bitcast.26), channel_id=1, replica_groups=mesh['sec'=4,'lat'=32] {'sec','lat'}, dimensions={0} | all-to-all | bytes 131072 | tf_op jit(solution)/shard_map/all_to_all | solution.py:396
  156.8 16.2 %step_3.1 = (f32[16,24,384]{2,1,0:T(8,128)S(1)}, f32[128,128]{1,0:T(8,128)S(1)}, f32[16,16,384]{2,1,0:T(8,128)S(1)}) custom-call(s32[2]{0:T(128)S(1)} %pad_add_fusion.refs_0_, f32[16,24,384]{2,1,0:T(8,128)S(1)} %get-tuple-element.49.refs_1_, bf16[192,384]{1,0:T(8,128)(2,1)S(1)} %collective-permute-done.8.refs_2_, ...), custom_call_target="tpu_custom_call" | custom-call | tf_op jit(solution)/shard_map/step_3/pallas_call | solution.py:305
  173.0 13.9 %all_to_all.47 = f32[128,1,128]{2,1,0:T(1,128)S(1)} all-to-all(f32[128,1,128]{2,1,0:T(1,128)S(1)} %bitcast.27), channel_id=1, replica_groups=mesh['sec'=4,'lat'=32] {'sec','lat'}, dimensions={0} | all-to-all | bytes 131072 | tf_op jit(solution)/shard_map/all_to_all | solution.py:396
  186.9 1.1 finish.1
  (33 shorter events, 2.1 us)
Async XLA Ops:
  0.6 17.3 %copy-start = (bf16[5,64,640]{2,1,0:T(8,128)(2,1)S(1)}, bf16[5,64,640]{2,1,0:T(8,128)(2,1)}, u32[]{:S(2)}) copy-start(bf16[5,64,640]{2,1,0:T(8,128)(2,1)} %refs_1_.1) | copy-start | bytes 1228804
  0.6 1.0 copy-start.1
  1.7 0.7 copy-start.4
  2.4 0.7 copy-start.5
  3.1 14.6 %copy-start.9 = (bf16[5,128,120]{1,2,0:T(8,128)(2,1)S(1)}, bf16[5,128,120]{1,2,0:T(8,128)(2,1)}, u32[]{:S(2)}) copy-start(bf16[5,128,120]{1,2,0:T(8,128)(2,1)} %param.13) | copy-start | bytes 460804
  3.1 14.8 %copy-start.2 = (bf16[5,32,320]{2,1,0:T(8,128)(2,1)S(1)}, bf16[5,32,320]{2,1,0:T(8,128)(2,1)}, u32[]{:S(2)}) copy-start(bf16[5,32,320]{2,1,0:T(8,128)(2,1)} %refs_2_.1) | copy-start | bytes 307204
  3.1 14.8 %copy-start.3 = (bf16[5,16,160]{2,1,0:T(8,128)(2,1)S(1)}, bf16[5,16,160]{2,1,0:T(8,128)(2,1)}, u32[]{:S(2)}) copy-start(bf16[5,16,160]{2,1,0:T(8,128)(2,1)} %refs_3_.1) | copy-start | bytes 76804
  3.1 14.8 %copy-start.6 = (f32[128]{0:T(128)S(1)}, f32[128]{0:T(128)}, u32[]{:S(2)}) copy-start(f32[128]{0:T(128)} %param.14) | copy-start | bytes 1540
  3.1 14.8 %copy-start.7 = (f32[64]{0:T(128)S(1)}, f32[64]{0:T(128)}, u32[]{:S(2)}) copy-start(f32[64]{0:T(128)} %param.16) | copy-start | bytes 772
  3.1 14.8 %copy-start.8 = (f32[32]{0:T(128)S(1)}, f32[32]{0:T(128)}, u32[]{:S(2)}) copy-start(f32[32]{0:T(128)} %param.18) | copy-start | bytes 388
  3.4 7.7 %collective-permute-start = (bf16[512,128]{1,0:T(8,128)(2,1)S(1)}, bf16[512,128]{1,0:T(8,128)(2,1)S(1)}, u32[]{:S(2)}, u32[]{:S(2)}) collective-permute-start(bf16[512,128]{1,0:T(8,128)(2,1)S(1)} %get-tuple-element.30), channel_id=1, source_target_pairs={{32,0},{64,32},{96,64},{33,1},{65,33},{97,65},{34,2},{66,34},{98,6... | collective-permute-start | bytes 393224 | tf_op jit(solution)/shard_map/ppermute | solution.py:360
  6.8 5.5 %collective-permute-start.1 = (bf16[512,128]{1,0:T(8,128)(2,1)S(1)}, bf16[512,128]{1,0:T(8,128)(2,1)S(1)}, u32[]{:S(2)}, u32[]{:S(2)}) collective-permute-start(bf16[512,128]{1,0:T(8,128)(2,1)S(1)} %get-tuple-element.31), channel_id=1, source_target_pairs={{0,32},{32,64},{64,96},{1,33},{33,65},{65,97},{2,34},{34,66},{66,9... | collective-permute-start | bytes 393224 | tf_op jit(solution)/shard_map/ppermute | solution.py:360
  12.4 7.8 %collective-permute-start.3 = (bf16[256,384]{1,0:T(8,128)(2,1)S(1)}, bf16[256,384]{1,0:T(8,128)(2,1)S(1)}, u32[]{:S(2)}, u32[]{:S(2)}) collective-permute-start(bf16[256,384]{1,0:T(8,128)(2,1)S(1)} %get-tuple-element.56), channel_id=1, source_target_pairs={{1,0},{2,1},{3,2},{4,3},{5,4},{6,5},{7,6},{8,7},{9,8},{10,9},{11,1... | collective-permute-start | bytes 589832 | tf_op jit(solution)/shard_map/ppermute | solution.py:360
  13.7 7.3 %collective-permute-start.2 = (bf16[256,384]{1,0:T(8,128)(2,1)S(1)}, bf16[256,384]{1,0:T(8,128)(2,1)S(1)}, u32[]{:S(2)}, u32[]{:S(2)}) collective-permute-start(bf16[256,384]{1,0:T(8,128)(2,1)S(1)} %get-tuple-element.57), channel_id=1, source_target_pairs={{0,1},{1,2},{2,3},{3,4},{4,5},{5,6},{6,7},{7,8},{8,9},{9,10},{10,1... | collective-permute-start | bytes 589832 | tf_op jit(solution)/shard_map/ppermute | solution.py:360
  39.7 36.7 %collective-permute-start.4 = (bf16[192,384]{1,0:T(8,128)(2,1)S(1)}, bf16[192,384]{1,0:T(8,128)(2,1)S(1)}, u32[]{:S(2)}, u32[]{:S(2)}) collective-permute-start(bf16[192,384]{1,0:T(8,128)(2,1)S(1)} %get-tuple-element.40), channel_id=1, source_target_pairs={{0,1},{1,2},{2,3},{3,4},{4,5},{5,6},{6,7},{7,8},{8,9},{9,10},{10,1... | collective-permute-start | bytes 442376 | tf_op jit(solution)/shard_map/ppermute | solution.py:360
  43.5 32.9 %collective-permute-start.5 = (bf16[192,384]{1,0:T(8,128)(2,1)S(1)}, bf16[192,384]{1,0:T(8,128)(2,1)S(1)}, u32[]{:S(2)}, u32[]{:S(2)}) collective-permute-start(bf16[192,384]{1,0:T(8,128)(2,1)S(1)} %get-tuple-element.41), channel_id=1, source_target_pairs={{1,0},{2,1},{3,2},{4,3},{5,4},{6,5},{7,6},{8,7},{9,8},{10,9},{11,1... | collective-permute-start | bytes 442376 | tf_op jit(solution)/shard_map/ppermute | solution.py:360
  94.2 22.8 %collective-permute-start.6 = (bf16[192,384]{1,0:T(8,128)(2,1)S(1)}, bf16[192,384]{1,0:T(8,128)(2,1)S(1)}, u32[]{:S(2)}, u32[]{:S(2)}) collective-permute-start(bf16[192,384]{1,0:T(8,128)(2,1)S(1)} %get-tuple-element.46), channel_id=1, source_target_pairs={{0,1},{1,2},{2,3},{3,4},{4,5},{5,6},{6,7},{7,8},{8,9},{9,10},{10,1... | collective-permute-start | bytes 442376 | tf_op jit(solution)/shard_map/ppermute | solution.py:360
  96.4 20.5 %collective-permute-start.7 = (bf16[192,384]{1,0:T(8,128)(2,1)S(1)}, bf16[192,384]{1,0:T(8,128)(2,1)S(1)}, u32[]{:S(2)}, u32[]{:S(2)}) collective-permute-start(bf16[192,384]{1,0:T(8,128)(2,1)S(1)} %get-tuple-element.47), channel_id=1, source_target_pairs={{1,0},{2,1},{3,2},{4,3},{5,4},{6,5},{7,6},{8,7},{9,8},{10,9},{11,1... | collective-permute-start | bytes 442376 | tf_op jit(solution)/shard_map/ppermute | solution.py:360
  134.0 22.8 %collective-permute-start.8 = (bf16[192,384]{1,0:T(8,128)(2,1)S(1)}, bf16[192,384]{1,0:T(8,128)(2,1)S(1)}, u32[]{:S(2)}, u32[]{:S(2)}) collective-permute-start(bf16[192,384]{1,0:T(8,128)(2,1)S(1)} %get-tuple-element.50), channel_id=1, source_target_pairs={{0,1},{1,2},{2,3},{3,4},{4,5},{5,6},{6,7},{7,8},{8,9},{9,10},{10,1... | collective-permute-start | bytes 442376 | tf_op jit(solution)/shard_map/ppermute | solution.py:360
  136.2 20.5 %collective-permute-start.9 = (bf16[192,384]{1,0:T(8,128)(2,1)S(1)}, bf16[192,384]{1,0:T(8,128)(2,1)S(1)}, u32[]{:S(2)}, u32[]{:S(2)}) collective-permute-start(bf16[192,384]{1,0:T(8,128)(2,1)S(1)} %get-tuple-element.51), channel_id=1, source_target_pairs={{1,0},{2,1},{3,2},{4,3},{5,4},{6,5},{7,6},{8,7},{9,8},{10,9},{11,1... | collective-permute-start | bytes 442376 | tf_op jit(solution)/shard_map/ppermute | solution.py:360

commit v6 on v5

--- a/solution.py
+++ b/solution.py
@@ -78,6 +78,51 @@
     )(*weights, *[bias[None] for bias in biases])
 
 
+def lanes_between(shape, low, high):
+    lane = lax.broadcasted_iota(jnp.int32, shape, 1)
+    return (lane >= low) & (lane < high)
+
+
+def fold_edge(tile, low):
+    height = tile.shape[0] // 4
+    folded = tile[0:height]
+    for part in range(1, 4):
+        moved = pltpu.roll(tile[part * height : (part + 1) * height], 32 * part, 1)
+        begin = (low + 32 * part) % 128
+        folded = jnp.where(lanes_between(moved.shape, begin, begin + 32), moved, folded)
+    return folded
+
+
+def unfold_edge(folded):
+    parts = [folded] + [pltpu.roll(folded, 128 - 32 * part, 1) for part in range(1, 4)]
+    return jnp.concatenate(parts, axis=0)
+
+
+def fold_sides(sides):
+    height = sides.shape[0] // 2
+    moved = pltpu.roll(sides[height:], 64, 1)
+    both = jnp.where(lanes_between(moved.shape, 32, 96), moved, sides[:height])
+    return jnp.concatenate([both[: height // 2], both[height // 2 :]], axis=1)
+
+
+def unfold_sides(folded):
+    both = jnp.concatenate([folded[:, 0:128], folded[:, 128:256]], axis=0)
+    return jnp.concatenate([both, pltpu.roll(both, 64, 1)], axis=0)
+
+
+def pack_rows(flat):
+    return jnp.concatenate([flat[:, 0:COLS], fold_sides(flat[:, COLS:])], axis=0)
+
+
+def unpack_rows(packed, state_ref, low):
+    height = HALO * 24
+    fields = packed[0 : height + height // 4].astype(F32)
+    state_ref[low : low + HALO, 0:24, 0:COLS] = fields[0:height].reshape(HALO, 24, COLS)
+    state_ref[low : low + HALO, 0:24, COLS:WIDE] = unfold_sides(fields[height:]).reshape(
+        HALO, 24, 128
+    )
+
+
 def prepare_kernel(state_ref, land_ref, count_ref, own_ref, left_ref, right_ref):
     levels = land_ref[...] * count_ref[...]
     own_ref[:, 24:32, :] = jnp.zeros((ROWS, 8, COLS), F32)
@@ -85,19 +130,48 @@
     for channel in range(24):
         wet = jnp.where(levels > channel % LEVELS, 1.0, 0.0)
         own_ref[:, channel, :] = state_ref[channel] * wet
-    flat = own_ref[...].reshape(ROWS * 32, COLS).astype(BF16)
-    left_ref[...] = flat[:, 0:128]
-    right_ref[...] = flat[:, COLS - 128 :]
+    flat = own_ref[...].reshape(ROWS * 32, COLS)
+    left_ref[...] = fold_edge(flat[:, 0:128], 0).astype(BF16)
+    right_ref[...] = fold_edge(flat[:, COLS - 128 :], 96).astype(BF16)
+
+
+def small_params():
+    return pltpu.CompilerParams(vmem_limit_bytes=24 * 2**20)
 
 
 def prepare(ocean_state, land_mask, layer_count):
     return pl.pallas_call(
         prepare_kernel,
         out_shape=[jax.ShapeDtypeStruct((ROWS, 32, COLS), F32)]
-        + [jax.ShapeDtypeStruct((ROWS * 32, 128), BF16)] * 2,
-        compiler_params=pltpu.CompilerParams(vmem_limit_bytes=24 * 2**20),
+        + [jax.ShapeDtypeStruct((ROWS * 8, 128), BF16)] * 2,
+        compiler_params=small_params(),
         name="prepare",
     )(ocean_state, land_mask, layer_count)
+
+
+def pack_kernel(own_ref, left_ref, right_ref, wide_ref, up_ref, down_ref):
+    right = unfold_edge(right_ref[...].astype(F32))
+    left = unfold_edge(left_ref[...].astype(F32))
+    sides = jnp.where(lanes_between(left.shape, 0, SIDE), right, left)
+    wide_ref[:, :, 0:COLS] = own_ref[...]
+    wide_ref[:, :, COLS:WIDE] = sides.reshape(ROWS, 32, 128)
+    for low, out_ref in ((0, down_ref), (ROWS - HALO, up_ref)):
+        fields = wide_ref[low : low + HALO, 0:24, :].reshape(HALO * 24, WIDE)
+        levels = wide_ref[low : low + HALO, 24, :]
+        rest = jnp.concatenate([levels[:, COLS:], jnp.zeros((HALO, 128), F32)], axis=1)
+        out_ref[...] = jnp.concatenate(
+            [pack_rows(fields), levels[:, 0:COLS], rest], axis=0
+        ).astype(BF16)
+
+
+def pack(own, left, right):
+    return pl.pallas_call(
+        pack_kernel,
+        out_shape=[jax.ShapeDtypeStruct((ROWS, 32, WIDE), F32)]
+        + [jax.ShapeDtypeStruct((HALO * 32, COLS), BF16)] * 2,
+        compiler_params=small_params(),
+        name="pack",
+    )(own, left, right)
 
 
 def spread(value, work_ref, out_ref, group, zero):
@@ -153,10 +227,7 @@
     start_ref = refs.pop(0)
     own_ref, top_ref, bottom_ref = refs[:3]
     refs = refs[3:]
-    if first:
-        left_ref, right_ref = refs[:2]
-        refs = refs[2:]
-    else:
+    if not first:
         recv_ref, wet_ref, sea_turned_ref = refs[:3]
         refs = refs[3:]
     w1_ref, w2_ref, w3_ref, w4_ref, b1_ref, b2_ref, b3_ref, new_ref, pay_ref = refs[:9]
@@ -169,16 +240,19 @@
     else:
         send_up_ref, send_down_ref = refs[:2]
         refs = refs[2:]
-    state_ref, a0_ref, a1_ref, a2_ref, a3_ref, work_ref, raw_ref, sea_ref, sum_ref = refs
+    state_ref, a0_ref, a1_ref, a2_ref, a3_ref, work_ref, raw_ref, sea_ref, sum_ref = refs[:9]
+    turn_ref = refs[9]
     zero = start_ref[1]
 
+    halves = ((top_ref, 0), (bottom_ref, HALO + ROWS))
+    for packed_ref, low in halves:
+        unpack_rows(packed_ref[...], state_ref, low)
     if first:
-        lane = lax.broadcasted_iota(jnp.int32, (ROWS * 32, 128), 1)
-        sides = jnp.where(lane < SIDE, right_ref[...].astype(F32), left_ref[...].astype(F32))
-        state_ref[HALO : HALO + ROWS, :, 0:COLS] = own_ref[...]
-        state_ref[HALO : HALO + ROWS, :, COLS:WIDE] = sides.reshape(ROWS, 32, 128)
-        state_ref[0:HALO] = top_ref[...].astype(F32).reshape(HALO, 32, WIDE)
-        state_ref[HALO + ROWS :] = bottom_ref[...].astype(F32).reshape(HALO, 32, WIDE)
+        state_ref[HALO : HALO + ROWS] = own_ref[...]
+        for packed_ref, low in halves:
+            levels = packed_ref[HALO * 30 :, :].astype(F32)
+            state_ref[low : low + HALO, 24, 0:COLS] = levels[0:HALO]
+            state_ref[low : low + HALO, 24, COLS:WIDE] = levels[HALO:, 0:128]
         levels = jnp.broadcast_to(state_ref[:, 24:25, :], (EXT_ROWS, 8, WIDE))
         level_of = lax.broadcasted_iota(jnp.int32, levels.shape, 1).astype(F32)
         wet_ref[...] = jnp.where(level_of < levels, 1.0, 0.0)
@@ -191,8 +265,6 @@
         sea_turned_ref[WIDE:, :] = jnp.zeros((8, 128), F32)
     else:
         state_ref[HALO : HALO + ROWS, 0:24, :] = own_ref[...]
-        state_ref[0:HALO, 0:24, :] = top_ref[...].astype(F32).reshape(HALO, 24, WIDE)
-        state_ref[HALO + ROWS :, 0:24, :] = bottom_ref[...].astype(F32).reshape(HALO, 24, WIDE)
         zonal_mean, merid_mean = device_means(recv_ref[...])
         for base, mean in ((0, zonal_mean), (8, merid_mean)):
             scaled = jnp.concatenate([TIME_STEP * mean] * 3, axis=1)
@@ -206,11 +278,16 @@
         sea_ref[layer - 1] = sea_turned_ref[begin : begin + span, :].astype(BF16)
 
     work_ref[:, span:, :] = jnp.zeros((4, 8, 128), F32)
-    for group in range(8):
+    turn_ref[:, span:, :] = jnp.zeros((1, 8, 128), F32)
+
+    def turn(group):
         flat = state_ref[4 * group : 4 * group + 4].reshape(128, WIDE)
         turned = jnp.transpose(flat)
         around = jnp.concatenate([turned[WIDE - margin :], turned[0 : COLS + margin]], axis=0)
-        spread(around, work_ref, a0_ref, group, zero)
+        spread(around, turn_ref, a0_ref, group, zero)
+
+    for group in range(8):
+        turn(group)
     for layer, refs in enumerate(
         (
             (a0_ref, w1_ref, b1_ref, a1_ref),
@@ -266,9 +343,9 @@
     if last:
         raw_out_ref[...] = raw_ref[...]
     else:
-        flat = new_ref[...].reshape(ROWS * 24, WIDE).astype(BF16)
-        send_down_ref[...] = flat[0 : HALO * 24]
-        send_up_ref[...] = flat[(ROWS - HALO) * 24 :]
+        flat = new_ref[...].reshape(ROWS * 24, WIDE)
+        send_down_ref[...] = pack_rows(flat[0 : HALO * 24]).astype(BF16)
+        send_up_ref[...] = pack_rows(flat[(ROWS - HALO) * 24 :]).astype(BF16)
 
     def lanes_of(field):
         by_column = jnp.sum(field, axis=0)
@@ -300,7 +377,7 @@
     if last:
         outs.append(jax.ShapeDtypeStruct((ROWS, 16, WIDE), F32))
     else:
-        outs += [jax.ShapeDtypeStruct((HALO * 24, WIDE), BF16)] * 2
+        outs += [jax.ShapeDtypeStruct((HALO * 30, COLS), BF16)] * 2
     vmem = pl.BlockSpec(memory_space=pltpu.VMEM)
     return pl.pallas_call(
         functools.partial(step_kernel, step=step),
@@ -317,6 +394,7 @@
             pltpu.VMEM((ROWS, 16, WIDE), F32),
             pltpu.VMEM((2, span, 128), BF16),
             pltpu.VMEM((span, 512), F32),
+            pltpu.VMEM((1, span + 8, 128), F32),
         ],
         compiler_params=pltpu.CompilerParams(vmem_limit_bytes=40 * 2**20),
         name=f"step_{step}",
@@ -378,14 +456,12 @@
         [conv1_weight, conv2_weight, conv3_weight, conv4_weight],
         [conv1_bias, conv2_bias, conv3_bias],
     )
-    lane = lax.broadcasted_iota(jnp.int32, left.shape, 1)
-    sides = jnp.where(lane < SIDE, right, left)
-    whole = jnp.concatenate([send_left, send_right, sides], axis=1)
-    halos = both_ways("lat", whole[HALO * 32 :], whole[: HALO * 32])
+    state, send_up, send_down = pack(state, left, right)
+    halos = both_ways("lat", send_up, send_down)
 
     start = (lax.axis_index("lat") * ROWS).astype(jnp.int32)
     start = jnp.stack([start, jnp.zeros((), jnp.int32)])
-    extras = [left, right]
+    extras = []
     for step in range(STEPS):
         results = ocean_network_step(step, [start, state, *halos, *extras, *weights])
         state = results[0]

time: 189 us -> 187 us (0.989)
  blocking collectives: 83.9 us -> 76.8 us
  local copies, waits for them, and re-layouts: 2.71 us -> 8.14 us
    all_to_all x4, blocking collectives: 83.9 us -> 76.8 us  [local(): received = lax.all_to_all(results[1], ('sec', 'lat'), 0, 0)]
    unnamed x21 -> x19, local copies, waits for them, and re-layouts: 2.67 us -> 8.14 us
  transfers between devices with their start and end apart: 10 -> 10, of which waited for: 3 -> 1; matrix products, arithmetic and copies ran while one was open for 0% -> 1% of each run, Pallas kernels for 1% -> 1%
where the time goes in v6:
time: 187 us; the launch traced here: 186 us
  blocking collectives  76.8 us (41%)
  Pallas kernels  73.5 us (39%)
  starting transfers between devices  23.7 us (13%)
  local copies, waits for them, and re-layouts  8.14 us (4%)
  waiting for transfers between devices  3.32 us (2%)
    all_to_all x4, blocking collectives, local(): received = lax.all_to_all(results[1], ('sec', 'lat'), 0, 0)  76.8 us
    pallas_call x4, Pallas kernels, ocean_network_step(): pl.pallas_call(functools.partial(step_kernel, step=step), out_shape=outs,...  69.8 us
    ppermute x10, starting transfers between devices, both_ways(): return (lax.ppermute(up, axis, forward), lax.ppermute(down, axis, backward))  23.7 us
    unnamed x19, local copies, waits for them, and re-layouts  8.14 us
  transfers between devices with their start and end apart: 10, of which 1 were waited for; matrix products, arithmetic and copies ran while one was open for 1% of the time, Pallas kernels for 1%

profile of v6, /device:TPU:1, one launch (start us, length us, event | category | flops | bytes accessed | tf_op | source)
XLA Modules:
  0.0 186.3 jit_solution(17517870021343823918)
XLA Ops:
  0.6 1.0 copy-done.1
  3.3 4.9 %collective-permute-start = (bf16[128,128]{1,0:T(8,128)(2,1)S(1)}, bf16[128,128]{1,0:T(8,128)(2,1)S(1)}, u32[]{:S(2)}, u32[]{:S(2)}) collective-permute-start(bf16[128,128]{1,0:T(8,128)(2,1)S(1)} %get-tuple-element.33), channel_id=1, source_target_pairs={{0,32},{32,64},{64,96},{1,33},{33,65},{65,97},{2,34},{34,66},{66,9... | collective-permute-start | bytes 98312 | tf_op jit(solution)/shard_map/ppermute | solution.py:438
  8.3 1.9 %collective-permute-start.1 = (bf16[128,128]{1,0:T(8,128)(2,1)S(1)}, bf16[128,128]{1,0:T(8,128)(2,1)S(1)}, u32[]{:S(2)}, u32[]{:S(2)}) collective-permute-start(bf16[128,128]{1,0:T(8,128)(2,1)S(1)} %get-tuple-element.34), channel_id=1, source_target_pairs={{32,0},{64,32},{96,64},{33,1},{65,33},{97,65},{34,2},{66,34},{98,6... | collective-permute-start | bytes 98312 | tf_op jit(solution)/shard_map/ppermute | solution.py:438
  10.2 3.3 %collective-permute-done.1.right_ref = bf16[128,128]{1,0:T(8,128)(2,1)S(1)} collective-permute-done((bf16[128,128]{1,0:T(8,128)(2,1)S(1)}, bf16[128,128]{1,0:T(8,128)(2,1)S(1)}, u32[]{:S(2)}, u32[]{:S(2)}) %collective-permute-start.1) | collective-permute-done | bytes 32800 | tf_op jit(solution)/shard_map/ppermute | solution.py:438
  13.7 3.2 %collective-permute-start.2 = (bf16[256,256]{1,0:T(8,128)(2,1)S(1)}, bf16[256,256]{1,0:T(8,128)(2,1)S(1)}, u32[]{:S(2)}, u32[]{:S(2)}) collective-permute-start(bf16[256,256]{1,0:T(8,128)(2,1)S(1)} %get-tuple-element.36), channel_id=1, source_target_pairs={{0,1},{1,2},{2,3},{3,4},{4,5},{5,6},{6,7},{7,8},{8,9},{9,10},{10,1... | collective-permute-start | bytes 393224 | tf_op jit(solution)/shard_map/ppermute | solution.py:438
  16.9 1.3 collective-permute-start.3
  18.2 1.1 copy.13.refs_0_
  19.3 1.0 copy-done
  23.9 2.2 %banded.1 = (bf16[1280,512]{1,0:T(8,128)(2,1)S(1)}, bf16[5120,256]{1,0:T(8,128)(2,1)S(1)}, bf16[2560,128]{1,0:T(8,128)(2,1)S(1)}, bf16[3200,256]{1,0:T(8,128)(2,...) custom-call(bf16[5,128,120]{2,1,0:T(8,128)(2,1)S(1)} %copy.13.refs_0_, ...), custom_call_target="tpu_custom_call" | custom-call | tf_op jit(solution)/shard_map/banded/pallas_call | solution.py:72
  26.2 18.5 %step_0.1 = (f32[16,24,384]{2,1,0:T(8,128)S(1)}, f32[128,128]{1,0:T(8,128)S(1)}, f32[32,8,384]{2,1,0:T(8,128)S(1)}, f32[392,128]{1,0:T(8,128)S(1)}, bf16[240,256...) custom-call(s32[2]{0:T(128)S(1)} %pad_add_fusion.refs_0_, f32[16,32,384]{2,1,0:T(8,128)S(1)} %get-tuple-element.35.refs_1_, ...), custom_call_target="tpu_custom_call" | custom-call | tf_op jit(solution)/shard_map/step_0/pallas_call | solution.py:382
  44.7 4.0 %collective-permute-start.4 = (bf16[240,256]{1,0:T(8,128)(2,1)S(1)}, bf16[240,256]{1,0:T(8,128)(2,1)S(1)}, u32[]{:S(2)}, u32[]{:S(2)}) collective-permute-start(bf16[240,256]{1,0:T(8,128)(2,1)S(1)} %get-tuple-element.46), channel_id=1, source_target_pairs={{0,1},{1,2},{2,3},{3,4},{4,5},{5,6},{6,7},{7,8},{8,9},{9,10},{10,1... | collective-permute-start | bytes 368648 | tf_op jit(solution)/shard_map/ppermute | solution.py:438
  48.7 1.3 collective-permute-start.5
  50.0 24.4 %all_to_all.44 = f32[128,1,128]{2,1,0:T(1,128)S(1)} all-to-all(f32[128,1,128]{2,1,0:T(1,128)S(1)} %bitcast.24), channel_id=1, replica_groups=mesh['sec'=4,'lat'=32] {'sec','lat'}, dimensions={0} | all-to-all | bytes 131072 | tf_op jit(solution)/shard_map/all_to_all | solution.py:472
  74.4 17.8 %step_1.1 = (f32[16,24,384]{2,1,0:T(8,128)S(1)}, f32[128,128]{1,0:T(8,128)S(1)}, bf16[240,256]{1,0:T(8,128)(2,1)S(1)}, bf16[240,256]{1,0:T(8,128)(2,1)S(1)}) custom-call(s32[2]{0:T(128)S(1)} %pad_add_fusion.refs_0_, f32[16,24,384]{2,1,0:T(8,128)S(1)} %get-tuple-element.45.refs_1_, bf16[240,256]{1,0:T(8,128)(2,1)S(1)} %collective-permute-done.4.refs_2_, ...), custom_call_target="tpu_custom_call" | custom-call | tf_op jit(solution)/shard_map/step_1/pallas_call | solution.py:382
  92.3 2.3 %collective-permute-start.6 = (bf16[240,256]{1,0:T(8,128)(2,1)S(1)}, bf16[240,256]{1,0:T(8,128)(2,1)S(1)}, u32[]{:S(2)}, u32[]{:S(2)}) collective-permute-start(bf16[240,256]{1,0:T(8,128)(2,1)S(1)} %get-tuple-element.52), channel_id=1, source_target_pairs={{0,1},{1,2},{2,3},{3,4},{4,5},{5,6},{6,7},{7,8},{8,9},{9,10},{10,1... | collective-permute-start | bytes 368648 | tf_op jit(solution)/shard_map/ppermute | solution.py:438
  94.5 1.3 collective-permute-start.7
  95.8 19.2 %all_to_all.45 = f32[128,1,128]{2,1,0:T(1,128)S(1)} all-to-all(f32[128,1,128]{2,1,0:T(1,128)S(1)} %bitcast.25), channel_id=1, replica_groups=mesh['sec'=4,'lat'=32] {'sec','lat'}, dimensions={0} | all-to-all | bytes 131072 | tf_op jit(solution)/shard_map/all_to_all | solution.py:472
  115.1 17.1 %step_2.1 = (f32[16,24,384]{2,1,0:T(8,128)S(1)}, f32[128,128]{1,0:T(8,128)S(1)}, bf16[240,256]{1,0:T(8,128)(2,1)S(1)}, bf16[240,256]{1,0:T(8,128)(2,1)S(1)}) custom-call(s32[2]{0:T(128)S(1)} %pad_add_fusion.refs_0_, f32[16,24,384]{2,1,0:T(8,128)S(1)} %get-tuple-element.51.refs_1_, bf16[240,256]{1,0:T(8,128)(2,1)S(1)} %collective-permute-done.6.refs_2_, ...), custom_call_target="tpu_custom_call" | custom-call | tf_op jit(solution)/shard_map/step_2/pallas_call | solution.py:382
  132.2 2.2 %collective-permute-start.8 = (bf16[240,256]{1,0:T(8,128)(2,1)S(1)}, bf16[240,256]{1,0:T(8,128)(2,1)S(1)}, u32[]{:S(2)}, u32[]{:S(2)}) collective-permute-start(bf16[240,256]{1,0:T(8,128)(2,1)S(1)} %get-tuple-element.56), channel_id=1, source_target_pairs={{0,1},{1,2},{2,3},{3,4},{4,5},{5,6},{6,7},{7,8},{8,9},{9,10},{10,1... | collective-permute-start | bytes 368648 | tf_op jit(solution)/shard_map/ppermute | solution.py:438
  134.4 1.3 collective-permute-start.9
  135.7 19.3 %all_to_all.46 = f32[128,1,128]{2,1,0:T(1,128)S(1)} all-to-all(f32[128,1,128]{2,1,0:T(1,128)S(1)} %bitcast.26), channel_id=1, replica_groups=mesh['sec'=4,'lat'=32] {'sec','lat'}, dimensions={0} | all-to-all | bytes 131072 | tf_op jit(solution)/shard_map/all_to_all | solution.py:472
  155.0 16.3 %step_3.1 = (f32[16,24,384]{2,1,0:T(8,128)S(1)}, f32[128,128]{1,0:T(8,128)S(1)}, f32[16,16,384]{2,1,0:T(8,128)S(1)}) custom-call(s32[2]{0:T(128)S(1)} %pad_add_fusion.refs_0_, f32[16,24,384]{2,1,0:T(8,128)S(1)} %get-tuple-element.55.refs_1_, bf16[240,256]{1,0:T(8,128)(2,1)S(1)} %collective-permute-done.8.refs_2_, ...), custom_call_target="tpu_custom_call" | custom-call | tf_op jit(solution)/shard_map/step_3/pallas_call | solution.py:382
  171.3 13.9 %all_to_all.47 = f32[128,1,128]{2,1,0:T(1,128)S(1)} all-to-all(f32[128,1,128]{2,1,0:T(1,128)S(1)} %bitcast.27), channel_id=1, replica_groups=mesh['sec'=4,'lat'=32] {'sec','lat'}, dimensions={0} | all-to-all | bytes 131072 | tf_op jit(solution)/shard_map/all_to_all | solution.py:472
  185.2 1.1 finish.1
  (28 shorter events, 5.6 us)
Async XLA Ops:
  0.6 1.0 copy-start.1
  1.6 0.7 copy-start.4
  2.3 0.7 copy-start.5
  3.3 6.9 %collective-permute-start = (bf16[128,128]{1,0:T(8,128)(2,1)S(1)}, bf16[128,128]{1,0:T(8,128)(2,1)S(1)}, u32[]{:S(2)}, u32[]{:S(2)}) collective-permute-start(bf16[128,128]{1,0:T(8,128)(2,1)S(1)} %get-tuple-element.33), channel_id=1, source_target_pairs={{0,32},{32,64},{64,96},{1,33},{33,65},{65,97},{2,34},{34,66},{66,9... | collective-permute-start | bytes 98312 | tf_op jit(solution)/shard_map/ppermute | solution.py:438
  8.3 5.2 %collective-permute-start.1 = (bf16[128,128]{1,0:T(8,128)(2,1)S(1)}, bf16[128,128]{1,0:T(8,128)(2,1)S(1)}, u32[]{:S(2)}, u32[]{:S(2)}) collective-permute-start(bf16[128,128]{1,0:T(8,128)(2,1)S(1)} %get-tuple-element.34), channel_id=1, source_target_pairs={{32,0},{64,32},{96,64},{33,1},{65,33},{97,65},{34,2},{66,34},{98,6... | collective-permute-start | bytes 98312 | tf_op jit(solution)/shard_map/ppermute | solution.py:438
  13.7 12.5 %collective-permute-start.2 = (bf16[256,256]{1,0:T(8,128)(2,1)S(1)}, bf16[256,256]{1,0:T(8,128)(2,1)S(1)}, u32[]{:S(2)}, u32[]{:S(2)}) collective-permute-start(bf16[256,256]{1,0:T(8,128)(2,1)S(1)} %get-tuple-element.36), channel_id=1, source_target_pairs={{0,1},{1,2},{2,3},{3,4},{4,5},{5,6},{6,7},{7,8},{8,9},{9,10},{10,1... | collective-permute-start | bytes 393224 | tf_op jit(solution)/shard_map/ppermute | solution.py:438
  16.9 9.3 %collective-permute-start.3 = (bf16[256,256]{1,0:T(8,128)(2,1)S(1)}, bf16[256,256]{1,0:T(8,128)(2,1)S(1)}, u32[]{:S(2)}, u32[]{:S(2)}) collective-permute-start(bf16[256,256]{1,0:T(8,128)(2,1)S(1)} %get-tuple-element.37), channel_id=1, source_target_pairs={{1,0},{2,1},{3,2},{4,3},{5,4},{6,5},{7,6},{8,7},{9,8},{10,9},{11,1... | collective-permute-start | bytes 393224 | tf_op jit(solution)/shard_map/ppermute | solution.py:438
  19.3 1.0 copy-start
  20.3 0.9 copy-start.2
  21.2 0.8 copy-start.3
  22.0 0.7 copy-start.6
  22.6 0.7 copy-start.7
  23.3 0.7 copy-start.8
  44.7 29.7 %collective-permute-start.4 = (bf16[240,256]{1,0:T(8,128)(2,1)S(1)}, bf16[240,256]{1,0:T(8,128)(2,1)S(1)}, u32[]{:S(2)}, u32[]{:S(2)}) collective-permute-start(bf16[240,256]{1,0:T(8,128)(2,1)S(1)} %get-tuple-element.46), channel_id=1, source_target_pairs={{0,1},{1,2},{2,3},{3,4},{4,5},{5,6},{6,7},{7,8},{8,9},{9,10},{10,1... | collective-permute-start | bytes 368648 | tf_op jit(solution)/shard_map/ppermute | solution.py:438
  48.7 25.7 %collective-permute-start.5 = (bf16[240,256]{1,0:T(8,128)(2,1)S(1)}, bf16[240,256]{1,0:T(8,128)(2,1)S(1)}, u32[]{:S(2)}, u32[]{:S(2)}) collective-permute-start(bf16[240,256]{1,0:T(8,128)(2,1)S(1)} %get-tuple-element.47), channel_id=1, source_target_pairs={{1,0},{2,1},{3,2},{4,3},{5,4},{6,5},{7,6},{8,7},{9,8},{10,9},{11,1... | collective-permute-start | bytes 368648 | tf_op jit(solution)/shard_map/ppermute | solution.py:438
  92.3 22.8 %collective-permute-start.6 = (bf16[240,256]{1,0:T(8,128)(2,1)S(1)}, bf16[240,256]{1,0:T(8,128)(2,1)S(1)}, u32[]{:S(2)}, u32[]{:S(2)}) collective-permute-start(bf16[240,256]{1,0:T(8,128)(2,1)S(1)} %get-tuple-element.52), channel_id=1, source_target_pairs={{0,1},{1,2},{2,3},{3,4},{4,5},{5,6},{6,7},{7,8},{8,9},{9,10},{10,1... | collective-permute-start | bytes 368648 | tf_op jit(solution)/shard_map/ppermute | solution.py:438
  94.5 20.5 %collective-permute-start.7 = (bf16[240,256]{1,0:T(8,128)(2,1)S(1)}, bf16[240,256]{1,0:T(8,128)(2,1)S(1)}, u32[]{:S(2)}, u32[]{:S(2)}) collective-permute-start(bf16[240,256]{1,0:T(8,128)(2,1)S(1)} %get-tuple-element.53), channel_id=1, source_target_pairs={{1,0},{2,1},{3,2},{4,3},{5,4},{6,5},{7,6},{8,7},{9,8},{10,9},{11,1... | collective-permute-start | bytes 368648 | tf_op jit(solution)/shard_map/ppermute | solution.py:438
  132.2 22.8 %collective-permute-start.8 = (bf16[240,256]{1,0:T(8,128)(2,1)S(1)}, bf16[240,256]{1,0:T(8,128)(2,1)S(1)}, u32[]{:S(2)}, u32[]{:S(2)}) collective-permute-start(bf16[240,256]{1,0:T(8,128)(2,1)S(1)} %get-tuple-element.56), channel_id=1, source_target_pairs={{0,1},{1,2},{2,3},{3,4},{4,5},{5,6},{6,7},{7,8},{8,9},{9,10},{10,1... | collective-permute-start | bytes 368648 | tf_op jit(solution)/shard_map/ppermute | solution.py:438
  134.4 20.6 %collective-permute-start.9 = (bf16[240,256]{1,0:T(8,128)(2,1)S(1)}, bf16[240,256]{1,0:T(8,128)(2,1)S(1)}, u32[]{:S(2)}, u32[]{:S(2)}) collective-permute-start(bf16[240,256]{1,0:T(8,128)(2,1)S(1)} %get-tuple-element.57), channel_id=1, source_target_pairs={{1,0},{2,1},{3,2},{4,3},{5,4},{6,5},{7,6},{8,7},{9,8},{10,9},{11,1... | collective-permute-start | bytes 368648 | tf_op jit(solution)/shard_map/ppermute | solution.py:438

commit v7 on v6

--- a/solution.py
+++ b/solution.py
@@ -25,18 +25,31 @@
 
 
 def banded_kernel(*refs):
-    weight_refs, bias_refs, band_refs, row_refs = refs[:4], refs[4:7], refs[7:11], refs[11:14]
-    flat_ref, turned_ref = refs[14:]
+    sources, band_refs, row_refs = refs[:7], refs[8:12], refs[12:15]
+    copies, (flat_ref, turned_ref, sems) = refs[15:22], refs[22:]
+    fetch = [
+        pltpu.make_async_copy(source, copy, sems.at[index])
+        for index, (source, copy) in enumerate(zip(sources, copies))
+    ]
+    for one in fetch:
+        one.start()
+    for one in fetch:
+        one.wait()
+    weight_refs, bias_refs = copies[:4], copies[4:]
     for layer in range(4):
         weight_ref, band_ref = weight_refs[layer], band_refs[layer]
-        out_width = weight_ref.shape[1]
-        in_width = weight_ref.shape[2] // 5
+        turned_already = layer == 0
+        out_width = weight_ref.shape[2 if turned_already else 1]
+        in_width = weight_ref.shape[1 if turned_already else 2] // 5
         in_pad = PADDED[layer]
         groups = band_ref.shape[0] // (20 * in_pad)
         out_rows = band_ref.shape[1] // out_width
         wide = -(-5 * in_width // 128) * 128
         flat_ref[...] = jnp.zeros(flat_ref.shape, F32)
         for offset in range(5):
+            if turned_already:
+                turned_ref[offset, 0 : 5 * in_width, 0:out_width] = weight_ref[offset].astype(F32)
+                continue
             flat_ref[0:out_width, 0 : 5 * in_width] = weight_ref[offset].astype(F32)
             turned_ref[offset, 0:wide, :] = jnp.transpose(flat_ref[:, 0:wide])
         extra = in_pad - in_width
@@ -65,17 +78,25 @@
         row_ref[...] = jnp.concatenate([bias_ref[...]] * 4, axis=1)
 
 
-def banded(weights, biases):
+def banded(weights, biases, after):
     shapes = [(1280, 512), (5120, 256), (2560, 128), (3200, 256)]
     outs = [jax.ShapeDtypeStruct(shape, BF16) for shape in shapes]
     outs += [jax.ShapeDtypeStruct((1, width), F32) for width in (512, 256, 128)]
+    first, *others = weights
+    args = [first.transpose(0, 2, 1), *others, *[bias[None] for bias in biases]]
     return pl.pallas_call(
         banded_kernel,
         out_shape=outs,
-        scratch_shapes=[pltpu.VMEM((128, 640), F32), pltpu.VMEM((5, 640, 128), F32)],
-        compiler_params=pltpu.CompilerParams(vmem_limit_bytes=24 * 2**20),
+        in_specs=[pl.BlockSpec(memory_space=pltpu.HBM)] * 7 + [pl.BlockSpec(memory_space=pl.ANY)],
+        scratch_shapes=[pltpu.VMEM(arg.shape, arg.dtype) for arg in args]
+        + [
+            pltpu.VMEM((128, 640), F32),
+            pltpu.VMEM((5, 640, 128), F32),
+            pltpu.SemaphoreType.DMA((7,)),
+        ],
+        compiler_params=small_params(),
         name="banded",
-    )(*weights, *[bias[None] for bias in biases])
+    )(*args, after)
 
 
 def lanes_between(shape, low, high):
@@ -123,7 +144,17 @@
     )
 
 
-def prepare_kernel(state_ref, land_ref, count_ref, own_ref, left_ref, right_ref):
+def prepare_kernel(*refs):
+    sources, (own_ref, left_ref, right_ref), copies, sems = refs[:3], refs[3:6], refs[6:9], refs[9]
+    fetch = [
+        pltpu.make_async_copy(source, copy, sems.at[index])
+        for index, (source, copy) in enumerate(zip(sources, copies))
+    ]
+    for one in fetch:
+        one.start()
+    for one in fetch:
+        one.wait()
+    state_ref, land_ref, count_ref = copies
     levels = land_ref[...] * count_ref[...]
     own_ref[:, 24:32, :] = jnp.zeros((ROWS, 8, COLS), F32)
     own_ref[:, 24, :] = levels.astype(F32)
@@ -136,17 +167,20 @@
 
 
 def small_params():
-    return pltpu.CompilerParams(vmem_limit_bytes=24 * 2**20)
-
-
-def prepare(ocean_state, land_mask, layer_count):
+    return pltpu.CompilerParams(vmem_limit_bytes=8 * 2**20)
+
+
+def prepare(*args):
     return pl.pallas_call(
         prepare_kernel,
         out_shape=[jax.ShapeDtypeStruct((ROWS, 32, COLS), F32)]
         + [jax.ShapeDtypeStruct((ROWS * 8, 128), BF16)] * 2,
+        in_specs=[pl.BlockSpec(memory_space=pltpu.HBM)] * 3,
+        scratch_shapes=[pltpu.VMEM(arg.shape, arg.dtype) for arg in args]
+        + [pltpu.SemaphoreType.DMA((3,))],
         compiler_params=small_params(),
         name="prepare",
-    )(ocean_state, land_mask, layer_count)
+    )(*args)
 
 
 def pack_kernel(own_ref, left_ref, right_ref, wide_ref, up_ref, down_ref):
@@ -187,19 +221,24 @@
             ].astype(BF16)
 
 
-def conv_layer(refs, raw_ref, sea_ref, work_ref, zero, layer, groups):
-    in_ref, weight_ref, bias_ref, out_ref = refs
+def conv_layer(refs, raw_ref, sea_ref, work_ref, zero, layer, groups, skip):
+    in_ref, weight_ref, bias_ref, out_ref, mask_ref = refs
+    span = in_ref.shape[1]
     width = weight_ref.shape[1]
 
     def activate(group):
         half = 0.5 * (raw_ref[:, 0:width] + bias_ref[...])
         value = half + half * jnp.tanh(half)
-        if layer:
+        if layer and sea_ref is not None:
             row_of = lax.broadcasted_iota(jnp.int32, (128, width), 0)
             lane_of = lax.broadcasted_iota(jnp.int32, (128, width), 1)
             wanted = 4 * group + 2 * (layer + 1) + lane_of // (width // 4)
             pick = jnp.where(row_of == wanted, 1.0, 0.0).astype(BF16)
-            value = value * jnp.dot(sea_ref[layer - 1], pick, preferred_element_type=F32)
+            mask = jnp.dot(sea_ref[layer - 1], pick, preferred_element_type=F32)
+            mask_ref[group] = mask
+            value = value * mask
+        elif layer:
+            value = value * mask_ref[group, skip : skip + span, :]
         spread(value, work_ref, out_ref, group, zero)
 
     def body(group, carry):
@@ -228,13 +267,13 @@
     own_ref, top_ref, bottom_ref = refs[:3]
     refs = refs[3:]
     if not first:
-        recv_ref, wet_ref, sea_turned_ref = refs[:3]
-        refs = refs[3:]
+        recv_ref, wet_ref, mask2_ref, mask3_ref = refs[:4]
+        refs = refs[4:]
     w1_ref, w2_ref, w3_ref, w4_ref, b1_ref, b2_ref, b3_ref, new_ref, pay_ref = refs[:9]
     refs = refs[9:]
     if first:
-        wet_ref, sea_turned_ref = refs[:2]
-        refs = refs[2:]
+        wet_ref, mask2_ref, mask3_ref = refs[:3]
+        refs = refs[3:]
     if last:
         raw_out_ref = refs.pop(0)
     else:
@@ -242,6 +281,7 @@
         refs = refs[2:]
     state_ref, a0_ref, a1_ref, a2_ref, a3_ref, work_ref, raw_ref, sea_ref, sum_ref = refs[:9]
     turn_ref = refs[9]
+    sea_turned_ref = refs[10] if first else None
     zero = start_ref[1]
 
     halves = ((top_ref, 0), (bottom_ref, HALO + ROWS))
@@ -273,7 +313,7 @@
             )
     first_channel = lax.broadcasted_iota(jnp.int32, (EXT_ROWS, 8, WIDE), 1) == 0
     state_ref[:, 24:32, :] = jnp.where(first_channel, 1.0 - wet_ref[...], 0.0)
-    for layer in (1, 2):
+    for layer in (1, 2) if first else ():
         begin = SIDE - margin + 2 * (layer + 1)
         sea_ref[layer - 1] = sea_turned_ref[begin : begin + span, :].astype(BF16)
 
@@ -290,12 +330,14 @@
         turn(group)
     for layer, refs in enumerate(
         (
-            (a0_ref, w1_ref, b1_ref, a1_ref),
-            (a1_ref, w2_ref, b2_ref, a2_ref),
-            (a2_ref, w3_ref, b3_ref, a3_ref),
+            (a0_ref, w1_ref, b1_ref, a1_ref, None),
+            (a1_ref, w2_ref, b2_ref, a2_ref, mask2_ref),
+            (a2_ref, w3_ref, b3_ref, a3_ref, mask3_ref),
         )
     ):
-        conv_layer(refs, sum_ref, sea_ref, work_ref, zero, layer, 7 - layer)
+        sea = sea_ref if first else None
+        skip = MARGINS[0] - margin
+        conv_layer(refs, sum_ref, sea, work_ref, zero, layer, 7 - layer, skip)
     left = margin - HALO
     count = COLS + 2 * left
     lhs = jnp.concatenate([a3_ref[group, 0:count, :] for group in range(5)], axis=1)
@@ -373,7 +415,8 @@
     ]
     if first:
         outs.append(jax.ShapeDtypeStruct((EXT_ROWS, LEVELS, WIDE), F32))
-        outs.append(jax.ShapeDtypeStruct((WIDE + 8, 128), F32))
+        outs.append(jax.ShapeDtypeStruct((6, span, 256), F32))
+        outs.append(jax.ShapeDtypeStruct((5, span, 128), F32))
     if last:
         outs.append(jax.ShapeDtypeStruct((ROWS, 16, WIDE), F32))
     else:
@@ -395,8 +438,9 @@
             pltpu.VMEM((2, span, 128), BF16),
             pltpu.VMEM((span, 512), F32),
             pltpu.VMEM((1, span + 8, 128), F32),
-        ],
-        compiler_params=pltpu.CompilerParams(vmem_limit_bytes=40 * 2**20),
+        ]
+        + ([pltpu.VMEM((WIDE + 8, 128), F32)] if first else []),
+        compiler_params=pltpu.CompilerParams(vmem_limit_bytes=32 * 2**20),
         name=f"step_{step}",
     )(*args)
 
@@ -426,7 +470,7 @@
             jax.ShapeDtypeStruct((16, ROWS, COLS), F32),
         ],
         scratch_shapes=[pltpu.VMEM((ROWS, 16, COLS), F32)],
-        compiler_params=pltpu.CompilerParams(vmem_limit_bytes=24 * 2**20),
+        compiler_params=pltpu.CompilerParams(vmem_limit_bytes=8 * 2**20),
         name="finish",
     )(received, state, raw, wet)
 
@@ -455,6 +499,7 @@
     weights = banded(
         [conv1_weight, conv2_weight, conv3_weight, conv4_weight],
         [conv1_bias, conv2_bias, conv3_bias],
+        send_left,
     )
     state, send_up, send_down = pack(state, left, right)
     halos = both_ways("lat", send_up, send_down)
@@ -466,11 +511,11 @@
         results = ocean_network_step(step, [start, state, *halos, *extras, *weights])
         state = results[0]
         if step == 0:
-            wet, sea = results[2:4]
+            wet, *masks = results[2:5]
         if step < STEPS - 1:
             halos = both_ways("lat", results[-2], results[-1])
         received = lax.all_to_all(results[1], ("sec", "lat"), 0, 0)
-        extras = [received, wet, sea]
+        extras = [received, wet, *masks]
     return finish(received, state, results[2], wet)
 
 

time: 187 us -> 186 us (level)
    pallas_call x4, Pallas kernels: 69.8 us -> 67.6 us  [ocean_network_step(): pl.pallas_call(functools.partial(step_kernel, step=step), out_shape=outs,...]
    unnamed x19 -> x20, local copies, waits for them, and re-layouts: 8.14 us -> 7.97 us
  transfers between devices with their start and end apart: 10 -> 10, of which waited for: 1 -> 1; matrix products, arithmetic and copies ran while one was open for 1% -> 0% of each run, Pallas kernels for 1% -> 2%
where the time goes in v7:
time: 186 us; the launch traced here: 185 us
  blocking collectives  76.7 us (41%)
  Pallas kernels  72.2 us (39%)
  starting transfers between devices  23.7 us (13%)
  local copies, waits for them, and re-layouts  7.97 us (4%)
  waiting for transfers between devices  3.32 us (2%)
    all_to_all x4, blocking collectives, local(): received = lax.all_to_all(results[1], ('sec', 'lat'), 0, 0)  76.7 us
    pallas_call x4, Pallas kernels, ocean_network_step(): pl.pallas_call(functools.partial(step_kernel, step=step), out_shape=outs,...  67.6 us
    ppermute x10, starting transfers between devices, both_ways(): return (lax.ppermute(up, axis, forward), lax.ppermute(down, axis, backward))  23.7 us
    unnamed x20, local copies, waits for them, and re-layouts  7.97 us
  transfers between devices with their start and end apart: 10, of which 1 were waited for; matrix products, arithmetic and copies ran while one was open for 0% of the time, Pallas kernels for 2%

profile of v7, /device:TPU:1, one launch (start us, length us, event | category | flops | bytes accessed | tf_op | source)
XLA Modules:
  0.0 184.9 jit_solution(2785782528116894698)
XLA Ops:
  0.6 1.0 copy-done.1
  3.6 4.9 %collective-permute-start = (bf16[128,128]{1,0:T(8,128)(2,1)S(1)}, bf16[128,128]{1,0:T(8,128)(2,1)S(1)}, u32[]{:S(2)}, u32[]{:S(2)}) collective-permute-start(bf16[128,128]{1,0:T(8,128)(2,1)S(1)} %get-tuple-element.34), channel_id=1, source_target_pairs={{0,32},{32,64},{64,96},{1,33},{33,65},{65,97},{2,34},{34,66},{66,9... | collective-permute-start | bytes 98312 | tf_op jit(solution)/shard_map/ppermute | solution.py:482
  8.5 1.9 %collective-permute-start.1 = (bf16[128,128]{1,0:T(8,128)(2,1)S(1)}, bf16[128,128]{1,0:T(8,128)(2,1)S(1)}, u32[]{:S(2)}, u32[]{:S(2)}) collective-permute-start(bf16[128,128]{1,0:T(8,128)(2,1)S(1)} %get-tuple-element.35.refs_7_), channel_id=1, source_target_pairs={{32,0},{64,32},{96,64},{33,1},{65,33},{97,65},{34,2},{66,34},{98,6... | collective-permute-start | bytes 98312 | tf_op jit(solution)/shard_map/ppermute | solution.py:482
  10.5 3.3 %collective-permute-done.1.right_ref = bf16[128,128]{1,0:T(8,128)(2,1)S(1)} collective-permute-done((bf16[128,128]{1,0:T(8,128)(2,1)S(1)}, bf16[128,128]{1,0:T(8,128)(2,1)S(1)}, u32[]{:S(2)}, u32[]{:S(2)}) %collective-permute-start.1) | collective-permute-done | bytes 32800 | tf_op jit(solution)/shard_map/ppermute | solution.py:482
  14.0 3.2 %collective-permute-start.2 = (bf16[256,256]{1,0:T(8,128)(2,1)S(1)}, bf16[256,256]{1,0:T(8,128)(2,1)S(1)}, u32[]{:S(2)}, u32[]{:S(2)}) collective-permute-start(bf16[256,256]{1,0:T(8,128)(2,1)S(1)} %get-tuple-element.37), channel_id=1, source_target_pairs={{0,1},{1,2},{2,3},{3,4},{4,5},{5,6},{6,7},{7,8},{8,9},{9,10},{10,1... | collective-permute-start | bytes 393224 | tf_op jit(solution)/shard_map/ppermute | solution.py:482
  17.2 1.3 collective-permute-start.3
  18.5 1.0 copy-done
  19.5 0.9 copy-done.2
  24.0 2.8 %banded.1 = (bf16[1280,512]{1,0:T(8,128)(2,1)S(1)}, bf16[5120,256]{1,0:T(8,128)(2,1)S(1)}, bf16[2560,128]{1,0:T(8,128)(2,1)S(1)}, bf16[3200,256]{1,0:T(8,128)(2,...) custom-call(bf16[5,120,128]{2,1,0:T(8,128)(2,1)S(1)} %bitcast.25, ...), custom_call_target="tpu_custom_call" | custom-call | tf_op jit(solution)/shard_map/banded/pallas_call | solution.py:87
  26.9 18.5 %step_0.1 = (f32[16,24,384]{2,1,0:T(8,128)S(1)}, f32[128,128]{1,0:T(8,128)S(1)}, f32[32,8,384]{2,1,0:T(8,128)S(1)}, f32[6,320,256]{2,1,0:T(8,128)S(1)}, f32[5,32...) custom-call(s32[2]{0:T(128)S(1)} %pad_add_fusion.refs_0_, ...), custom_call_target="tpu_custom_call" | custom-call | tf_op jit(solution)/shard_map/step_0/pallas_call | solution.py:425
  45.4 4.0 %collective-permute-start.4 = (bf16[240,256]{1,0:T(8,128)(2,1)S(1)}, bf16[240,256]{1,0:T(8,128)(2,1)S(1)}, u32[]{:S(2)}, u32[]{:S(2)}) collective-permute-start(bf16[240,256]{1,0:T(8,128)(2,1)S(1)} %get-tuple-element.47), channel_id=1, source_target_pairs={{0,1},{1,2},{2,3},{3,4},{4,5},{5,6},{6,7},{7,8},{8,9},{9,10},{10,1... | collective-permute-start | bytes 368648 | tf_op jit(solution)/shard_map/ppermute | solution.py:482
  49.4 1.3 collective-permute-start.5
  50.7 24.4 %all_to_all.44 = f32[128,1,128]{2,1,0:T(1,128)S(1)} all-to-all(f32[128,1,128]{2,1,0:T(1,128)S(1)} %bitcast.26), channel_id=1, replica_groups=mesh['sec'=4,'lat'=32] {'sec','lat'}, dimensions={0} | all-to-all | bytes 131072 | tf_op jit(solution)/shard_map/all_to_all | solution.py:517
  75.1 17.1 %step_1.1 = (f32[16,24,384]{2,1,0:T(8,128)S(1)}, f32[128,128]{1,0:T(8,128)S(1)}, bf16[240,256]{1,0:T(8,128)(2,1)S(1)}, bf16[240,256]{1,0:T(8,128)(2,1)S(1)}) custom-call(s32[2]{0:T(128)S(1)} %pad_add_fusion.refs_0_, f32[16,24,384]{2,1,0:T(8,128)S(1)} %get-tuple-element.46.refs_1_, bf16[240,256]{1,0:T(8,128)(2,1)S(1)} %collective-permute-done.4.refs_2_, ...), custom_call_target="tpu_custom_call" | custom-call | tf_op jit(solution)/shard_map/step_1/pallas_call | solution.py:425
  92.2 2.3 %collective-permute-start.6 = (bf16[240,256]{1,0:T(8,128)(2,1)S(1)}, bf16[240,256]{1,0:T(8,128)(2,1)S(1)}, u32[]{:S(2)}, u32[]{:S(2)}) collective-permute-start(bf16[240,256]{1,0:T(8,128)(2,1)S(1)} %get-tuple-element.54), channel_id=1, source_target_pairs={{0,1},{1,2},{2,3},{3,4},{4,5},{5,6},{6,7},{7,8},{8,9},{9,10},{10,1... | collective-permute-start | bytes 368648 | tf_op jit(solution)/shard_map/ppermute | solution.py:482
  94.5 1.3 collective-permute-start.7
  95.8 19.2 %all_to_all.45 = f32[128,1,128]{2,1,0:T(1,128)S(1)} all-to-all(f32[128,1,128]{2,1,0:T(1,128)S(1)} %bitcast.28), channel_id=1, replica_groups=mesh['sec'=4,'lat'=32] {'sec','lat'}, dimensions={0} | all-to-all | bytes 131072 | tf_op jit(solution)/shard_map/all_to_all | solution.py:517
  115.0 16.4 %step_2.1 = (f32[16,24,384]{2,1,0:T(8,128)S(1)}, f32[128,128]{1,0:T(8,128)S(1)}, bf16[240,256]{1,0:T(8,128)(2,1)S(1)}, bf16[240,256]{1,0:T(8,128)(2,1)S(1)}) custom-call(s32[2]{0:T(128)S(1)} %pad_add_fusion.refs_0_, f32[16,24,384]{2,1,0:T(8,128)S(1)} %get-tuple-element.53.refs_1_, bf16[240,256]{1,0:T(8,128)(2,1)S(1)} %collective-permute-done.6.refs_2_, ...), custom_call_target="tpu_custom_call" | custom-call | tf_op jit(solution)/shard_map/step_2/pallas_call | solution.py:425
  131.4 2.3 %collective-permute-start.8 = (bf16[240,256]{1,0:T(8,128)(2,1)S(1)}, bf16[240,256]{1,0:T(8,128)(2,1)S(1)}, u32[]{:S(2)}, u32[]{:S(2)}) collective-permute-start(bf16[240,256]{1,0:T(8,128)(2,1)S(1)} %get-tuple-element.58), channel_id=1, source_target_pairs={{0,1},{1,2},{2,3},{3,4},{4,5},{5,6},{6,7},{7,8},{8,9},{9,10},{10,1... | collective-permute-start | bytes 368648 | tf_op jit(solution)/shard_map/ppermute | solution.py:482
  133.7 1.3 collective-permute-start.9
  135.0 19.2 %all_to_all.46 = f32[128,1,128]{2,1,0:T(1,128)S(1)} all-to-all(f32[128,1,128]{2,1,0:T(1,128)S(1)} %bitcast.29), channel_id=1, replica_groups=mesh['sec'=4,'lat'=32] {'sec','lat'}, dimensions={0} | all-to-all | bytes 131072 | tf_op jit(solution)/shard_map/all_to_all | solution.py:517
  154.2 15.6 %step_3.1 = (f32[16,24,384]{2,1,0:T(8,128)S(1)}, f32[128,128]{1,0:T(8,128)S(1)}, f32[16,16,384]{2,1,0:T(8,128)S(1)}) custom-call(s32[2]{0:T(128)S(1)} %pad_add_fusion.refs_0_, f32[16,24,384]{2,1,0:T(8,128)S(1)} %get-tuple-element.57.refs_1_, bf16[240,256]{1,0:T(8,128)(2,1)S(1)} %collective-permute-done.8.refs_2_, ...), custom_call_target="tpu_custom_call" | custom-call | tf_op jit(solution)/shard_map/step_3/pallas_call | solution.py:425
  169.8 13.9 %all_to_all.47 = f32[128,1,128]{2,1,0:T(1,128)S(1)} all-to-all(f32[128,1,128]{2,1,0:T(1,128)S(1)} %bitcast.27), channel_id=1, replica_groups=mesh['sec'=4,'lat'=32] {'sec','lat'}, dimensions={0} | all-to-all | bytes 131072 | tf_op jit(solution)/shard_map/all_to_all | solution.py:517
  183.8 1.1 finish.1
  (29 shorter events, 5.9 us)
Async XLA Ops:
  0.6 1.0 copy-start.1
  1.6 0.7 copy-start.5
  2.3 0.7 copy-start.6
  3.6 6.9 %collective-permute-start = (bf16[128,128]{1,0:T(8,128)(2,1)S(1)}, bf16[128,128]{1,0:T(8,128)(2,1)S(1)}, u32[]{:S(2)}, u32[]{:S(2)}) collective-permute-start(bf16[128,128]{1,0:T(8,128)(2,1)S(1)} %get-tuple-element.34), channel_id=1, source_target_pairs={{0,32},{32,64},{64,96},{1,33},{33,65},{65,97},{2,34},{34,66},{66,9... | collective-permute-start | bytes 98312 | tf_op jit(solution)/shard_map/ppermute | solution.py:482
  8.5 5.2 %collective-permute-start.1 = (bf16[128,128]{1,0:T(8,128)(2,1)S(1)}, bf16[128,128]{1,0:T(8,128)(2,1)S(1)}, u32[]{:S(2)}, u32[]{:S(2)}) collective-permute-start(bf16[128,128]{1,0:T(8,128)(2,1)S(1)} %get-tuple-element.35.refs_7_), channel_id=1, source_target_pairs={{32,0},{64,32},{96,64},{33,1},{65,33},{97,65},{34,2},{66,34},{98,6... | collective-permute-start | bytes 98312 | tf_op jit(solution)/shard_map/ppermute | solution.py:482
  14.0 13.0 %collective-permute-start.2 = (bf16[256,256]{1,0:T(8,128)(2,1)S(1)}, bf16[256,256]{1,0:T(8,128)(2,1)S(1)}, u32[]{:S(2)}, u32[]{:S(2)}) collective-permute-start(bf16[256,256]{1,0:T(8,128)(2,1)S(1)} %get-tuple-element.37), channel_id=1, source_target_pairs={{0,1},{1,2},{2,3},{3,4},{4,5},{5,6},{6,7},{7,8},{8,9},{9,10},{10,1... | collective-permute-start | bytes 393224 | tf_op jit(solution)/shard_map/ppermute | solution.py:482
  17.2 9.7 %collective-permute-start.3 = (bf16[256,256]{1,0:T(8,128)(2,1)S(1)}, bf16[256,256]{1,0:T(8,128)(2,1)S(1)}, u32[]{:S(2)}, u32[]{:S(2)}) collective-permute-start(bf16[256,256]{1,0:T(8,128)(2,1)S(1)} %get-tuple-element.38), channel_id=1, source_target_pairs={{1,0},{2,1},{3,2},{4,3},{5,4},{6,5},{7,6},{8,7},{9,8},{10,9},{11,1... | collective-permute-start | bytes 393224 | tf_op jit(solution)/shard_map/ppermute | solution.py:482
  18.5 1.0 copy-start
  19.5 0.9 copy-start.2
  20.4 0.9 copy-start.3
  21.3 0.8 copy-start.4
  22.1 0.7 copy-start.7
  22.7 0.7 copy-start.8
  23.4 0.7 copy-start.9
  45.4 29.7 %collective-permute-start.4 = (bf16[240,256]{1,0:T(8,128)(2,1)S(1)}, bf16[240,256]{1,0:T(8,128)(2,1)S(1)}, u32[]{:S(2)}, u32[]{:S(2)}) collective-permute-start(bf16[240,256]{1,0:T(8,128)(2,1)S(1)} %get-tuple-element.47), channel_id=1, source_target_pairs={{0,1},{1,2},{2,3},{3,4},{4,5},{5,6},{6,7},{7,8},{8,9},{9,10},{10,1... | collective-permute-start | bytes 368648 | tf_op jit(solution)/shard_map/ppermute | solution.py:482
  49.4 25.7 %collective-permute-start.5 = (bf16[240,256]{1,0:T(8,128)(2,1)S(1)}, bf16[240,256]{1,0:T(8,128)(2,1)S(1)}, u32[]{:S(2)}, u32[]{:S(2)}) collective-permute-start(bf16[240,256]{1,0:T(8,128)(2,1)S(1)} %get-tuple-element.48), channel_id=1, source_target_pairs={{1,0},{2,1},{3,2},{4,3},{5,4},{6,5},{7,6},{8,7},{9,8},{10,9},{11,1... | collective-permute-start | bytes 368648 | tf_op jit(solution)/shard_map/ppermute | solution.py:482
  92.2 22.8 %collective-permute-start.6 = (bf16[240,256]{1,0:T(8,128)(2,1)S(1)}, bf16[240,256]{1,0:T(8,128)(2,1)S(1)}, u32[]{:S(2)}, u32[]{:S(2)}) collective-permute-start(bf16[240,256]{1,0:T(8,128)(2,1)S(1)} %get-tuple-element.54), channel_id=1, source_target_pairs={{0,1},{1,2},{2,3},{3,4},{4,5},{5,6},{6,7},{7,8},{8,9},{9,10},{10,1... | collective-permute-start | bytes 368648 | tf_op jit(solution)/shard_map/ppermute | solution.py:482
  94.5 20.5 %collective-permute-start.7 = (bf16[240,256]{1,0:T(8,128)(2,1)S(1)}, bf16[240,256]{1,0:T(8,128)(2,1)S(1)}, u32[]{:S(2)}, u32[]{:S(2)}) collective-permute-start(bf16[240,256]{1,0:T(8,128)(2,1)S(1)} %get-tuple-element.55), channel_id=1, source_target_pairs={{1,0},{2,1},{3,2},{4,3},{5,4},{6,5},{7,6},{8,7},{9,8},{10,9},{11,1... | collective-permute-start | bytes 368648 | tf_op jit(solution)/shard_map/ppermute | solution.py:482
  131.4 22.8 %collective-permute-start.8 = (bf16[240,256]{1,0:T(8,128)(2,1)S(1)}, bf16[240,256]{1,0:T(8,128)(2,1)S(1)}, u32[]{:S(2)}, u32[]{:S(2)}) collective-permute-start(bf16[240,256]{1,0:T(8,128)(2,1)S(1)} %get-tuple-element.58), channel_id=1, source_target_pairs={{0,1},{1,2},{2,3},{3,4},{4,5},{5,6},{6,7},{7,8},{8,9},{9,10},{10,1... | collective-permute-start | bytes 368648 | tf_op jit(solution)/shard_map/ppermute | solution.py:482
  133.7 20.5 %collective-permute-start.9 = (bf16[240,256]{1,0:T(8,128)(2,1)S(1)}, bf16[240,256]{1,0:T(8,128)(2,1)S(1)}, u32[]{:S(2)}, u32[]{:S(2)}) collective-permute-start(bf16[240,256]{1,0:T(8,128)(2,1)S(1)} %get-tuple-element.59), channel_id=1, source_target_pairs={{1,0},{2,1},{3,2},{4,3},{5,4},{6,5},{7,6},{8,7},{9,8},{10,9},{11,1... | collective-permute-start | bytes 368648 | tf_op jit(solution)/shard_map/ppermute | solution.py:482

commit v8 on v7

--- a/solution.py
+++ b/solution.py
@@ -25,8 +25,8 @@
 
 
 def banded_kernel(*refs):
-    sources, band_refs, row_refs = refs[:7], refs[8:12], refs[12:15]
-    copies, (flat_ref, turned_ref, sems) = refs[15:22], refs[22:]
+    sources, band_refs, row_refs = refs[:5], refs[6:10], refs[10:13]
+    copies, (flat_ref, turned_ref, sems) = refs[13:18], refs[18:]
     fetch = [
         pltpu.make_async_copy(source, copy, sems.at[index])
         for index, (source, copy) in enumerate(zip(sources, copies))
@@ -35,7 +35,7 @@
         one.start()
     for one in fetch:
         one.wait()
-    weight_refs, bias_refs = copies[:4], copies[4:]
+    weight_refs, bias_ref = copies[:4], copies[4]
     for layer in range(4):
         weight_ref, band_ref = weight_refs[layer], band_refs[layer]
         turned_already = layer == 0
@@ -74,8 +74,11 @@
                         parts.append(part)
                     base = ((group * 5 + shift) * 4 + row) * in_pad
                     band_ref[base : base + in_pad, :] = jnp.concatenate(parts, axis=1).astype(BF16)
-    for bias_ref, row_ref in zip(bias_refs, row_refs):
-        row_ref[...] = jnp.concatenate([bias_ref[...]] * 4, axis=1)
+    begin = 0
+    for row_ref in row_refs:
+        width = row_ref.shape[1] // 4
+        row_ref[...] = jnp.concatenate([bias_ref[:, begin : begin + width]] * 4, axis=1)
+        begin += width
 
 
 def banded(weights, biases, after):
@@ -83,16 +86,16 @@
     outs = [jax.ShapeDtypeStruct(shape, BF16) for shape in shapes]
     outs += [jax.ShapeDtypeStruct((1, width), F32) for width in (512, 256, 128)]
     first, *others = weights
-    args = [first.transpose(0, 2, 1), *others, *[bias[None] for bias in biases]]
+    args = [first.transpose(0, 2, 1), *others, jnp.concatenate(biases)[None]]
     return pl.pallas_call(
         banded_kernel,
         out_shape=outs,
-        in_specs=[pl.BlockSpec(memory_space=pltpu.HBM)] * 7 + [pl.BlockSpec(memory_space=pl.ANY)],
+        in_specs=[pl.BlockSpec(memory_space=pltpu.HBM)] * 5 + [pl.BlockSpec(memory_space=pl.ANY)],
         scratch_shapes=[pltpu.VMEM(arg.shape, arg.dtype) for arg in args]
         + [
             pltpu.VMEM((128, 640), F32),
             pltpu.VMEM((5, 640, 128), F32),
-            pltpu.SemaphoreType.DMA((7,)),
+            pltpu.SemaphoreType.DMA((5,)),
         ],
         compiler_params=small_params(),
         name="banded",
@@ -145,7 +148,7 @@
 
 
 def prepare_kernel(*refs):
-    sources, (own_ref, left_ref, right_ref), copies, sems = refs[:3], refs[3:6], refs[6:9], refs[9]
+    sources, (own_ref, left_ref, right_ref), copies, sems = refs[:2], refs[2:5], refs[5:7], refs[7]
     fetch = [
         pltpu.make_async_copy(source, copy, sems.at[index])
         for index, (source, copy) in enumerate(zip(sources, copies))
@@ -154,8 +157,8 @@
         one.start()
     for one in fetch:
         one.wait()
-    state_ref, land_ref, count_ref = copies
-    levels = land_ref[...] * count_ref[...]
+    state_ref, levels_ref = copies
+    levels = levels_ref[...]
     own_ref[:, 24:32, :] = jnp.zeros((ROWS, 8, COLS), F32)
     own_ref[:, 24, :] = levels.astype(F32)
     for channel in range(24):
@@ -175,9 +178,9 @@
         prepare_kernel,
         out_shape=[jax.ShapeDtypeStruct((ROWS, 32, COLS), F32)]
         + [jax.ShapeDtypeStruct((ROWS * 8, 128), BF16)] * 2,
-        in_specs=[pl.BlockSpec(memory_space=pltpu.HBM)] * 3,
+        in_specs=[pl.BlockSpec(memory_space=pltpu.HBM)] * 2,
         scratch_shapes=[pltpu.VMEM(arg.shape, arg.dtype) for arg in args]
-        + [pltpu.SemaphoreType.DMA((3,))],
+        + [pltpu.SemaphoreType.DMA((2,))],
         compiler_params=small_params(),
         name="prepare",
     )(*args)
@@ -282,7 +285,7 @@
     state_ref, a0_ref, a1_ref, a2_ref, a3_ref, work_ref, raw_ref, sea_ref, sum_ref = refs[:9]
     turn_ref = refs[9]
     sea_turned_ref = refs[10] if first else None
-    zero = start_ref[1]
+    zero = start_ref[0] // 65536
 
     halves = ((top_ref, 0), (bottom_ref, HALO + ROWS))
     for packed_ref, low in halves:
@@ -494,7 +497,7 @@
     conv3_bias,
     conv4_weight,
 ):
-    state, send_left, send_right = prepare(ocean_state, land_mask, layer_count)
+    state, send_left, send_right = prepare(ocean_state, land_mask * layer_count)
     left, right = both_ways("sec", send_right, send_left)
     weights = banded(
         [conv1_weight, conv2_weight, conv3_weight, conv4_weight],
@@ -504,8 +507,7 @@
     state, send_up, send_down = pack(state, left, right)
     halos = both_ways("lat", send_up, send_down)
 
-    start = (lax.axis_index("lat") * ROWS).astype(jnp.int32)
-    start = jnp.stack([start, jnp.zeros((), jnp.int32)])
+    start = (lax.axis_index("lat") * ROWS).astype(jnp.int32)[None]
     extras = []
     for step in range(STEPS):
         results = ocean_network_step(step, [start, state, *halos, *extras, *weights])

time: 186 us -> 181 us (0.973)
  local copies, waits for them, and re-layouts: 7.97 us -> 4.59 us
  Pallas kernels: 72.2 us -> 70 us
    unnamed x20 -> x10, local copies, waits for them, and re-layouts: 7.97 us -> 4.59 us
    pallas_call x4, Pallas kernels: 67.6 us -> 65.5 us  [ocean_network_step(): pl.pallas_call(functools.partial(step_kernel, step=step), out_shape=outs,...]
where the time goes in v8:
time: 181 us
  blocking collectives  76.8 us (42%)
  Pallas kernels  70 us (39%)
  starting transfers between devices  23.8 us (13%)
  local copies, waits for them, and re-layouts  4.59 us (3%)
  waiting for transfers between devices  3.32 us (2%)
    all_to_all x4, blocking collectives, local(): received = lax.all_to_all(results[1], ('sec', 'lat'), 0, 0)  76.8 us
    pallas_call x4, Pallas kernels, ocean_network_step(): pl.pallas_call(functools.partial(step_kernel, step=step), out_shape=outs,...  65.5 us
    ppermute x10, starting transfers between devices, both_ways(): return (lax.ppermute(up, axis, forward), lax.ppermute(down, axis, backward))  23.8 us
    unnamed x10, local copies, waits for them, and re-layouts  4.59 us
  transfers between devices with their start and end apart: 10, of which 1 were waited for; matrix products, arithmetic and copies ran while one was open for 0% of the time, Pallas kernels for 2%

profile of v8, /device:TPU:1, one launch (start us, length us, event | category | flops | bytes accessed | tf_op | source)
XLA Modules:
  0.0 180.7 jit_solution(12429326152822749023)
XLA Ops:
  1.4 1.0 copy-done.1
  2.9 4.9 %collective-permute-start = (bf16[128,128]{1,0:T(8,128)(2,1)S(1)}, bf16[128,128]{1,0:T(8,128)(2,1)S(1)}, u32[]{:S(2)}, u32[]{:S(2)}) collective-permute-start(bf16[128,128]{1,0:T(8,128)(2,1)S(1)} %get-tuple-element.34), channel_id=1, source_target_pairs={{0,32},{32,64},{64,96},{1,33},{33,65},{65,97},{2,34},{34,66},{66,9... | collective-permute-start | bytes 98312 | tf_op jit(solution)/shard_map/ppermute | solution.py:485
  7.8 1.9 %collective-permute-start.1 = (bf16[128,128]{1,0:T(8,128)(2,1)S(1)}, bf16[128,128]{1,0:T(8,128)(2,1)S(1)}, u32[]{:S(2)}, u32[]{:S(2)}) collective-permute-start(bf16[128,128]{1,0:T(8,128)(2,1)S(1)} %get-tuple-element.35.refs_5_), channel_id=1, source_target_pairs={{32,0},{64,32},{96,64},{33,1},{65,33},{97,65},{34,2},{66,34},{98,6... | collective-permute-start | bytes 98312 | tf_op jit(solution)/shard_map/ppermute | solution.py:485
  9.7 3.3 %collective-permute-done.1.right_ref = bf16[128,128]{1,0:T(8,128)(2,1)S(1)} collective-permute-done((bf16[128,128]{1,0:T(8,128)(2,1)S(1)}, bf16[128,128]{1,0:T(8,128)(2,1)S(1)}, u32[]{:S(2)}, u32[]{:S(2)}) %collective-permute-start.1) | collective-permute-done | bytes 32800 | tf_op jit(solution)/shard_map/ppermute | solution.py:485
  13.2 3.2 %collective-permute-start.2 = (bf16[256,256]{1,0:T(8,128)(2,1)S(1)}, bf16[256,256]{1,0:T(8,128)(2,1)S(1)}, u32[]{:S(2)}, u32[]{:S(2)}) collective-permute-start(bf16[256,256]{1,0:T(8,128)(2,1)S(1)} %get-tuple-element.37), channel_id=1, source_target_pairs={{0,1},{1,2},{2,3},{3,4},{4,5},{5,6},{6,7},{7,8},{8,9},{9,10},{10,1... | collective-permute-start | bytes 393224 | tf_op jit(solution)/shard_map/ppermute | solution.py:485
  16.4 1.3 collective-permute-start.3
  18.5 1.0 copy-done
  19.5 0.9 copy-done.2
  22.1 2.8 %banded.1 = (bf16[1280,512]{1,0:T(8,128)(2,1)S(1)}, bf16[5120,256]{1,0:T(8,128)(2,1)S(1)}, bf16[2560,128]{1,0:T(8,128)(2,1)S(1)}, bf16[3200,256]{1,0:T(8,128)(2,...) custom-call(bf16[5,120,128]{2,1,0:T(8,128)(2,1)S(1)} %bitcast.23, ...), custom_call_target="tpu_custom_call" | custom-call | tf_op jit(solution)/shard_map/banded/pallas_call | solution.py:90
  24.9 18.0 %step_0.1 = (f32[16,24,384]{2,1,0:T(8,128)S(1)}, f32[128,128]{1,0:T(8,128)S(1)}, f32[32,8,384]{2,1,0:T(8,128)S(1)}, f32[6,320,256]{2,1,0:T(8,128)S(1)}, f32[5,32...) custom-call(s32[1]{0:T(128)} %bitcast.refs_0_, ...), custom_call_target="tpu_custom_call" | custom-call | tf_op jit(solution)/shard_map/step_0/pallas_call | solution.py:428
  42.9 4.0 %collective-permute-start.4 = (bf16[240,256]{1,0:T(8,128)(2,1)S(1)}, bf16[240,256]{1,0:T(8,128)(2,1)S(1)}, u32[]{:S(2)}, u32[]{:S(2)}) collective-permute-start(bf16[240,256]{1,0:T(8,128)(2,1)S(1)} %get-tuple-element.47), channel_id=1, source_target_pairs={{0,1},{1,2},{2,3},{3,4},{4,5},{5,6},{6,7},{7,8},{8,9},{9,10},{10,1... | collective-permute-start | bytes 368648 | tf_op jit(solution)/shard_map/ppermute | solution.py:485
  46.9 1.3 collective-permute-start.5
  48.2 24.4 %all_to_all.44 = f32[128,1,128]{2,1,0:T(1,128)S(1)} all-to-all(f32[128,1,128]{2,1,0:T(1,128)S(1)} %bitcast.24), channel_id=1, replica_groups=mesh['sec'=4,'lat'=32] {'sec','lat'}, dimensions={0} | all-to-all | bytes 131072 | tf_op jit(solution)/shard_map/all_to_all | solution.py:519
  72.6 16.5 %step_1.1 = (f32[16,24,384]{2,1,0:T(8,128)S(1)}, f32[128,128]{1,0:T(8,128)S(1)}, bf16[240,256]{1,0:T(8,128)(2,1)S(1)}, bf16[240,256]{1,0:T(8,128)(2,1)S(1)}) custom-call(s32[1]{0:T(128)} %bitcast.refs_0_, f32[16,24,384]{2,1,0:T(8,128)S(1)} %get-tuple-element.46.refs_1_, bf16[240,256]{1,0:T(8,128)(2,1)S(1)} %collective-permute-done.4.refs_2_, ...), custom_call_target="tpu_custom_call" | custom-call | tf_op jit(solution)/shard_map/step_1/pallas_call | solution.py:428
  89.1 2.3 %collective-permute-start.6 = (bf16[240,256]{1,0:T(8,128)(2,1)S(1)}, bf16[240,256]{1,0:T(8,128)(2,1)S(1)}, u32[]{:S(2)}, u32[]{:S(2)}) collective-permute-start(bf16[240,256]{1,0:T(8,128)(2,1)S(1)} %get-tuple-element.54), channel_id=1, source_target_pairs={{0,1},{1,2},{2,3},{3,4},{4,5},{5,6},{6,7},{7,8},{8,9},{9,10},{10,1... | collective-permute-start | bytes 368648 | tf_op jit(solution)/shard_map/ppermute | solution.py:485
  91.4 1.3 collective-permute-start.7
  92.7 19.2 %all_to_all.45 = f32[128,1,128]{2,1,0:T(1,128)S(1)} all-to-all(f32[128,1,128]{2,1,0:T(1,128)S(1)} %bitcast.26), channel_id=1, replica_groups=mesh['sec'=4,'lat'=32] {'sec','lat'}, dimensions={0} | all-to-all | bytes 131072 | tf_op jit(solution)/shard_map/all_to_all | solution.py:519
  111.9 15.9 %step_2.1 = (f32[16,24,384]{2,1,0:T(8,128)S(1)}, f32[128,128]{1,0:T(8,128)S(1)}, bf16[240,256]{1,0:T(8,128)(2,1)S(1)}, bf16[240,256]{1,0:T(8,128)(2,1)S(1)}) custom-call(s32[1]{0:T(128)} %bitcast.refs_0_, f32[16,24,384]{2,1,0:T(8,128)S(1)} %get-tuple-element.53.refs_1_, bf16[240,256]{1,0:T(8,128)(2,1)S(1)} %collective-permute-done.6.refs_2_, ...), custom_call_target="tpu_custom_call" | custom-call | tf_op jit(solution)/shard_map/step_2/pallas_call | solution.py:428
  127.8 2.3 %collective-permute-start.8 = (bf16[240,256]{1,0:T(8,128)(2,1)S(1)}, bf16[240,256]{1,0:T(8,128)(2,1)S(1)}, u32[]{:S(2)}, u32[]{:S(2)}) collective-permute-start(bf16[240,256]{1,0:T(8,128)(2,1)S(1)} %get-tuple-element.58), channel_id=1, source_target_pairs={{0,1},{1,2},{2,3},{3,4},{4,5},{5,6},{6,7},{7,8},{8,9},{9,10},{10,1... | collective-permute-start | bytes 368648 | tf_op jit(solution)/shard_map/ppermute | solution.py:485
  130.1 1.3 collective-permute-start.9
  131.4 19.2 %all_to_all.46 = f32[128,1,128]{2,1,0:T(1,128)S(1)} all-to-all(f32[128,1,128]{2,1,0:T(1,128)S(1)} %bitcast.27), channel_id=1, replica_groups=mesh['sec'=4,'lat'=32] {'sec','lat'}, dimensions={0} | all-to-all | bytes 131072 | tf_op jit(solution)/shard_map/all_to_all | solution.py:519
  150.6 15.1 %step_3.1 = (f32[16,24,384]{2,1,0:T(8,128)S(1)}, f32[128,128]{1,0:T(8,128)S(1)}, f32[16,16,384]{2,1,0:T(8,128)S(1)}) custom-call(s32[1]{0:T(128)} %bitcast.refs_0_, f32[16,24,384]{2,1,0:T(8,128)S(1)} %get-tuple-element.57.refs_1_, bf16[240,256]{1,0:T(8,128)(2,1)S(1)} %collective-permute-done.8.refs_2_, bf16[240,256]{1,0:T(8,128)(2,1)S(1)} %collective-permute-done.9.refs_3_, ...), custom_call_target="tpu_custom_call" | custom-call | tf_op jit(solution)/shard_map/step_3/pallas_call | solution.py:428
  165.7 13.9 %all_to_all.47 = f32[128,1,128]{2,1,0:T(1,128)S(1)} all-to-all(f32[128,1,128]{2,1,0:T(1,128)S(1)} %bitcast.25), channel_id=1, replica_groups=mesh['sec'=4,'lat'=32] {'sec','lat'}, dimensions={0} | all-to-all | bytes 131072 | tf_op jit(solution)/shard_map/all_to_all | solution.py:519
  179.6 1.1 finish.1
  (20 shorter events, 3.9 us)
Async XLA Ops:
  1.4 1.0 copy-start.1
  2.9 6.9 %collective-permute-start = (bf16[128,128]{1,0:T(8,128)(2,1)S(1)}, bf16[128,128]{1,0:T(8,128)(2,1)S(1)}, u32[]{:S(2)}, u32[]{:S(2)}) collective-permute-start(bf16[128,128]{1,0:T(8,128)(2,1)S(1)} %get-tuple-element.34), channel_id=1, source_target_pairs={{0,32},{32,64},{64,96},{1,33},{33,65},{65,97},{2,34},{34,66},{66,9... | collective-permute-start | bytes 98312 | tf_op jit(solution)/shard_map/ppermute | solution.py:485
  7.8 5.2 %collective-permute-start.1 = (bf16[128,128]{1,0:T(8,128)(2,1)S(1)}, bf16[128,128]{1,0:T(8,128)(2,1)S(1)}, u32[]{:S(2)}, u32[]{:S(2)}) collective-permute-start(bf16[128,128]{1,0:T(8,128)(2,1)S(1)} %get-tuple-element.35.refs_5_), channel_id=1, source_target_pairs={{32,0},{64,32},{96,64},{33,1},{65,33},{97,65},{34,2},{66,34},{98,6... | collective-permute-start | bytes 98312 | tf_op jit(solution)/shard_map/ppermute | solution.py:485
  13.2 11.6 %collective-permute-start.2 = (bf16[256,256]{1,0:T(8,128)(2,1)S(1)}, bf16[256,256]{1,0:T(8,128)(2,1)S(1)}, u32[]{:S(2)}, u32[]{:S(2)}) collective-permute-start(bf16[256,256]{1,0:T(8,128)(2,1)S(1)} %get-tuple-element.37), channel_id=1, source_target_pairs={{0,1},{1,2},{2,3},{3,4},{4,5},{5,6},{6,7},{7,8},{8,9},{9,10},{10,1... | collective-permute-start | bytes 393224 | tf_op jit(solution)/shard_map/ppermute | solution.py:485
  16.4 8.4 %collective-permute-start.3 = (bf16[256,256]{1,0:T(8,128)(2,1)S(1)}, bf16[256,256]{1,0:T(8,128)(2,1)S(1)}, u32[]{:S(2)}, u32[]{:S(2)}) collective-permute-start(bf16[256,256]{1,0:T(8,128)(2,1)S(1)} %get-tuple-element.38), channel_id=1, source_target_pairs={{1,0},{2,1},{3,2},{4,3},{5,4},{6,5},{7,6},{8,7},{9,8},{10,9},{11,1... | collective-permute-start | bytes 393224 | tf_op jit(solution)/shard_map/ppermute | solution.py:485
  18.5 1.0 copy-start
  19.5 0.9 copy-start.2
  20.4 0.9 copy-start.3
  21.3 0.8 copy-start.4
  42.9 29.7 %collective-permute-start.4 = (bf16[240,256]{1,0:T(8,128)(2,1)S(1)}, bf16[240,256]{1,0:T(8,128)(2,1)S(1)}, u32[]{:S(2)}, u32[]{:S(2)}) collective-permute-start(bf16[240,256]{1,0:T(8,128)(2,1)S(1)} %get-tuple-element.47), channel_id=1, source_target_pairs={{0,1},{1,2},{2,3},{3,4},{4,5},{5,6},{6,7},{7,8},{8,9},{9,10},{10,1... | collective-permute-start | bytes 368648 | tf_op jit(solution)/shard_map/ppermute | solution.py:485
  46.9 25.7 %collective-permute-start.5 = (bf16[240,256]{1,0:T(8,128)(2,1)S(1)}, bf16[240,256]{1,0:T(8,128)(2,1)S(1)}, u32[]{:S(2)}, u32[]{:S(2)}) collective-permute-start(bf16[240,256]{1,0:T(8,128)(2,1)S(1)} %get-tuple-element.48), channel_id=1, source_target_pairs={{1,0},{2,1},{3,2},{4,3},{5,4},{6,5},{7,6},{8,7},{9,8},{10,9},{11,1... | collective-permute-start | bytes 368648 | tf_op jit(solution)/shard_map/ppermute | solution.py:485
  89.1 22.8 %collective-permute-start.6 = (bf16[240,256]{1,0:T(8,128)(2,1)S(1)}, bf16[240,256]{1,0:T(8,128)(2,1)S(1)}, u32[]{:S(2)}, u32[]{:S(2)}) collective-permute-start(bf16[240,256]{1,0:T(8,128)(2,1)S(1)} %get-tuple-element.54), channel_id=1, source_target_pairs={{0,1},{1,2},{2,3},{3,4},{4,5},{5,6},{6,7},{7,8},{8,9},{9,10},{10,1... | collective-permute-start | bytes 368648 | tf_op jit(solution)/shard_map/ppermute | solution.py:485
  91.4 20.5 %collective-permute-start.7 = (bf16[240,256]{1,0:T(8,128)(2,1)S(1)}, bf16[240,256]{1,0:T(8,128)(2,1)S(1)}, u32[]{:S(2)}, u32[]{:S(2)}) collective-permute-start(bf16[240,256]{1,0:T(8,128)(2,1)S(1)} %get-tuple-element.55), channel_id=1, source_target_pairs={{1,0},{2,1},{3,2},{4,3},{5,4},{6,5},{7,6},{8,7},{9,8},{10,9},{11,1... | collective-permute-start | bytes 368648 | tf_op jit(solution)/shard_map/ppermute | solution.py:485
  127.8 22.8 %collective-permute-start.8 = (bf16[240,256]{1,0:T(8,128)(2,1)S(1)}, bf16[240,256]{1,0:T(8,128)(2,1)S(1)}, u32[]{:S(2)}, u32[]{:S(2)}) collective-permute-start(bf16[240,256]{1,0:T(8,128)(2,1)S(1)} %get-tuple-element.58), channel_id=1, source_target_pairs={{0,1},{1,2},{2,3},{3,4},{4,5},{5,6},{6,7},{7,8},{8,9},{9,10},{10,1... | collective-permute-start | bytes 368648 | tf_op jit(solution)/shard_map/ppermute | solution.py:485
  130.1 20.5 %collective-permute-start.9 = (bf16[240,256]{1,0:T(8,128)(2,1)S(1)}, bf16[240,256]{1,0:T(8,128)(2,1)S(1)}, u32[]{:S(2)}, u32[]{:S(2)}) collective-permute-start(bf16[240,256]{1,0:T(8,128)(2,1)S(1)} %get-tuple-element.59), channel_id=1, source_target_pairs={{1,0},{2,1},{3,2},{4,3},{5,4},{6,5},{7,6},{8,7},{9,8},{10,9},{11,1... | collective-permute-start | bytes 368648 | tf_op jit(solution)/shard_map/ppermute | solution.py:485
